TPU v7x, 32 devices: a whole 2x2x4 slice. The times are simulated.
32 devices in a mesh: fsdp: 8 (over z, x), tp: 4 (over y, core).
Axes of the slice: x: 2, y: 2, z: 4, core: 2. Of those that a mesh axis runs over, the one named last changes fastest.
Arguments:
- tokens: bfloat16 [1024, 4096], P('fsdp'), may hold values from -6 to 6
- gate_left: bfloat16 [4096, 1024], P('fsdp', 'tp'), may hold values from -0.09375 to 0.09375
- gate_right: bfloat16 [1024, 14336], P('fsdp', 'tp'), may hold values from -0.1875 to 0.1875
- gate_values: bfloat16 [108, 16384], P('tp', 'fsdp'), may hold values from -0.5 to 0.5
- gate_rows: int32 [108], P('tp'), may hold values from 0 to 31
- gate_cols: int32 [108], P('tp'), may hold values from 0 to 111, as said below
- up_left: bfloat16 [4096, 1024], P('fsdp', 'tp'), may hold values from -0.09375 to 0.09375
- up_right: bfloat16 [1024, 14336], P('fsdp', 'tp'), may hold values from -0.1875 to 0.1875
- up_values: bfloat16 [108, 16384], P('tp', 'fsdp'), may hold values from -0.5 to 0.5
- up_rows: int32 [108], P('tp'), may hold values from 0 to 31
- up_cols: int32 [108], P('tp'), may hold values from 0 to 111, as said below
- grad_hidden: bfloat16 [1024, 14336], P('fsdp', 'tp'), may hold values from -6 to 6
Outputs:
- hidden: bfloat16 [1024, 14336], P('fsdp', 'tp')
- grad_gate_values: float32 [108, 16384], P('tp', 'fsdp')
- grad_up_values: float32 [108, 16384], P('tp', 'fsdp')
Inputs may be any that keep to these rules, and one draw needn't show every extreme that they name: `gate_cols`: support blocks of one projection are distinct (row block, column block) pairs; the entries that lie on index t of tp have column blocks from t * 14336 // (128 * 4) to (t + 1) * 14336 // (128 * 4) - 1. Rows and columns of one projection go together. `up_cols`: as for the gate projection.
All inputs are finite; a program needn't handle non-finite values.
Results may differ from a plain program's by a relative error of at most 0.005.
Values may be sent and summed in bfloat16 or wider, within the bound.
No kernel may reach another device: no remote copies, remote signals or barrier semaphores. Data moves between devices by JAX's collectives and lax.ppermute only.
A program may use at most 128 MiB of HBM per device.

v0:
```python
import jax
import jax.numpy as jnp
from jax import lax
from jax.sharding import PartitionSpec as P

BLK = 128


def support_forward(tokens, blocks, rows, cols_local, col_blocks):
    width = tokens.shape[1] // BLK
    sources = tokens.reshape(tokens.shape[0], width, BLK)[:, rows, :]
    parts = jnp.einsum("tkb,kbc->tkc", sources, blocks, preferred_element_type=jnp.float32)
    placed = (
        jnp.zeros((tokens.shape[0], col_blocks, BLK), jnp.float32).at[:, cols_local, :].add(parts)
    )
    return (placed.reshape(tokens.shape[0], col_blocks * BLK), sources)


def value_terms(sources_gate, dpre_gate, local_gate, sources_up, dpre_up, local_up, col_blocks):
    picked_gate = dpre_gate.reshape(dpre_gate.shape[0], col_blocks, BLK)[:, local_gate, :]
    picked_up = dpre_up.reshape(dpre_up.shape[0], col_blocks, BLK)[:, local_up, :]
    value_gate = jnp.einsum(
        "tkb,tkc->kbc", sources_gate, picked_gate, preferred_element_type=jnp.float32
    )
    value_up = jnp.einsum("tkb,tkc->kbc", sources_up, picked_up, preferred_element_type=jnp.float32)
    return (
        value_gate.reshape(value_gate.shape[0], BLK * BLK),
        value_up.reshape(value_up.shape[0], BLK * BLK),
    )


def on_device(
    tokens,
    gate_left,
    gate_right,
    gate_values,
    gate_rows,
    gate_cols,
    up_left,
    up_right,
    up_values,
    up_rows,
    up_cols,
    grad_hidden,
):
    left_gate, left_up = (
        lax.all_gather(gate_left, "fsdp", axis=0, tiled=True),
        lax.all_gather(up_left, "fsdp", axis=0, tiled=True),
    )
    rank_gate = jnp.dot(tokens, left_gate, preferred_element_type=jnp.float32).astype(jnp.bfloat16)
    rank_up = jnp.dot(tokens, left_up, preferred_element_type=jnp.float32).astype(jnp.bfloat16)
    full_gate, full_up = (
        lax.all_gather(rank_gate, "tp", axis=1, tiled=True),
        lax.all_gather(rank_up, "tp", axis=1, tiled=True),
    )
    flat_gate, flat_up = (
        lax.all_gather(gate_values, "fsdp", axis=1, tiled=True),
        lax.all_gather(up_values, "fsdp", axis=1, tiled=True),
    )
    blocks_gate = flat_gate.reshape(flat_gate.shape[0], BLK, BLK)
    blocks_up = flat_up.reshape(flat_up.shape[0], BLK, BLK)
    right_gate = lax.all_gather(gate_right, "fsdp", axis=0, tiled=True)
    right_up = lax.all_gather(up_right, "fsdp", axis=0, tiled=True)
    col_blocks = right_gate.shape[1] // BLK
    col_base = lax.axis_index("tp") * col_blocks
    local_gate = gate_cols - col_base
    local_up = up_cols - col_base
    sparse_gate, sources_gate = support_forward(
        tokens, blocks_gate, gate_rows, local_gate, col_blocks
    )
    sparse_up, sources_up = support_forward(tokens, blocks_up, up_rows, local_up, col_blocks)
    pre_gate = jnp.dot(full_gate, right_gate, preferred_element_type=jnp.float32) + sparse_gate
    pre_up = jnp.dot(full_up, right_up, preferred_element_type=jnp.float32) + sparse_up
    sigma = jax.nn.sigmoid(pre_gate)
    silu = pre_gate * sigma
    upstream = grad_hidden.astype(jnp.float32)
    dpre_gate = (upstream * pre_up * sigma * (1.0 + pre_gate * (1.0 - sigma))).astype(jnp.bfloat16)
    dpre_up = (upstream * silu).astype(jnp.bfloat16)
    hidden = (silu * pre_up).astype(jnp.bfloat16)
    value_gate, value_up = value_terms(
        sources_gate, dpre_gate, local_gate, sources_up, dpre_up, local_up, col_blocks
    )
    grad_gate_values, grad_up_values = (
        lax.psum_scatter(value_gate, "fsdp", scatter_dimension=1, tiled=True),
        lax.psum_scatter(value_up, "fsdp", scatter_dimension=1, tiled=True),
    )
    return (hidden, grad_gate_values, grad_up_values)


def solution(mesh):
    return jax.shard_map(
        on_device,
        mesh=mesh,
        in_specs=(
            P("fsdp", None),
            P("fsdp", "tp"),
            P("fsdp", "tp"),
            P("tp", "fsdp"),
            P("tp"),
            P("tp"),
            P("fsdp", "tp"),
            P("fsdp", "tp"),
            P("tp", "fsdp"),
            P("tp"),
            P("tp"),
            P("fsdp", "tp"),
        ),
        out_specs=(P("fsdp", "tp"), P("tp", "fsdp"), P("tp", "fsdp")),
        check_vma=False,
    )
```

profile of v0, /device:TPU:0, one launch (start us, length us, event | category | flops | bytes accessed | tf_op | source)
XLA Modules:
  0.0 506.7 jit_solution(9324583249922640998)
XLA Ops:
  11.4 36.4 %all_gather.27 = bf16[27,16384]{1,0:T(8,128)(2,1)S(1)} all-gather(bf16[27,2048]{1,0:T(8,128)(2,1)S(1)} %copy-done.9), channel_id=1, replica_groups=mesh['fsdp'=8,'tp'=4] {'fsdp'}, dimensions={1}, use_global_device_ids=true | all-gather | bytes 995328 | tf_op jit(solution)/shard_map/all_gather | solution.py:57
  47.8 1.2 copy.44
  49.8 3.1 fusion.7
  53.1 4.6 scatter_fusion
  57.7 1.7 copy.31
  59.4 2.8 copy.32
  62.2 0.7 gather_fusion.1
  63.1 36.5 %all_gather.31 = bf16[27,16384]{1,0:T(8,128)(2,1)S(1)} all-gather(bf16[27,2048]{1,0:T(8,128)(2,1)S(1)} %copy-done.10), channel_id=1, replica_groups=mesh['fsdp'=8,'tp'=4] {'fsdp'}, dimensions={1}, use_global_device_ids=true | all-gather | bytes 995328 | tf_op jit(solution)/shard_map/all_gather | solution.py:58
  99.9 1.7 fusion.5
  101.7 4.6 scatter_fusion.1
  106.3 1.7 copy.34
  108.0 2.8 copy.35
  110.8 2.1 convolution_convert_fusion.1
  112.8 5.8 %all_gather.25 = bf16[128,1024]{1,0:T(8,128)(2,1)S(1)} all-gather(bf16[128,256]{1,0:T(8,128)(2,1)S(1)} %convolution_convert_fusion.1), channel_id=1, replica_groups=mesh['fsdp'=8,'tp'=4] {'tp'}, dimensions={1}, use_global_device_ids=true | all-gather | bytes 327680 | tf_op jit(solution)/shard_map/all_gather | solution.py:53
  118.6 3.5 all-gather.9.cloned.1.call-done
  122.2 2.0 convolution_convert_fusion
  124.2 6.0 %all_gather.29 = bf16[128,1024]{1,0:T(8,128)(2,1)S(1)} all-gather(bf16[128,256]{1,0:T(8,128)(2,1)S(1)} %convolution_convert_fusion), channel_id=1, replica_groups=mesh['fsdp'=8,'tp'=4] {'tp'}, dimensions={1}, use_global_device_ids=true | all-gather | bytes 327680 | tf_op jit(solution)/shard_map/all_gather | solution.py:54
  130.1 104.3 %all-gather.7.cloned.1.call-done = bf16[1024,3584]{1,0:T(8,128)(2,1)} async-done(((bf16[128,3584]{1,0:T(8,128)(2,1)}), bf16[1024,3584]{1,0:T(8,128)(2,1)}) %all-gather.7.cloned.1.call-update) | async-done | bytes 7340048 | tf_op jit(solution)/shard_map/all_gather | solution.py:62
  234.4 5.5 %convolution_add_fusion.1 = f32[128,3584]{1,0:T(8,128)} fusion(f32[128,3584]{1,0:T(8,128)S(1)} %copy-done.7, bf16[128,1024]{1,0:T(8,128)(2,1)S(1)} %all_gather.25, bf16[1024,3584]{1,0:T(8,128)(2,1)} %all-gather.7.cloned.1.call-done), kind=kOutput, calls=%fused_computation.7 | convolution fusion | flops 939982848 | bytes 11272192 | tf_op jit(solution)/shard_map/dot_general | solution.py:72
  239.9 106.3 %all-gather.11.cloned.1.call-done = bf16[1024,3584]{1,0:T(8,128)(2,1)} async-done(((bf16[128,3584]{1,0:T(8,128)(2,1)}), bf16[1024,3584]{1,0:T(8,128)(2,1)}) %all-gather.11.cloned.1.call-update) | async-done | bytes 7340048 | tf_op jit(solution)/shard_map/all_gather | solution.py:63
  346.2 7.5 %fusion.2 = (bf16[128,3584]{1,0:T(8,128)(2,1)}, bf16[128,3584]{1,0:T(8,128)(2,1)}, bf16[128,3584]{1,0:T(8,128)(2,1)S(1)}) fusion(bf16[128,3584]{1,0:T(8,128)(2,1)} %param.23, f32[128,3584]{1,0:T(8,128)} %convolution_add_fusion.1, f32[128,3584]{1,0:T(8,128)} %copy.35, bf16[128,1024]{1,0:T(8,128)(2,1)S(1)} %all_gather.29, ...), kind=kOutput, calls=%fused_computation.12 | convolution fusion | flops 947322880 | bytes 14942208 | tf_op jit(solution)/shard_map/dot_general | solution.py:73
  353.7 1.3 copy.39
  354.9 1.7 copy.40
  356.6 0.7 gather_fusion.3
  358.0 2.5 copy.47
  360.7 1.1 copy-done.8
  361.8 1.3 copy.36
  363.1 1.7 copy.37
  364.7 0.7 gather_fusion.2
  366.1 2.5 copy.46
  368.7 59.4 %reduce-scatter.5.cloned.1.call-done = f32[27,2048]{1,0:T(8,128)} async-done(((f32[27,16384]{1,0:T(8,128)}), f32[27,2048]{1,0:T(8,128)}) %reduce-scatter.5.cloned.1.call-update) | async-done | bytes 221200 | tf_op jit(solution)/shard_map/reduce_scatter | solution.py:85
  428.1 71.8 %reduce-scatter.3.cloned.1.call-done = f32[27,2048]{1,0:T(8,128)} async-done(((f32[27,16384]{1,0:T(8,128)}), f32[27,2048]{1,0:T(8,128)}) %reduce-scatter.3.cloned.1.call-update) | async-done | bytes 221200 | tf_op jit(solution)/shard_map/reduce_scatter | solution.py:84
  (59 shorter events, 7.1 us)
Async XLA Ops:
  7.2 2.9 copy-start
  7.2 103.6 %all-gather.5.cloned.1.call-start = ((), (), s32[]{:S(2)}) async-start(), calls=%async_computation.2 | async-start | bytes 2359296 | tf_op jit(solution)/shard_map/all_gather | solution.py:47
  7.9 114.2 %all-gather.9.cloned.1.call-start = ((), (), s32[]{:S(2)}) async-start(), calls=%async_computation.4 | async-start | bytes 2359296 | tf_op jit(solution)/shard_map/all_gather | solution.py:48
  8.7 225.8 %all-gather.7.cloned.1.call-start = ((), (), s32[]{:S(2)}) async-start(), calls=%async_computation.3 | async-start | bytes 8257536 | tf_op jit(solution)/shard_map/all_gather | solution.py:62
  9.4 336.8 %all-gather.11.cloned.1.call-start = ((), (), s32[]{:S(2)}) async-start(), calls=%async_computation.5 | async-start | bytes 8257536 | tf_op jit(solution)/shard_map/all_gather | solution.py:63
  10.0 418.1 %reduce-scatter.5.cloned.1.call-start = ((), (), s32[]{:S(2)}) async-start(), calls=%async_computation.7 | async-start | bytes 2359296 | tf_op jit(solution)/shard_map/reduce_scatter | solution.py:85
  10.0 1.4 copy-start.9
  11.4 38.4 %copy-start.1 = (bf16[128,32,128]{2,0,1:T(8,128)(2,1)}, bf16[128,32,128]{2,0,1:T(8,128)(2,1)S(1)}, u32[]{:S(2)}) copy-start(bf16[128,32,128]{2,0,1:T(8,128)(2,1)S(1)} %copy.30) | copy-start | bytes 3145732
  11.4 37.6 %copy-start.13 = (s32[27]{0:T(128)S(1)}, s32[27]{0:T(128)}, u32[]{:S(2)}) copy-start(s32[27]{0:T(128)} %param.16) | copy-start | bytes 328
  47.8 2.0 copy-start.11
  47.8 2.0 copy-start.12
  49.8 3.1 copy-start.3
  59.4 2.8 copy-start.14
  59.4 2.9 copy-start.2
  62.2 0.9 copy-start.10
  63.1 38.4 %copy-start.5 = (bf16[27,128,128]{2,1,0:T(8,128)(2,1)}, bf16[27,128,128]{2,1,0:T(8,128)(2,1)S(1)}, u32[]{:S(2)}) copy-start(bf16[27,128,128]{2,1,0:T(8,128)(2,1)S(1)} %gather_fusion.1) | copy-start | bytes 2654212
  118.6 115.8 %copy-start.7 = (f32[128,3584]{1,0:T(8,128)S(1)}, f32[128,3584]{1,0:T(8,128)}, u32[]{:S(2)}) copy-start(f32[128,3584]{1,0:T(8,128)} %copy.32) | copy-start | bytes 5505028
  354.9 2.4 copy-start.6
  360.6 1.2 copy-start.8
  360.6 139.3 %reduce-scatter.3.cloned.1.call-start = ((), (), s32[]{:S(2)}) async-start(), calls=%async_computation.6 | async-start | bytes 2359296 | tf_op jit(solution)/shard_map/reduce_scatter | solution.py:84
  363.1 2.4 copy-start.4
Sparse Core Ops, SparseCore 0:
  10.1 57.4 all-gather.4
  69.7 52.3 all-gather.8
  124.3 110.0 all-gather.6
  236.5 109.6 all-gather.10
  360.7 67.2 reduce-scatter.4
  432.0 67.7 reduce-scatter.2
where the time goes:
time: 507 us
  waiting for transfers between devices  348 us (69%)
  blocking collectives  84.6 us (17%)
  local copies, waits for them, and re-layouts  27.7 us (5%)
  matrix products  22.7 us (4%)
  between operations  14.4 us (3%)
  other arithmetic  9.17 us (2%)
    all_gather x1, waiting for transfers between devices, on_device(): right_up = lax.all_gather(up_right, 'fsdp', axis=0, tiled=True)  106 us
    all_gather x1, waiting for transfers between devices, on_device(): right_gate = lax.all_gather(gate_right, 'fsdp', axis=0, tiled=True)  104 us
    reduce_scatter x1, waiting for transfers between devices, on_device(): lax.psum_scatter(value_gate, 'fsdp', scatter_dimension=1, tiled=True)  71.8 us
    reduce_scatter x1, waiting for transfers between devices, on_device(): lax.psum_scatter(value_up, 'fsdp', scatter_dimension=1, tiled=True)  59.4 us
    all_gather x1, blocking collectives, on_device(): lax.all_gather(up_values, 'fsdp', axis=1, tiled=True)  36.5 us
    all_gather x1, blocking collectives, on_device(): lax.all_gather(gate_values, 'fsdp', axis=1, tiled=True)  36.4 us
  transfers between devices with their start and end apart: 6, of which 5 were waited for; matrix products, arithmetic and copies ran while one was open for 9% of the time, Pallas kernels for 0%

commit v1 on v0

--- a/solution.py
+++ b/solution.py
@@ -1,6 +1,10 @@
+import functools
+
 import jax
 import jax.numpy as jnp
 from jax import lax
+from jax.experimental import pallas as pl
+from jax.experimental.pallas import tpu as pltpu
 from jax.sharding import PartitionSpec as P
 
 BLK = 128
@@ -87,9 +91,269 @@
     return (hidden, grad_gate_values, grad_up_values)
 
 
+ANY = pl.BlockSpec(memory_space=pl.ANY)
+VMEM = pl.BlockSpec(memory_space=pltpu.VMEM)
+SMEM = pl.BlockSpec(memory_space=pltpu.SMEM)
+BF16, F32 = jnp.bfloat16, jnp.float32
+
+
+def at(start, size):
+    return pl.ds(pl.multiple_of(start, BLK), size)
+
+
+def run_copies(pairs, sems):
+    copies = [pltpu.make_async_copy(s, d, sems.at[i]) for i, (s, d) in enumerate(pairs)]
+    for copy in copies:
+        copy.start()
+    return copies
+
+
+def partial_kernel(nz, idx, tokens, *refs):
+    mine, other = refs[: nz - 1], refs[nz - 1 : 2 * nz - 2]
+    left_g, left_u, recv_g, recv_u = refs[2 * nz - 2 : 2 * nz + 2]
+    own_out, outs = refs[2 * nz + 2], refs[2 * nz + 3 : 3 * nz + 2]
+    left, toks, sems = refs[3 * nz + 2 :]
+    z, x, c = idx[0], idx[1], idx[2]
+    depth, width = left_g.shape
+    pairs = [
+        (left_g, left.at[x, :, pl.ds(0, width)]),
+        (left_u, left.at[x, :, pl.ds(width, width)]),
+        (recv_g, left.at[1 - x, :, pl.ds(0, width)]),
+        (recv_u, left.at[1 - x, :, pl.ds(width, width)]),
+        (tokens.at[:, at(z * 2 * depth, 2 * depth)], toks.at[0]),
+    ]
+    for j in range(1, nz):
+        pairs.append((mine[j - 1], toks.at[j, :, at(c * depth, depth)]))
+        pairs.append((other[j - 1], toks.at[j, :, at((1 - c) * depth, depth)]))
+    for copy in run_copies(pairs, sems):
+        copy.wait()
+    weights = left[...].reshape(2 * depth, 2 * width)
+    rows = toks.shape[1]
+    total = jnp.dot(
+        toks[...].reshape(nz * rows, 2 * depth), weights, preferred_element_type=F32
+    )
+    own_out[...] = total[:rows]
+    for j in range(1, nz):
+        outs[j - 1][...] = total[j * rows : (j + 1) * rows].astype(BF16)
+
+
+def lowrank_kernel(nf, nt, idx, *refs):
+    ranks, rights = refs[:nt], refs[nt : nt + nf]
+    outs = refs[nt + nf : nt + 2 * nf]
+    rank, weight, sems = refs[nt + 2 * nf :]
+    f, t = idx[3], idx[4]
+    pairs = [(ranks[s], rank.at[t ^ s]) for s in range(nt)]
+    pairs += [(rights[k], weight.at[f ^ k]) for k in range(nf)]
+    for copy in run_copies(pairs, sems):
+        copy.wait()
+    rows, width = rank.shape[2], rank.shape[3]
+    cols = weight.shape[2]
+    weights = weight[...].reshape(nt, width, cols)
+    group = min(4, nf)
+    for m in range(0, nf, group):
+        total = None
+        for s in range(nt):
+            lhs = rank[s, m : m + group].reshape(group * rows, width)
+            part = jnp.dot(lhs, weights[s], preferred_element_type=F32)
+            total = part if total is None else total + part
+        for i in range(group):
+            outs[m + i][...] = total[i * rows : (i + 1) * rows].astype(BF16)
+
+
+def sparse_kernel(nf, idx, gate_rows, gate_cols, up_rows, up_cols, tokens, *refs):
+    values, out, blocks, sems = refs[:nf], refs[nf], refs[nf + 1], refs[nf + 2]
+    f = idx[3]
+    copies = run_copies([(values[k], blocks.at[:, f ^ k]) for k in range(nf)], sems)
+    out[...] = jnp.zeros_like(out)
+    for copy in copies:
+        copy.wait()
+    count = gate_rows.shape[0]
+    for p, (rows, cols) in enumerate(((gate_rows, gate_cols), (up_rows, up_cols))):
+
+        def step(k, carry, p=p, rows=rows, cols=cols):
+            source = tokens[:, at(rows[k] * BLK, BLK)]
+            block = blocks[p * count + k].reshape(BLK, BLK)
+            here = at(cols[k] * BLK, BLK)
+            out[p, :, here] += jnp.dot(source, block, preferred_element_type=F32)
+            return carry
+
+        lax.fori_loop(0, count, step, 0, unroll=True)
+
+
+def final_kernel(nf, idx, gate_rows, gate_cols, up_rows, up_cols, tokens, grad, sparse, *refs):
+    pieces, hidden, grads = refs[:nf], refs[nf], refs[nf + 1]
+    pre, dpre, sems = refs[nf + 2 :]
+    f = idx[3]
+    pairs = [(pieces[k], pre.at[(f ^ k) % 2, (f ^ k) // 2]) for k in range(nf)]
+    for copy in run_copies(pairs, sems):
+        copy.wait()
+    width = pre.shape[3]
+    for j in range(pre.shape[1]):
+        here = pl.ds(j * width, width)
+        gate = pre[0, j].astype(F32) + sparse[0, :, here]
+        up = pre[1, j].astype(F32) + sparse[1, :, here]
+        sigma = jax.nn.sigmoid(gate)
+        silu = gate * sigma
+        upstream = grad[:, here].astype(F32)
+        dpre[0, :, here] = (upstream * up * sigma * (1.0 + gate * (1.0 - sigma))).astype(BF16)
+        dpre[1, :, here] = (upstream * silu).astype(BF16)
+        hidden[:, here] = (silu * up).astype(BF16)
+    count = gate_rows.shape[0]
+    for p, (rows, cols) in enumerate(((gate_rows, gate_cols), (up_rows, up_cols))):
+
+        def step(k, carry, p=p, rows=rows, cols=cols):
+            source = tokens[:, at(rows[k] * BLK, BLK)]
+            picked = dpre[p, :, at(cols[k] * BLK, BLK)]
+            value = lax.dot_general(
+                source, picked, (((0,), (0,)), ((), ())), preferred_element_type=F32
+            )
+            grads[:, p * count + k] = value.astype(BF16).reshape(nf, BLK // nf, BLK)
+            return carry
+
+        lax.fori_loop(0, count, step, 0, unroll=True)
+
+
+def exchange_device(
+    mesh,
+    tokens,
+    gate_left,
+    gate_right,
+    gate_values,
+    gate_rows,
+    gate_cols,
+    up_left,
+    up_right,
+    up_values,
+    up_rows,
+    up_cols,
+    grad_hidden,
+):
+    nf, nt = mesh.shape["fsdp"], mesh.shape["tp"]
+    nz = nf // 2
+    rows, width = tokens.shape[0], gate_right.shape[1]
+    depth, slice_width = gate_left.shape
+    cols = width // nz
+    count = gate_values.shape[0]
+    share = BLK // nf
+    f, t = lax.axis_index("fsdp"), lax.axis_index("tp")
+    z, x, c = f // 2, f % 2, t % 2
+    idx = jnp.stack([z, x, c, f, t]).astype(jnp.int32)
+
+    def move(value, df=0, dt=0):
+        pairs = [(i * nt + j, (i ^ df) * nt + (j ^ dt)) for i in range(nf) for j in range(nt)]
+        return lax.ppermute(value, ("fsdp", "tp"), pairs)
+
+    halves = [
+        lax.dynamic_slice(tokens, (0, (z ^ j) * 2 * depth + c * depth), (rows, depth))
+        for j in range(1, nz)
+    ]
+    mine = [move(h, df=2 * j) for j, h in enumerate(halves, 1)]
+    recv_g, recv_u = move(gate_left, df=1), move(up_left, df=1)
+    other = [move(h, dt=1) for h in mine]
+    sums = pl.pallas_call(
+        functools.partial(partial_kernel, nz),
+        out_shape=[jax.ShapeDtypeStruct((rows, 2 * slice_width), F32)]
+        + [jax.ShapeDtypeStruct((rows, 2 * slice_width), BF16)] * (nz - 1),
+        in_specs=[SMEM] + [ANY] * (2 * nz + 3),
+        out_specs=[VMEM] * nz,
+        scratch_shapes=[
+            pltpu.VMEM((2, depth, 2 * slice_width), BF16),
+            pltpu.VMEM((nz, rows, 2 * depth), BF16),
+            pltpu.SemaphoreType.DMA((2 * nz + 3,)),
+        ],
+        name="rank_partial",
+    )(idx, tokens, *mine, *other, gate_left, up_left, recv_g, recv_u)
+    total = sums[0]
+    for j in range(1, nz):
+        total = total + move(sums[j], df=2 * j).astype(F32)
+    rank = total.astype(BF16)
+    rank_gate, rank_up = rank[:, :slice_width], rank[:, slice_width:]
+    rank_own = jnp.where(x == 0, rank_gate, rank_up)
+    rank_other = jnp.where(x == 0, rank_up, rank_gate)
+    slots = [rank_own] + [move(rank_other if k % 2 else rank_own, df=k) for k in range(1, nf)]
+    stack = jnp.stack(slots)
+    ranks = [stack, move(stack, dt=1)]
+    ranks.append(move(stack, dt=2))
+    ranks.append(move(ranks[2], dt=1))
+
+    rights = []
+    for k in range(nf):
+        start = (0, (z ^ (k // 2)) * cols)
+        size = (gate_right.shape[0], cols)
+        rights.append(
+            jnp.where(
+                (x ^ (k % 2)) == 0,
+                lax.dynamic_slice(gate_right, start, size),
+                lax.dynamic_slice(up_right, start, size),
+            )
+        )
+    rights = [rights[0]] + [move(rights[k], df=k) for k in range(1, nf)]
+
+    own_values = jnp.concatenate([gate_values, up_values], 0).reshape(2 * count, share, BLK)
+    over_z = [own_values] + [move(own_values, df=2 * j) for j in range(1, nz)]
+    values = []
+    for j in range(nz):
+        values += [over_z[j], move(over_z[j], df=1)]
+    base = t * (width // BLK)
+    index = (idx, gate_rows, gate_cols - base, up_rows, up_cols - base)
+    sparse = pl.pallas_call(
+        functools.partial(sparse_kernel, nf),
+        out_shape=jax.ShapeDtypeStruct((2, rows, width), F32),
+        in_specs=[SMEM] * 5 + [VMEM] + [ANY] * nf,
+        out_specs=VMEM,
+        scratch_shapes=[
+            pltpu.VMEM((2 * count, nf, share, BLK), BF16),
+            pltpu.SemaphoreType.DMA((nf,)),
+        ],
+        name="sparse_forward",
+    )(*index, tokens, *values)
+
+    lowrank = pl.pallas_call(
+        functools.partial(lowrank_kernel, nf, nt),
+        out_shape=[jax.ShapeDtypeStruct((rows, cols), BF16)] * nf,
+        in_specs=[SMEM] + [ANY] * (nt + nf),
+        out_specs=[VMEM] * nf,
+        scratch_shapes=[
+            pltpu.VMEM((nt, nf, rows, slice_width), BF16),
+            pltpu.VMEM((nf, gate_right.shape[0], cols), BF16),
+            pltpu.SemaphoreType.DMA((nt + nf,)),
+        ],
+        name="lowrank",
+    )(idx, *ranks, *rights)
+    pieces = [lowrank[0]] + [move(lowrank[k], df=k) for k in range(1, nf)]
+
+    hidden, grads = pl.pallas_call(
+        functools.partial(final_kernel, nf),
+        out_shape=[
+            jax.ShapeDtypeStruct((rows, width), BF16),
+            jax.ShapeDtypeStruct((nf, 2 * count, share, BLK), BF16),
+        ],
+        in_specs=[SMEM] * 5 + [VMEM] * 3 + [ANY] * nf,
+        out_specs=[VMEM] * 2,
+        scratch_shapes=[
+            pltpu.VMEM((2, nz, rows, cols), BF16),
+            pltpu.VMEM((2, rows, width), BF16),
+            pltpu.SemaphoreType.DMA((nf,)),
+        ],
+        name="hidden_and_grads",
+    )(*index, tokens, grad_hidden, sparse, *pieces)
+    shares = lax.all_to_all(grads, "fsdp", 0, 0, tiled=True)
+    summed = jnp.sum(shares.astype(F32), axis=0).reshape(2 * count, share * BLK)
+    return hidden, summed[:count], summed[count:]
+
+
+def dispatch(mesh, *args):
+    nf, nt = mesh.shape["fsdp"], mesh.shape["tp"]
+    width = args[2].shape[1]
+    direct = nf in (4, 8) and nt == 4 and width % (BLK * (nf // 2)) == 0
+    if direct:
+        return exchange_device(mesh, *args)
+    return on_device(*args)
+
+
 def solution(mesh):
     return jax.shard_map(
-        on_device,
+        functools.partial(dispatch, mesh),
         mesh=mesh,
         in_specs=(
             P("fsdp", None),

time: 507 us -> 232 us (0.46)
  waiting for transfers between devices: 348 us -> 94 us
  starting transfers between devices: 0.23 us -> 55.2 us
  blocking collectives: 84.6 us -> 47.2 us
  Pallas kernels: 0 us -> 24.5 us
  matrix products: 22.7 us -> 0 us
  local copies, waits for them, and re-layouts: 27.7 us -> 6.14 us
  between operations: 14.4 us -> 1.11 us
  other arithmetic: 9.17 us -> 2.91 us
    all_gather x4 -> x0, waiting for transfers between devices: 214 us -> none  [the longest x1 106 us: on_device(): right_up = lax.all_gather(up_right, 'fsdp', axis=0, tiled=True)]
    reduce_scatter x2 -> x0, waiting for transfers between devices: 131 us -> none  [the longest x1 71.8 us: on_device(): lax.psum_scatter(value_gate, 'fsdp', scatter_dimension=1, tiled=True)]
    ppermute x0 -> x42, waiting for transfers between devices: none -> 94 us  [move(): return lax.ppermute(value, ('fsdp', 'tp'), pairs)]
    all_gather x4 -> x0, blocking collectives: 84.6 us -> none  [the longest x1 36.5 us: on_device(): lax.all_gather(up_values, 'fsdp', axis=1, tiled=True)]
    ppermute x0 -> x42, starting transfers between devices: none -> 55.2 us  [move(): return lax.ppermute(value, ('fsdp', 'tp'), pairs)]
    all_to_all x0 -> x1, blocking collectives: none -> 47.2 us  [exchange_device(): shares = lax.all_to_all(grads, 'fsdp', 0, 0, tiled=True)]
    pallas_call x0 -> x4, Pallas kernels: none -> 24.5 us  [the longest x1 8.97 us: exchange_device(): pl.pallas_call(functools.partial(final_kernel, nf), out_shape=[jax.ShapeD...]
    dot_general x8 -> x0, matrix products: 22.7 us -> none  [the longest x1 7.48 us: on_device(): jnp.dot(full_up, right_up, preferred_element_type=jnp.float32) + sparse_up]
  transfers between devices with their start and end apart: 6 -> 42, of which waited for: 5 -> 19; matrix products, arithmetic and copies ran while one was open for 9% -> 1% of each run, Pallas kernels for 0% -> 5%
where the time goes in v1:
time: 232 us; the launch traced here: 231 us
  waiting for transfers between devices  94 us (41%)
  starting transfers between devices  55.2 us (24%)
  blocking collectives  47.2 us (20%)
  Pallas kernels  24.5 us (11%)
  local copies, waits for them, and re-layouts  6.14 us (3%)
  other arithmetic  2.91 us (1%)
    ppermute x42, waiting for transfers between devices, move(): return lax.ppermute(value, ('fsdp', 'tp'), pairs)  94 us
    ppermute x42, starting transfers between devices, move(): return lax.ppermute(value, ('fsdp', 'tp'), pairs)  55.2 us
    all_to_all x1, blocking collectives, exchange_device(): shares = lax.all_to_all(grads, 'fsdp', 0, 0, tiled=True)  47.2 us
    pallas_call x1, Pallas kernels, exchange_device(): pl.pallas_call(functools.partial(final_kernel, nf), out_shape=[jax.ShapeD...  8.97 us
    pallas_call x1, Pallas kernels, exchange_device(): pl.pallas_call(functools.partial(lowrank_kernel, nf, nt), out_shape=[jax....  6.14 us
    pallas_call x1, Pallas kernels, exchange_device(): pl.pallas_call(functools.partial(sparse_kernel, nf), out_shape=jax.ShapeD...  5.73 us
  transfers between devices with their start and end apart: 42, of which 19 were waited for; matrix products, arithmetic and copies ran while one was open for 1% of the time, Pallas kernels for 5%

profile of v1, /device:TPU:0, one launch (start us, length us, event | category | flops | bytes accessed | tf_op | source)
XLA Modules:
  0.0 231.1 jit_solution(10469690661968893721)
XLA Ops:
  0.6 3.0 %collective-permute-start.13 = (bf16[512,256]{1,0:T(8,128)(2,1)}, bf16[512,256]{1,0:T(8,128)(2,1)S(1)}, u32[]{:S(2)}, u32[]{:S(2)}) collective-permute-start(bf16[512,256]{1,0:T(8,128)(2,1)} %refs_6_.1), channel_id=1, source_target_pairs={{0,4},{1,5},{2,6},{3,7},{4,0},{5,1},{6,2},{7,3},{8,12},{9,13},{10,... | collective-permute-start | bytes 786440 | tf_op jit(solution)/shard_map/ppermute | solution.py:244
  4.8 4.1 %collective-permute-start.9 = (bf16[128,512]{1,0:T(8,128)(2,1)S(1)}, bf16[128,512]{1,0:T(8,128)(2,1)S(1)}, u32[]{:S(2)}, u32[]{:S(2)}) collective-permute-start(bf16[128,512]{1,0:T(8,128)(2,1)S(1)} %get-tuple-element.41), channel_id=1, source_target_pairs={{0,24},{1,25},{2,26},{3,27},{4,28},{5,29},{6,30},{7,31},{8,16},{9,... | collective-permute-start | bytes 393224 | tf_op jit(solution)/shard_map/ppermute | solution.py:244
  9.6 3.8 %collective-permute-done.9.refs_2_ = bf16[128,512]{1,0:T(8,128)(2,1)S(1)} collective-permute-done((bf16[128,512]{1,0:T(8,128)(2,1)S(1)}, bf16[128,512]{1,0:T(8,128)(2,1)S(1)}, u32[]{:S(2)}, u32[]{:S(2)}) %collective-permute-start.9) | collective-permute-done | bytes 131104 | tf_op jit(solution)/shard_map/ppermute | solution.py:244
  13.3 6.1 %collective-permute-done.8.refs_1_ = bf16[128,512]{1,0:T(8,128)(2,1)S(1)} collective-permute-done((bf16[128,512]{1,0:T(8,128)(2,1)S(1)}, bf16[128,512]{1,0:T(8,128)(2,1)S(1)}, u32[]{:S(2)}, u32[]{:S(2)}) %collective-permute-start.8) | collective-permute-done | bytes 131104 | tf_op jit(solution)/shard_map/ppermute | solution.py:244
  22.1 3.7 %rank_partial.1 = (f32[128,512]{1,0:T(8,128)}, bf16[128,512]{1,0:T(8,128)(2,1)}, bf16[128,512]{1,0:T(8,128)(2,1)}, bf16[128,512]{1,0:T(8,128)(2,1)}) custom-call(s32[5]{0:T(128)} %stack.50.idx, bf16[128,4096]{1,0:T(8,128)(2,1)} %tokens.5, bf16[128,512]{1,0:T(8,128)(2,1)} %copy-done.29, bf16[128,512]{1,0:T(8,128)(2,1)} %copy-done.28, ...), custom_call_target="tpu_custom_call" | custom-call | tf_op jit(solution)/shard_map/rank_partial/pallas_call | solution.py:253
  25.9 3.0 %collective-permute-start.16 = (bf16[128,512]{1,0:T(8,128)(2,1)}, bf16[128,512]{1,0:T(8,128)(2,1)S(1)}, u32[]{:S(2)}, u32[]{:S(2)}) collective-permute-start(bf16[128,512]{1,0:T(8,128)(2,1)} %get-tuple-element.19), channel_id=1, source_target_pairs={{0,16},{1,17},{2,18},{3,19},{4,20},{5,21},{6,22},{7,23},{8,24},{9,... | collective-permute-start | bytes 393224 | tf_op jit(solution)/shard_map/ppermute | solution.py:244
  30.3 3.7 %collective-permute-done.15 = bf16[128,512]{1,0:T(8,128)(2,1)S(1)} collective-permute-done((bf16[128,512]{1,0:T(8,128)(2,1)}, bf16[128,512]{1,0:T(8,128)(2,1)S(1)}, u32[]{:S(2)}, u32[]{:S(2)}) %collective-permute-start.15) | collective-permute-done | bytes 131104 | tf_op jit(solution)/shard_map/ppermute | solution.py:244
  33.9 5.2 %collective-permute-done.16 = bf16[128,512]{1,0:T(8,128)(2,1)S(1)} collective-permute-done((bf16[128,512]{1,0:T(8,128)(2,1)}, bf16[128,512]{1,0:T(8,128)(2,1)S(1)}, u32[]{:S(2)}, u32[]{:S(2)}) %collective-permute-start.16) | collective-permute-done | bytes 131104 | tf_op jit(solution)/shard_map/ppermute | solution.py:244
  40.2 3.4 %collective-permute-start.24 = (bf16[128,256]{1,0:T(8,128)(2,1)S(1)}, bf16[128,256]{1,0:T(8,128)(2,1)S(1)}, u32[]{:S(2)}, u32[]{:S(2)}) collective-permute-start(bf16[128,256]{1,0:T(8,128)(2,1)S(1)} %broadcast_select_fusion.8), channel_id=1, source_target_pairs={{0,28},{1,29},{2,30},{3,31},{4,24},{5,25},{6,26},{7,27},{8,20},{9,... | collective-permute-start | bytes 196616 | tf_op jit(solution)/shard_map/ppermute | solution.py:244
  47.0 2.7 %collective-permute-start.21 = (bf16[128,256]{1,0:T(8,128)(2,1)S(1)}, bf16[128,256]{1,0:T(8,128)(2,1)S(1)}, u32[]{:S(2)}, u32[]{:S(2)}) collective-permute-start(bf16[128,256]{1,0:T(8,128)(2,1)S(1)} %get-tuple-element.32), channel_id=1, source_target_pairs={{0,16},{1,17},{2,18},{3,19},{4,20},{5,21},{6,22},{7,23},{8,24},{9,... | collective-permute-start | bytes 196616 | tf_op jit(solution)/shard_map/ppermute | solution.py:244
  53.1 2.6 %collective-permute-done.19 = bf16[128,256]{1,0:T(8,128)(2,1)S(1)} collective-permute-done((bf16[128,256]{1,0:T(8,128)(2,1)S(1)}, bf16[128,256]{1,0:T(8,128)(2,1)S(1)}, u32[]{:S(2)}, u32[]{:S(2)}) %collective-permute-start.19) | collective-permute-done | bytes 65568 | tf_op jit(solution)/shard_map/ppermute | solution.py:244
  55.7 2.5 %collective-permute-start.23 = (bf16[128,256]{1,0:T(8,128)(2,1)S(1)}, bf16[128,256]{1,0:T(8,128)(2,1)S(1)}, u32[]{:S(2)}, u32[]{:S(2)}) collective-permute-start(bf16[128,256]{1,0:T(8,128)(2,1)S(1)} %get-tuple-element.32), channel_id=1, source_target_pairs={{0,24},{1,25},{2,26},{3,27},{4,28},{5,29},{6,30},{7,31},{8,16},{9,... | collective-permute-start | bytes 196616 | tf_op jit(solution)/shard_map/ppermute | solution.py:244
  58.2 3.6 %collective-permute-done.23 = bf16[128,256]{1,0:T(8,128)(2,1)S(1)} collective-permute-done((bf16[128,256]{1,0:T(8,128)(2,1)S(1)}, bf16[128,256]{1,0:T(8,128)(2,1)S(1)}, u32[]{:S(2)}, u32[]{:S(2)}) %collective-permute-start.23) | collective-permute-done | bytes 65568 | tf_op jit(solution)/shard_map/ppermute | solution.py:244
  64.5 2.2 collective-permute-start.34
  66.7 2.0 collective-permute-start.33
  68.6 7.1 %collective-permute-done.34.refs_11_ = bf16[128,896]{1,0:T(8,128)(2,1)S(1)} collective-permute-done((bf16[128,896]{1,0:T(8,128)(2,1)S(1)}, bf16[128,896]{1,0:T(8,128)(2,1)S(1)}, u32[]{:S(2)}, u32[]{:S(2)}) %collective-permute-start.34) | collective-permute-done | bytes 229408 | tf_op jit(solution)/shard_map/ppermute | solution.py:244
  76.1 3.5 %collective-permute-done.29.refs_6_ = bf16[128,896]{1,0:T(8,128)(2,1)S(1)} collective-permute-done((bf16[128,896]{1,0:T(8,128)(2,1)S(1)}, bf16[128,896]{1,0:T(8,128)(2,1)S(1)}, u32[]{:S(2)}, u32[]{:S(2)}) %collective-permute-start.29) | collective-permute-done | bytes 229408 | tf_op jit(solution)/shard_map/ppermute | solution.py:244
  81.2 3.6 %collective-permute-done.33.refs_10_ = bf16[128,896]{1,0:T(8,128)(2,1)S(1)} collective-permute-done((bf16[128,896]{1,0:T(8,128)(2,1)S(1)}, bf16[128,896]{1,0:T(8,128)(2,1)S(1)}, u32[]{:S(2)}, u32[]{:S(2)}) %collective-permute-start.33) | collective-permute-done | bytes 229408 | tf_op jit(solution)/shard_map/ppermute | solution.py:244
  84.8 4.5 %collective-permute-start.32 = (bf16[128,896]{1,0:T(8,128)(2,1)S(1)}, bf16[128,896]{1,0:T(8,128)(2,1)S(1)}, u32[]{:S(2)}, u32[]{:S(2)}) collective-permute-start(bf16[128,896]{1,0:T(8,128)(2,1)S(1)} %get-tuple-element.39), channel_id=1, source_target_pairs={{0,20},{1,21},{2,22},{3,23},{4,16},{5,17},{6,18},{7,19},{8,28},{9,... | collective-permute-start | bytes 688136 | tf_op jit(solution)/shard_map/ppermute | solution.py:244
  89.3 11.1 %collective-permute-done.31.refs_8_ = bf16[128,896]{1,0:T(8,128)(2,1)S(1)} collective-permute-done((bf16[128,896]{1,0:T(8,128)(2,1)S(1)}, bf16[128,896]{1,0:T(8,128)(2,1)S(1)}, u32[]{:S(2)}, u32[]{:S(2)}) %collective-permute-start.31) | collective-permute-done | bytes 229408 | tf_op jit(solution)/shard_map/ppermute | solution.py:244
  102.1 9.7 %collective-permute-done.32.refs_9_ = bf16[128,896]{1,0:T(8,128)(2,1)S(1)} collective-permute-done((bf16[128,896]{1,0:T(8,128)(2,1)S(1)}, bf16[128,896]{1,0:T(8,128)(2,1)S(1)}, u32[]{:S(2)}, u32[]{:S(2)}) %collective-permute-start.32) | collective-permute-done | bytes 229408 | tf_op jit(solution)/shard_map/ppermute | solution.py:244
  112.0 2.0 collective-permute-start.1
  115.6 6.1 %lowrank.1 = (bf16[128,896]{1,0:T(8,128)(2,1)}, bf16[128,896]{1,0:T(8,128)(2,1)}, bf16[128,896]{1,0:T(8,128)(2,1)}, bf16[128,896]{1,0:T(8,128)(2,1)}, bf16[128,8...) custom-call(s32[5]{0:T(128)} %stack.50.idx, ...), custom_call_target="tpu_custom_call" | custom-call | tf_op jit(solution)/shard_map/lowrank/pallas_call | solution.py:311
  127.1 10.5 %collective-permute-done.6.refs_7_ = bf16[54,16,128]{2,1,0:T(8,128)(2,1)S(1)} collective-permute-done((bf16[54,16,128]{2,1,0:T(8,128)(2,1)}, bf16[54,16,128]{2,1,0:T(8,128)(2,1)S(1)}, u32[]{:S(2)}, u32[]{:S(2)}) %collective-permute-start.6) | collective-permute-done | bytes 221216 | tf_op jit(solution)/shard_map/ppermute | solution.py:244
  138.6 2.7 %collective-permute-done.4.refs_5_ = bf16[54,16,128]{2,1,0:T(8,128)(2,1)S(1)} collective-permute-done((bf16[54,16,128]{2,1,0:T(8,128)(2,1)}, bf16[54,16,128]{2,1,0:T(8,128)(2,1)S(1)}, u32[]{:S(2)}, u32[]{:S(2)}) %collective-permute-start.4) | collective-permute-done | bytes 221216 | tf_op jit(solution)/shard_map/ppermute | solution.py:244
  141.4 4.4 %collective-permute-done.2.refs_3_ = bf16[54,16,128]{2,1,0:T(8,128)(2,1)S(1)} collective-permute-done((bf16[54,16,128]{2,1,0:T(8,128)(2,1)}, bf16[54,16,128]{2,1,0:T(8,128)(2,1)S(1)}, u32[]{:S(2)}, u32[]{:S(2)}) %collective-permute-start.2) | collective-permute-done | bytes 221216 | tf_op jit(solution)/shard_map/ppermute | solution.py:244
  145.8 5.0 %collective-permute-start.40 = (bf16[128,896]{1,0:T(8,128)(2,1)}, bf16[128,896]{1,0:T(8,128)(2,1)S(1)}, u32[]{:S(2)}, u32[]{:S(2)}) collective-permute-start(bf16[128,896]{1,0:T(8,128)(2,1)} %get-tuple-element.27), channel_id=1, source_target_pairs={{0,24},{1,25},{2,26},{3,27},{4,28},{5,29},{6,30},{7,31},{8,16},{9,... | collective-permute-start | bytes 688136 | tf_op jit(solution)/shard_map/ppermute | solution.py:244
  152.1 5.7 %sparse_forward.1.sparse = f32[2,128,3584]{2,1,0:T(8,128)} custom-call(s32[5]{0:T(128)} %stack.50.idx, s32[27]{0:T(128)} %gate_rows.3, s32[27]{0:T(128)} %get-tuple-element.47.gate_cols, s32[27]{0:T(128)} %up_rows.3, s32[27]{0:T(128)} %get-tuple-element.46.up_cols, bf16[128,4096]{1,0:T(8,128)(2,1)} %tokens.5, bf16[54,16,128]{2,1,0:T(8,128)(2,1)} %copy-done.2, ...), custom_call_target="tpu_custom_call" | custom-call | tf_op jit(solution)/shard_map/sparse_forward/pallas_call | solution.py:299
  157.9 8.2 %collective-permute-done.38.refs_4_ = bf16[128,896]{1,0:T(8,128)(2,1)S(1)} collective-permute-done((bf16[128,896]{1,0:T(8,128)(2,1)}, bf16[128,896]{1,0:T(8,128)(2,1)S(1)}, u32[]{:S(2)}, u32[]{:S(2)}) %collective-permute-start.38) | collective-permute-done | bytes 229408 | tf_op jit(solution)/shard_map/ppermute | solution.py:244
  166.1 6.1 %collective-permute-done.39.refs_5_ = bf16[128,896]{1,0:T(8,128)(2,1)S(1)} collective-permute-done((bf16[128,896]{1,0:T(8,128)(2,1)}, bf16[128,896]{1,0:T(8,128)(2,1)S(1)}, u32[]{:S(2)}, u32[]{:S(2)}) %collective-permute-start.39) | collective-permute-done | bytes 229408 | tf_op jit(solution)/shard_map/ppermute | solution.py:244
  173.0 9.0 %hidden_and_grads.1 = (bf16[128,3584]{1,0:T(8,128)(2,1)}, bf16[8,54,16,128]{3,2,1,0:T(8,128)(2,1)}) custom-call(s32[5]{0:T(128)} %stack.50.idx, s32[27]{0:T(128)} %gate_rows.3, s32[27]{0:T(128)} %get-tuple-element.47.gate_cols, s32[27]{0:T(128)} %up_rows.3, s32[27]{0:T(128)} %get-tuple-element.46.up_cols, bf16[128,4096]{1,0:T(8,128)(2,1)} %tokens.5, ...), custom_call_target="tpu_custom_call" | custom-call | tf_op jit(solution)/shard_map/hidden_and_grads/pallas_call | solution.py:325
  182.0 47.2 %all_to_all.5 = bf16[8,54,16,128]{3,2,1,0:T(8,128)(2,1)S(1)} all-to-all(bf16[8,54,16,128]{3,2,1,0:T(8,128)(2,1)} %get-tuple-element.30), channel_id=1, replica_groups=mesh['fsdp'=8,'tp'=4] {'fsdp'}, dimensions={0} | all-to-all | bytes 3538944 | tf_op jit(solution)/shard_map/all_to_all | solution.py:340
  (154 shorter events, 32.0 us)
Async XLA Ops:
  0.6 19.9 %collective-permute-start.13 = (bf16[512,256]{1,0:T(8,128)(2,1)}, bf16[512,256]{1,0:T(8,128)(2,1)S(1)}, u32[]{:S(2)}, u32[]{:S(2)}) collective-permute-start(bf16[512,256]{1,0:T(8,128)(2,1)} %refs_6_.1), channel_id=1, source_target_pairs={{0,4},{1,5},{2,6},{3,7},{4,0},{5,1},{6,2},{7,3},{8,12},{9,13},{10,... | collective-permute-start | bytes 786440 | tf_op jit(solution)/shard_map/ppermute | solution.py:244
  3.7 16.9 %collective-permute-start.14 = (bf16[512,256]{1,0:T(8,128)(2,1)}, bf16[512,256]{1,0:T(8,128)(2,1)S(1)}, u32[]{:S(2)}, u32[]{:S(2)}) collective-permute-start(bf16[512,256]{1,0:T(8,128)(2,1)} %refs_7_.1), channel_id=1, source_target_pairs={{0,4},{1,5},{2,6},{3,7},{4,0},{5,1},{6,2},{7,3},{8,12},{9,13},{10,... | collective-permute-start | bytes 786440 | tf_op jit(solution)/shard_map/ppermute | solution.py:244
  8.9 10.5 %collective-permute-start.7 = (bf16[128,512]{1,0:T(8,128)(2,1)S(1)}, bf16[128,512]{1,0:T(8,128)(2,1)S(1)}, u32[]{:S(2)}, u32[]{:S(2)}) collective-permute-start(bf16[128,512]{1,0:T(8,128)(2,1)S(1)} %get-tuple-element.43), channel_id=1, source_target_pairs={{0,8},{1,9},{2,10},{3,11},{4,12},{5,13},{6,14},{7,15},{8,0},{9,1},... | collective-permute-start | bytes 393224 | tf_op jit(solution)/shard_map/ppermute | solution.py:244
  25.9 13.2 %collective-permute-start.16 = (bf16[128,512]{1,0:T(8,128)(2,1)}, bf16[128,512]{1,0:T(8,128)(2,1)S(1)}, u32[]{:S(2)}, u32[]{:S(2)}) collective-permute-start(bf16[128,512]{1,0:T(8,128)(2,1)} %get-tuple-element.19), channel_id=1, source_target_pairs={{0,16},{1,17},{2,18},{3,19},{4,20},{5,21},{6,22},{7,23},{8,24},{9,... | collective-permute-start | bytes 393224 | tf_op jit(solution)/shard_map/ppermute | solution.py:244
  40.2 21.6 %collective-permute-start.24 = (bf16[128,256]{1,0:T(8,128)(2,1)S(1)}, bf16[128,256]{1,0:T(8,128)(2,1)S(1)}, u32[]{:S(2)}, u32[]{:S(2)}) collective-permute-start(bf16[128,256]{1,0:T(8,128)(2,1)S(1)} %broadcast_select_fusion.8), channel_id=1, source_target_pairs={{0,28},{1,29},{2,30},{3,31},{4,24},{5,25},{6,26},{7,27},{8,20},{9,... | collective-permute-start | bytes 196616 | tf_op jit(solution)/shard_map/ppermute | solution.py:244
  43.6 14.6 %collective-permute-start.22 = (bf16[128,256]{1,0:T(8,128)(2,1)S(1)}, bf16[128,256]{1,0:T(8,128)(2,1)S(1)}, u32[]{:S(2)}, u32[]{:S(2)}) collective-permute-start(bf16[128,256]{1,0:T(8,128)(2,1)S(1)} %broadcast_select_fusion.8), channel_id=1, source_target_pairs={{0,20},{1,21},{2,22},{3,23},{4,16},{5,17},{6,18},{7,19},{8,28},{9,... | collective-permute-start | bytes 196616 | tf_op jit(solution)/shard_map/ppermute | solution.py:244
  45.2 13.0 %collective-permute-start.20 = (bf16[128,256]{1,0:T(8,128)(2,1)S(1)}, bf16[128,256]{1,0:T(8,128)(2,1)S(1)}, u32[]{:S(2)}, u32[]{:S(2)}) collective-permute-start(bf16[128,256]{1,0:T(8,128)(2,1)S(1)} %broadcast_select_fusion.8), channel_id=1, source_target_pairs={{0,12},{1,13},{2,14},{3,15},{4,8},{5,9},{6,10},{7,11},{8,4},{9,5},... | collective-permute-start | bytes 196616 | tf_op jit(solution)/shard_map/ppermute | solution.py:244
  47.0 11.1 %collective-permute-start.21 = (bf16[128,256]{1,0:T(8,128)(2,1)S(1)}, bf16[128,256]{1,0:T(8,128)(2,1)S(1)}, u32[]{:S(2)}, u32[]{:S(2)}) collective-permute-start(bf16[128,256]{1,0:T(8,128)(2,1)S(1)} %get-tuple-element.32), channel_id=1, source_target_pairs={{0,16},{1,17},{2,18},{3,19},{4,20},{5,21},{6,22},{7,23},{8,24},{9,... | collective-permute-start | bytes 196616 | tf_op jit(solution)/shard_map/ppermute | solution.py:244
  61.8 14.3 %collective-permute-start.26 = (bf16[8,128,256]{2,1,0:T(8,128)(2,1)S(1)}, bf16[8,128,256]{2,1,0:T(8,128)(2,1)S(1)}, u32[]{:S(2)}, u32[]{:S(2)}) collective-permute-start(bf16[8,128,256]{2,1,0:T(8,128)(2,1)S(1)} %bitcast_dynamic-update-slice_fusion.refs_0_), channel_id=1, source_target_pairs={{0,2},{1,3},{2,0},{3,1},{4,6},{5,7},{6,4},{7,5},{8,10},{9,11},{10,... | collective-permute-start | bytes 1572872 | tf_op jit(solution)/shard_map/ppermute | solution.py:244
  64.5 11.3 %collective-permute-start.34 = (bf16[128,896]{1,0:T(8,128)(2,1)S(1)}, bf16[128,896]{1,0:T(8,128)(2,1)S(1)}, u32[]{:S(2)}, u32[]{:S(2)}) collective-permute-start(bf16[128,896]{1,0:T(8,128)(2,1)S(1)} %get-tuple-element.33), channel_id=1, source_target_pairs={{0,28},{1,29},{2,30},{3,31},{4,24},{5,25},{6,26},{7,27},{8,20},{9,... | collective-permute-start | bytes 688136 | tf_op jit(solution)/shard_map/ppermute | solution.py:244
  66.7 47.3 %collective-permute-start.25 = (bf16[8,128,256]{2,1,0:T(8,128)(2,1)S(1)}, bf16[8,128,256]{2,1,0:T(8,128)(2,1)S(1)}, u32[]{:S(2)}, u32[]{:S(2)}) collective-permute-start(bf16[8,128,256]{2,1,0:T(8,128)(2,1)S(1)} %bitcast_dynamic-update-slice_fusion.refs_0_), channel_id=1, source_target_pairs={{0,1},{1,0},{2,3},{3,2},{4,5},{5,4},{6,7},{7,6},{8,9},{9,8},{10,11... | collective-permute-start | bytes 1572872 | tf_op jit(solution)/shard_map/ppermute | solution.py:244
  66.7 12.9 %collective-permute-start.29 = (bf16[128,896]{1,0:T(8,128)(2,1)S(1)}, bf16[128,896]{1,0:T(8,128)(2,1)S(1)}, u32[]{:S(2)}, u32[]{:S(2)}) collective-permute-start(bf16[128,896]{1,0:T(8,128)(2,1)S(1)} %get-tuple-element.34), channel_id=1, source_target_pairs={{0,8},{1,9},{2,10},{3,11},{4,12},{5,13},{6,14},{7,15},{8,0},{9,1},... | collective-permute-start | bytes 688136 | tf_op jit(solution)/shard_map/ppermute | solution.py:244
  66.7 18.2 %collective-permute-start.33 = (bf16[128,896]{1,0:T(8,128)(2,1)S(1)}, bf16[128,896]{1,0:T(8,128)(2,1)S(1)}, u32[]{:S(2)}, u32[]{:S(2)}) collective-permute-start(bf16[128,896]{1,0:T(8,128)(2,1)S(1)} %get-tuple-element.36), channel_id=1, source_target_pairs={{0,24},{1,25},{2,26},{3,27},{4,28},{5,29},{6,30},{7,31},{8,16},{9,... | collective-permute-start | bytes 688136 | tf_op jit(solution)/shard_map/ppermute | solution.py:244
  75.8 24.6 %collective-permute-start.31 = (bf16[128,896]{1,0:T(8,128)(2,1)S(1)}, bf16[128,896]{1,0:T(8,128)(2,1)S(1)}, u32[]{:S(2)}, u32[]{:S(2)}) collective-permute-start(bf16[128,896]{1,0:T(8,128)(2,1)S(1)} %get-tuple-element.37), channel_id=1, source_target_pairs={{0,16},{1,17},{2,18},{3,19},{4,20},{5,21},{6,22},{7,23},{8,24},{9,... | collective-permute-start | bytes 688136 | tf_op jit(solution)/shard_map/ppermute | solution.py:244
  76.1 38.7 %collective-permute-start.27 = (bf16[8,128,256]{2,1,0:T(8,128)(2,1)S(1)}, bf16[8,128,256]{2,1,0:T(8,128)(2,1)S(1)}, u32[]{:S(2)}, u32[]{:S(2)}) collective-permute-start(bf16[8,128,256]{2,1,0:T(8,128)(2,1)S(1)} %collective-permute-done.26.refs_2_), channel_id=1, source_target_pairs={{0,1},{1,0},{2,3},{3,2},{4,5},{5,4},{6,7},{7,6},{8,9},{9,8},{10,11... | collective-permute-start | bytes 1572872 | tf_op jit(solution)/shard_map/ppermute | solution.py:244
  79.6 21.0 %collective-permute-start.30 = (bf16[128,896]{1,0:T(8,128)(2,1)S(1)}, bf16[128,896]{1,0:T(8,128)(2,1)S(1)}, u32[]{:S(2)}, u32[]{:S(2)}) collective-permute-start(bf16[128,896]{1,0:T(8,128)(2,1)S(1)} %get-tuple-element.38), channel_id=1, source_target_pairs={{0,12},{1,13},{2,14},{3,15},{4,8},{5,9},{6,10},{7,11},{8,4},{9,5},... | collective-permute-start | bytes 688136 | tf_op jit(solution)/shard_map/ppermute | solution.py:244
  84.8 27.1 %collective-permute-start.32 = (bf16[128,896]{1,0:T(8,128)(2,1)S(1)}, bf16[128,896]{1,0:T(8,128)(2,1)S(1)}, u32[]{:S(2)}, u32[]{:S(2)}) collective-permute-start(bf16[128,896]{1,0:T(8,128)(2,1)S(1)} %get-tuple-element.39), channel_id=1, source_target_pairs={{0,20},{1,21},{2,22},{3,23},{4,16},{5,17},{6,18},{7,19},{8,28},{9,... | collective-permute-start | bytes 688136 | tf_op jit(solution)/shard_map/ppermute | solution.py:244
  100.4 11.6 %collective-permute-start.28 = (bf16[128,896]{1,0:T(8,128)(2,1)S(1)}, bf16[128,896]{1,0:T(8,128)(2,1)S(1)}, u32[]{:S(2)}, u32[]{:S(2)}) collective-permute-start(bf16[128,896]{1,0:T(8,128)(2,1)S(1)} %get-tuple-element.40), channel_id=1, source_target_pairs={{0,4},{1,5},{2,6},{3,7},{4,0},{5,1},{6,2},{7,3},{8,12},{9,13},{10,... | collective-permute-start | bytes 688136 | tf_op jit(solution)/shard_map/ppermute | solution.py:244
  100.6 22.5 %collective-permute-start.5 = (bf16[54,16,128]{2,1,0:T(8,128)(2,1)S(1)}, bf16[54,16,128]{2,1,0:T(8,128)(2,1)}, u32[]{:S(2)}, u32[]{:S(2)}) collective-permute-start(bf16[54,16,128]{2,1,0:T(8,128)(2,1)S(1)} %slice.28.refs_0_), channel_id=1, source_target_pairs={{0,24},{1,25},{2,26},{3,27},{4,28},{5,29},{6,30},{7,31},{8,16},{9,... | collective-permute-start | bytes 663560 | tf_op jit(solution)/shard_map/ppermute | solution.py:244
  111.9 11.3 %collective-permute-start.3 = (bf16[54,16,128]{2,1,0:T(8,128)(2,1)S(1)}, bf16[54,16,128]{2,1,0:T(8,128)(2,1)}, u32[]{:S(2)}, u32[]{:S(2)}) collective-permute-start(bf16[54,16,128]{2,1,0:T(8,128)(2,1)S(1)} %slice.28.refs_0_), channel_id=1, source_target_pairs={{0,16},{1,17},{2,18},{3,19},{4,20},{5,21},{6,22},{7,23},{8,24},{9,... | collective-permute-start | bytes 663560 | tf_op jit(solution)/shard_map/ppermute | solution.py:244
  112.0 13.1 %collective-permute-start.1 = (bf16[54,16,128]{2,1,0:T(8,128)(2,1)S(1)}, bf16[54,16,128]{2,1,0:T(8,128)(2,1)}, u32[]{:S(2)}, u32[]{:S(2)}) collective-permute-start(bf16[54,16,128]{2,1,0:T(8,128)(2,1)S(1)} %slice.28.refs_0_), channel_id=1, source_target_pairs={{0,8},{1,9},{2,10},{3,11},{4,12},{5,13},{6,14},{7,15},{8,0},{9,1},... | collective-permute-start | bytes 663560 | tf_op jit(solution)/shard_map/ppermute | solution.py:244
  114.0 11.7 %collective-permute-start = (bf16[54,16,128]{2,1,0:T(8,128)(2,1)S(1)}, bf16[54,16,128]{2,1,0:T(8,128)(2,1)S(1)}, u32[]{:S(2)}, u32[]{:S(2)}) collective-permute-start(bf16[54,16,128]{2,1,0:T(8,128)(2,1)S(1)} %slice.28.refs_0_), channel_id=1, source_target_pairs={{0,4},{1,5},{2,6},{3,7},{4,0},{5,1},{6,2},{7,3},{8,12},{9,13},{10,... | collective-permute-start | bytes 663560 | tf_op jit(solution)/shard_map/ppermute | solution.py:244
  121.7 24.1 %collective-permute-start.35 = (bf16[128,896]{1,0:T(8,128)(2,1)}, bf16[128,896]{1,0:T(8,128)(2,1)S(1)}, u32[]{:S(2)}, u32[]{:S(2)}) collective-permute-start(bf16[128,896]{1,0:T(8,128)(2,1)} %get-tuple-element.22), channel_id=1, source_target_pairs={{0,4},{1,5},{2,6},{3,7},{4,0},{5,1},{6,2},{7,3},{8,12},{9,13},{10,... | collective-permute-start | bytes 688136 | tf_op jit(solution)/shard_map/ppermute | solution.py:244
  123.0 27.8 %collective-permute-start.36 = (bf16[128,896]{1,0:T(8,128)(2,1)}, bf16[128,896]{1,0:T(8,128)(2,1)S(1)}, u32[]{:S(2)}, u32[]{:S(2)}) collective-permute-start(bf16[128,896]{1,0:T(8,128)(2,1)} %get-tuple-element.23), channel_id=1, source_target_pairs={{0,8},{1,9},{2,10},{3,11},{4,12},{5,13},{6,14},{7,15},{8,0},{9,1},... | collective-permute-start | bytes 688136 | tf_op jit(solution)/shard_map/ppermute | solution.py:244
  123.2 14.4 %collective-permute-start.6 = (bf16[54,16,128]{2,1,0:T(8,128)(2,1)}, bf16[54,16,128]{2,1,0:T(8,128)(2,1)S(1)}, u32[]{:S(2)}, u32[]{:S(2)}) collective-permute-start(bf16[54,16,128]{2,1,0:T(8,128)(2,1)} %collective-permute-done.5.refs_6_), channel_id=1, source_target_pairs={{0,4},{1,5},{2,6},{3,7},{4,0},{5,1},{6,2},{7,3},{8,12},{9,13},{10,... | collective-permute-start | bytes 663560 | tf_op jit(solution)/shard_map/ppermute | solution.py:244
  125.1 16.1 %collective-permute-start.4 = (bf16[54,16,128]{2,1,0:T(8,128)(2,1)}, bf16[54,16,128]{2,1,0:T(8,128)(2,1)S(1)}, u32[]{:S(2)}, u32[]{:S(2)}) collective-permute-start(bf16[54,16,128]{2,1,0:T(8,128)(2,1)} %collective-permute-done.3.refs_4_), channel_id=1, source_target_pairs={{0,4},{1,5},{2,6},{3,7},{4,0},{5,1},{6,2},{7,3},{8,12},{9,13},{10,... | collective-permute-start | bytes 663560 | tf_op jit(solution)/shard_map/ppermute | solution.py:244
  125.7 20.1 %collective-permute-start.2 = (bf16[54,16,128]{2,1,0:T(8,128)(2,1)}, bf16[54,16,128]{2,1,0:T(8,128)(2,1)S(1)}, u32[]{:S(2)}, u32[]{:S(2)}) collective-permute-start(bf16[54,16,128]{2,1,0:T(8,128)(2,1)} %collective-permute-done.1.refs_2_), channel_id=1, source_target_pairs={{0,4},{1,5},{2,6},{3,7},{4,0},{5,1},{6,2},{7,3},{8,12},{9,13},{10,... | collective-permute-start | bytes 663560 | tf_op jit(solution)/shard_map/ppermute | solution.py:244
  137.7 20.2 %collective-permute-start.37 = (bf16[128,896]{1,0:T(8,128)(2,1)}, bf16[128,896]{1,0:T(8,128)(2,1)S(1)}, u32[]{:S(2)}, u32[]{:S(2)}) collective-permute-start(bf16[128,896]{1,0:T(8,128)(2,1)} %get-tuple-element.24), channel_id=1, source_target_pairs={{0,12},{1,13},{2,14},{3,15},{4,8},{5,9},{6,10},{7,11},{8,4},{9,5},... | collective-permute-start | bytes 688136 | tf_op jit(solution)/shard_map/ppermute | solution.py:244
  141.2 24.8 %collective-permute-start.38 = (bf16[128,896]{1,0:T(8,128)(2,1)}, bf16[128,896]{1,0:T(8,128)(2,1)S(1)}, u32[]{:S(2)}, u32[]{:S(2)}) collective-permute-start(bf16[128,896]{1,0:T(8,128)(2,1)} %get-tuple-element.25), channel_id=1, source_target_pairs={{0,16},{1,17},{2,18},{3,19},{4,20},{5,21},{6,22},{7,23},{8,24},{9,... | collective-permute-start | bytes 688136 | tf_op jit(solution)/shard_map/ppermute | solution.py:244
  145.8 26.4 %collective-permute-start.39 = (bf16[128,896]{1,0:T(8,128)(2,1)}, bf16[128,896]{1,0:T(8,128)(2,1)S(1)}, u32[]{:S(2)}, u32[]{:S(2)}) collective-permute-start(bf16[128,896]{1,0:T(8,128)(2,1)} %get-tuple-element.26), channel_id=1, source_target_pairs={{0,20},{1,21},{2,22},{3,23},{4,16},{5,17},{6,18},{7,19},{8,28},{9,... | collective-permute-start | bytes 688136 | tf_op jit(solution)/shard_map/ppermute | solution.py:244
  145.8 26.4 %collective-permute-start.40 = (bf16[128,896]{1,0:T(8,128)(2,1)}, bf16[128,896]{1,0:T(8,128)(2,1)S(1)}, u32[]{:S(2)}, u32[]{:S(2)}) collective-permute-start(bf16[128,896]{1,0:T(8,128)(2,1)} %get-tuple-element.27), channel_id=1, source_target_pairs={{0,24},{1,25},{2,26},{3,27},{4,28},{5,29},{6,30},{7,31},{8,16},{9,... | collective-permute-start | bytes 688136 | tf_op jit(solution)/shard_map/ppermute | solution.py:244
  150.8 21.4 %collective-permute-start.41 = (bf16[128,896]{1,0:T(8,128)(2,1)}, bf16[128,896]{1,0:T(8,128)(2,1)S(1)}, u32[]{:S(2)}, u32[]{:S(2)}) collective-permute-start(bf16[128,896]{1,0:T(8,128)(2,1)} %get-tuple-element.28), channel_id=1, source_target_pairs={{0,28},{1,29},{2,30},{3,31},{4,24},{5,25},{6,26},{7,27},{8,20},{9,... | collective-permute-start | bytes 688136 | tf_op jit(solution)/shard_map/ppermute | solution.py:244
  (47 other events, 606.2 us)

commit v2 on v1

--- a/solution.py
+++ b/solution.py
@@ -5,6 +5,7 @@
 from jax import lax
 from jax.experimental import pallas as pl
 from jax.experimental.pallas import tpu as pltpu
+from jax.sharding import Mesh
 from jax.sharding import PartitionSpec as P
 
 BLK = 128
@@ -95,6 +96,7 @@
 VMEM = pl.BlockSpec(memory_space=pltpu.VMEM)
 SMEM = pl.BlockSpec(memory_space=pltpu.SMEM)
 BF16, F32 = jnp.bfloat16, jnp.float32
+AXES = ("z", "x", "y", "c")
 
 
 def at(start, size):
@@ -137,33 +139,43 @@
         outs[j - 1][...] = total[j * rows : (j + 1) * rows].astype(BF16)
 
 
-def lowrank_kernel(nf, nt, idx, *refs):
+def rank_round_kernel(own, *refs):
+    others, out = refs[:-1], refs[-1]
+    total = own[...]
+    for other in others:
+        total = total + other[...].astype(F32)
+    width = out.shape[2]
+    for k in range(out.shape[0]):
+        out[k] = total[:, k % 2 * width : (k % 2 + 1) * width].astype(BF16)
+
+
+def lowrank_kernel(nf, nt, slots, idx, *refs):
     ranks, rights = refs[:nt], refs[nt : nt + nf]
-    outs = refs[nt + nf : nt + 2 * nf]
-    rank, weight, sems = refs[nt + 2 * nf :]
+    outs = refs[nt + nf : nt + nf + len(slots)]
+    rank, weight, sems = refs[nt + nf + len(slots) :]
     f, t = idx[3], idx[4]
-    pairs = [(ranks[s], rank.at[t ^ s]) for s in range(nt)]
-    pairs += [(rights[k], weight.at[f ^ k]) for k in range(nf)]
+    slice_width = ranks[0].shape[2]
+    pairs = [(rights[k], weight.at[f ^ k]) for k in range(nf)]
+    for s in range(nt):
+        lanes = at((t ^ s) * slice_width, slice_width)
+        pairs += [(ranks[s].at[f ^ m], rank.at[i, :, lanes]) for i, m in enumerate(slots)]
     for copy in run_copies(pairs, sems):
         copy.wait()
-    rows, width = rank.shape[2], rank.shape[3]
+    count, rows, depth = rank.shape
     cols = weight.shape[2]
-    weights = weight[...].reshape(nt, width, cols)
-    group = min(4, nf)
-    for m in range(0, nf, group):
-        total = None
-        for s in range(nt):
-            lhs = rank[s, m : m + group].reshape(group * rows, width)
-            part = jnp.dot(lhs, weights[s], preferred_element_type=F32)
-            total = part if total is None else total + part
-        for i in range(group):
-            outs[m + i][...] = total[i * rows : (i + 1) * rows].astype(BF16)
+    weights = weight[...].reshape(depth, cols)
+    total = jnp.dot(rank[...].reshape(count * rows, depth), weights, preferred_element_type=F32)
+    for i in range(count):
+        outs[i][...] = total[i * rows : (i + 1) * rows].astype(BF16)
 
 
 def sparse_kernel(nf, idx, gate_rows, gate_cols, up_rows, up_cols, tokens, *refs):
     values, out, blocks, sems = refs[:nf], refs[nf], refs[nf + 1], refs[nf + 2]
-    f = idx[3]
-    copies = run_copies([(values[k], blocks.at[:, f ^ k]) for k in range(nf)], sems)
+    z, f = idx[0], idx[3]
+    inner = jnp.logical_or(z == 1, z == 2)
+    across = jnp.where(inner, 6, 4)
+    slots = [0, 1, 2, 3, across, across + 1, 10 - across, 11 - across]
+    copies = run_copies([(v, blocks.at[:, f ^ k]) for v, k in zip(values, slots)], sems)
     out[...] = jnp.zeros_like(out)
     for copy in copies:
         copy.wait()
@@ -180,16 +192,36 @@
         lax.fori_loop(0, count, step, 0, unroll=True)
 
 
-def final_kernel(nf, idx, gate_rows, gate_cols, up_rows, up_cols, tokens, grad, sparse, *refs):
-    pieces, hidden, grads = refs[:nf], refs[nf], refs[nf + 1]
-    pre, dpre, sems = refs[nf + 2 :]
-    f = idx[3]
+def final_kernel(nf, idx, gate_rows, gate_cols, up_rows, up_cols, *refs):
+    nz = nf // 2
+    tokens_in, grad_in, sparse_in = refs[:3]
+    pieces = refs[3 : nf + 3]
+    hidden_out, gate_keep_out, gate_send_out, up_keep_out = refs[nf + 3 : nf + 7]
+    up_send_outs = refs[nf + 7 : nf + 6 + nz]
+    tokens, grad, sparse, pre, dpre, hidden = refs[nf + 6 + nz : nf + 12 + nz]
+    gate_keep, gate_send, up_keep, up_send, sems, out_sems = refs[nf + 12 + nz :]
+    z, x, f = idx[0], idx[1], idx[3]
+    width = pre.shape[3]
     pairs = [(pieces[k], pre.at[(f ^ k) % 2, (f ^ k) // 2]) for k in range(nf)]
-    for copy in run_copies(pairs, sems):
+    for j in range(nz):
+        here = pl.ds(j * width, width)
+        pairs.append((sparse_in.at[:, :, here], sparse.at[:, :, here]))
+        pairs.append((grad_in.at[:, here], grad.at[:, here]))
+    pairs.append((tokens_in, tokens))
+    copies = run_copies(pairs, sems)
+    for copy in copies[:nf]:
         copy.wait()
-    width = pre.shape[3]
-    for j in range(pre.shape[1]):
+    sent = []
+
+    def send(source, target):
+        copy = pltpu.make_async_copy(source, target, out_sems.at[len(sent)])
+        copy.start()
+        sent.append(copy)
+
+    for j in range(nz):
         here = pl.ds(j * width, width)
+        copies[nf + 2 * j].wait()
+        copies[nf + 2 * j + 1].wait()
         gate = pre[0, j].astype(F32) + sparse[0, :, here]
         up = pre[1, j].astype(F32) + sparse[1, :, here]
         sigma = jax.nn.sigmoid(gate)
@@ -198,19 +230,49 @@
         dpre[0, :, here] = (upstream * up * sigma * (1.0 + gate * (1.0 - sigma))).astype(BF16)
         dpre[1, :, here] = (upstream * silu).astype(BF16)
         hidden[:, here] = (silu * up).astype(BF16)
+        send(hidden.at[:, here], hidden_out.at[:, here])
+    copies[-1].wait()
     count = gate_rows.shape[0]
-    for p, (rows, cols) in enumerate(((gate_rows, gate_cols), (up_rows, up_cols))):
-
-        def step(k, carry, p=p, rows=rows, cols=cols):
-            source = tokens[:, at(rows[k] * BLK, BLK)]
-            picked = dpre[p, :, at(cols[k] * BLK, BLK)]
-            value = lax.dot_general(
-                source, picked, (((0,), (0,)), ((), ())), preferred_element_type=F32
-            )
-            grads[:, p * count + k] = value.astype(BF16).reshape(nf, BLK // nf, BLK)
-            return carry
-
-        lax.fori_loop(0, count, step, 0, unroll=True)
+
+    def partial(p, rows, cols, k):
+        source = tokens[:, at(rows[k] * BLK, BLK)]
+        picked = dpre[p, :, at(cols[k] * BLK, BLK)]
+        value = lax.dot_general(
+            source, picked, (((0,), (0,)), ((), ())), preferred_element_type=F32
+        )
+        return value.reshape(nz, 2, BLK // nf, BLK)
+
+    def up_step(k, carry):
+        value = partial(1, up_rows, up_cols, k)
+        for j in range(nz):
+            up_keep[z ^ j, :, k] = value[j]
+            up_send[z ^ j, :, k] = value[j].astype(BF16)
+        return carry
+
+    def gate_step(k, carry):
+        value = partial(0, gate_rows, gate_cols, k)
+        keep = jnp.where(x == 0, value[:, 0], value[:, 1])
+        other = jnp.where(x == 0, value[:, 1], value[:, 0]).astype(BF16)
+        for j in range(nz):
+            gate_keep[z ^ j, k] = keep[j]
+            gate_send[z ^ j, k] = other[j]
+        return carry
+
+    lax.fori_loop(0, count, up_step, 0, unroll=True)
+    for j in range(1, nz):
+        send(up_send.at[j], up_send_outs[j - 1])
+    send(up_keep.at[0], up_keep_out)
+    lax.fori_loop(0, count, gate_step, 0, unroll=True)
+    send(gate_send, gate_send_out)
+    send(gate_keep, gate_keep_out)
+    for copy in sent:
+        copy.wait()
+
+
+def gate_add_kernel(keep, got, own, *sends):
+    own[...] = keep[0] + got[0].astype(F32)
+    for j, send in enumerate(sends, 1):
+        send[...] = (keep[j] + got[j].astype(F32)).astype(BF16)
 
 
 def exchange_device(
@@ -235,13 +297,13 @@
     cols = width // nz
     count = gate_values.shape[0]
     share = BLK // nf
-    f, t = lax.axis_index("fsdp"), lax.axis_index("tp")
-    z, x, c = f // 2, f % 2, t % 2
+    z, x, c = lax.axis_index("z"), lax.axis_index("x"), lax.axis_index("c")
+    f, t = 2 * z + x, 2 * lax.axis_index("y") + c
     idx = jnp.stack([z, x, c, f, t]).astype(jnp.int32)
 
-    def move(value, df=0, dt=0):
-        pairs = [(i * nt + j, (i ^ df) * nt + (j ^ dt)) for i in range(nf) for j in range(nt)]
-        return lax.ppermute(value, ("fsdp", "tp"), pairs)
+    def move(value, df=0, dt=0, only=range(nf)):
+        pairs = [(i, i ^ (df * nt + dt)) for i in range(nf * nt) if i // (2 * nt) in only]
+        return lax.ppermute(value, AXES, pairs)
 
     halves = [
         lax.dynamic_slice(tokens, (0, (z ^ j) * 2 * depth + c * depth), (rows, depth))
@@ -263,17 +325,16 @@
         ],
         name="rank_partial",
     )(idx, tokens, *mine, *other, gate_left, up_left, recv_g, recv_u)
-    total = sums[0]
-    for j in range(1, nz):
-        total = total + move(sums[j], df=2 * j).astype(F32)
-    rank = total.astype(BF16)
-    rank_gate, rank_up = rank[:, :slice_width], rank[:, slice_width:]
-    rank_own = jnp.where(x == 0, rank_gate, rank_up)
-    rank_other = jnp.where(x == 0, rank_up, rank_gate)
-    slots = [rank_own] + [move(rank_other if k % 2 else rank_own, df=k) for k in range(1, nf)]
-    stack = jnp.stack(slots)
-    ranks = [stack, move(stack, dt=1)]
-    ranks.append(move(stack, dt=2))
+    got = [move(sums[j], df=2 * j) for j in range(1, nz)]
+    for_f = pl.pallas_call(
+        rank_round_kernel,
+        out_shape=jax.ShapeDtypeStruct((nf, rows, slice_width), BF16),
+        in_specs=[VMEM] * nz,
+        out_specs=VMEM,
+        name="rank_round",
+    )(sums[0], *got)
+    stack = lax.all_to_all(for_f, ("z", "x"), 0, 0, tiled=True)
+    ranks = [stack, move(stack, dt=1), move(stack, dt=2)]
     ranks.append(move(ranks[2], dt=1))
 
     rights = []
@@ -290,10 +351,16 @@
     rights = [rights[0]] + [move(rights[k], df=k) for k in range(1, nf)]
 
     own_values = jnp.concatenate([gate_values, up_values], 0).reshape(2 * count, share, BLK)
-    over_z = [own_values] + [move(own_values, df=2 * j) for j in range(1, nz)]
-    values = []
-    for j in range(nz):
-        values += [over_z[j], move(over_z[j], df=1)]
+    near = move(own_values, df=2)
+    inner = (z == 1) | (z == 2)
+    from_across = [
+        jnp.where(inner, got, move(got, df=2, only=(1, 2)))
+        for got in (move(v, df=6, only=(1, 2)) for v in (own_values, near))
+    ]
+    values = [own_values, move(own_values, df=1)]
+    values += [near, move(near, df=1)]
+    for v in from_across:
+        values += [v, move(v, df=1)]
     base = t * (width // BLK)
     index = (idx, gate_rows, gate_cols - base, up_rows, up_cols - base)
     sparse = pl.pallas_call(
@@ -308,67 +375,98 @@
         name="sparse_forward",
     )(*index, tokens, *values)
 
-    lowrank = pl.pallas_call(
-        functools.partial(lowrank_kernel, nf, nt),
-        out_shape=[jax.ShapeDtypeStruct((rows, cols), BF16)] * nf,
-        in_specs=[SMEM] + [ANY] * (nt + nf),
-        out_specs=[VMEM] * nf,
-        scratch_shapes=[
-            pltpu.VMEM((nt, nf, rows, slice_width), BF16),
-            pltpu.VMEM((nf, gate_right.shape[0], cols), BF16),
-            pltpu.SemaphoreType.DMA((nt + nf,)),
-        ],
-        name="lowrank",
-    )(idx, *ranks, *rights)
-    pieces = [lowrank[0]] + [move(lowrank[k], df=k) for k in range(1, nf)]
-
-    hidden, grads = pl.pallas_call(
+    pieces = [None] * nf
+    for slots in (range(nf // 2, nf), range(nf // 2)):
+        lowrank = pl.pallas_call(
+            functools.partial(lowrank_kernel, nf, nt, slots),
+            out_shape=[jax.ShapeDtypeStruct((rows, cols), BF16)] * len(slots),
+            in_specs=[SMEM] + [ANY] * (nt + nf),
+            out_specs=[VMEM] * len(slots),
+            scratch_shapes=[
+                pltpu.VMEM((len(slots), rows, nt * slice_width), BF16),
+                pltpu.VMEM((nf, gate_right.shape[0], cols), BF16),
+                pltpu.SemaphoreType.DMA((nt * len(slots) + nf,)),
+            ],
+            name="lowrank",
+        )(idx, *ranks, *rights)
+        for k, product in zip(slots, lowrank):
+            pieces[k] = move(product, df=k) if k else product
+
+    support = (count, share, BLK)
+    outs = pl.pallas_call(
         functools.partial(final_kernel, nf),
         out_shape=[
             jax.ShapeDtypeStruct((rows, width), BF16),
-            jax.ShapeDtypeStruct((nf, 2 * count, share, BLK), BF16),
-        ],
-        in_specs=[SMEM] * 5 + [VMEM] * 3 + [ANY] * nf,
-        out_specs=[VMEM] * 2,
+            jax.ShapeDtypeStruct((nz,) + support, F32),
+            jax.ShapeDtypeStruct((nz,) + support, BF16),
+            jax.ShapeDtypeStruct((2,) + support, F32),
+        ]
+        + [jax.ShapeDtypeStruct((2,) + support, BF16)] * (nz - 1),
+        in_specs=[SMEM] * 5 + [ANY] * (nf + 3),
+        out_specs=[ANY] * (nz + 3),
         scratch_shapes=[
+            pltpu.VMEM(tokens.shape, BF16),
+            pltpu.VMEM((rows, width), BF16),
+            pltpu.VMEM((2, rows, width), F32),
             pltpu.VMEM((2, nz, rows, cols), BF16),
             pltpu.VMEM((2, rows, width), BF16),
-            pltpu.SemaphoreType.DMA((nf,)),
+            pltpu.VMEM((rows, width), BF16),
+            pltpu.VMEM((nz,) + support, F32),
+            pltpu.VMEM((nz,) + support, BF16),
+            pltpu.VMEM((nz, 2) + support, F32),
+            pltpu.VMEM((nz, 2) + support, BF16),
+            pltpu.SemaphoreType.DMA((nf + 2 * nz + 1,)),
+            pltpu.SemaphoreType.DMA((2 * nz + 2,)),
         ],
         name="hidden_and_grads",
     )(*index, tokens, grad_hidden, sparse, *pieces)
-    shares = lax.all_to_all(grads, "fsdp", 0, 0, tiled=True)
-    summed = jnp.sum(shares.astype(F32), axis=0).reshape(2 * count, share * BLK)
-    return hidden, summed[:count], summed[count:]
-
-
-def dispatch(mesh, *args):
+    hidden, gate_keep, gate_send, up_keep, *up_sends = outs
+
+    up_sum = up_keep
+    for j in range(1, nz):
+        up_sum = up_sum + move(up_sends[j - 1], df=2 * j).astype(F32)
+    gate_got = move(gate_send, df=1)
+    gate_total, *gate_sums = pl.pallas_call(
+        gate_add_kernel,
+        out_shape=[jax.ShapeDtypeStruct(support, F32)]
+        + [jax.ShapeDtypeStruct(support, BF16)] * (nz - 1),
+        in_specs=[VMEM] * 2,
+        out_specs=[VMEM] * nz,
+        name="gate_add",
+    )(gate_keep, gate_got)
+    for j in range(1, nz):
+        gate_total = gate_total + move(gate_sums[j - 1], df=2 * j).astype(F32)
+    up_here = jnp.where(x == 0, up_sum[0], up_sum[1])
+    up_there = jnp.where(x == 0, up_sum[1], up_sum[0]).astype(BF16)
+    up_total = up_here + move(up_there, df=1).astype(F32)
+    return hidden, gate_total.reshape(count, share * BLK), up_total.reshape(count, share * BLK)
+
+
+def placed(mesh, axes, step):
+    fsdp, tp = axes
+    both = P(fsdp, tp)
+    swapped = P(tp, fsdp)
+    return jax.shard_map(
+        step,
+        mesh=mesh,
+        in_specs=(P(fsdp, None),) + (both, both, swapped, P(tp), P(tp)) * 2 + (both,),
+        out_specs=(both, swapped, swapped),
+        check_vma=False,
+    )
+
+
+def solution(mesh):
     nf, nt = mesh.shape["fsdp"], mesh.shape["tp"]
-    width = args[2].shape[1]
-    direct = nf in (4, 8) and nt == 4 and width % (BLK * (nf // 2)) == 0
-    if direct:
-        return exchange_device(mesh, *args)
-    return on_device(*args)
-
-
-def solution(mesh):
-    return jax.shard_map(
-        functools.partial(dispatch, mesh),
-        mesh=mesh,
-        in_specs=(
-            P("fsdp", None),
-            P("fsdp", "tp"),
-            P("fsdp", "tp"),
-            P("tp", "fsdp"),
-            P("tp"),
-            P("tp"),
-            P("fsdp", "tp"),
-            P("fsdp", "tp"),
-            P("tp", "fsdp"),
-            P("tp"),
-            P("tp"),
-            P("fsdp", "tp"),
-        ),
-        out_specs=(P("fsdp", "tp"), P("tp", "fsdp"), P("tp", "fsdp")),
-        check_vma=False,
-    )
+
+    def step(*args):
+        width = args[2].shape[1] // nt
+        if nf == 8 and nt == 4 and width % (BLK * (nf // 2)) == 0:
+            split = Mesh(mesh.devices.reshape(nf // 2, 2, 2, 2), AXES)
+
+            def body(*local):
+                return exchange_device(mesh, *local)
+
+            return placed(split, (("z", "x"), ("y", "c")), body)(*args)
+        return placed(mesh, ("fsdp", "tp"), on_device)(*args)
+
+    return step

time: 232 us -> 222 us (0.957)
  blocking collectives: 47.2 us -> 19.6 us
  starting transfers between devices: 55.2 us -> 75.6 us
  waiting for transfers between devices: 94 us -> 81 us
  Pallas kernels: 24.5 us -> 29.9 us
  other arithmetic: 2.91 us -> 6.62 us
    all_to_all x1, blocking collectives: 47.2 us -> 19.6 us  [exchange_device(): stack = lax.all_to_all(for_f, ('z', 'x'), 0, 0, tiled=True)]
    ppermute x42 -> x45, starting transfers between devices: 55.2 us -> 75.6 us  [move(): return lax.ppermute(value, AXES, pairs)]
    ppermute x42 -> x45, waiting for transfers between devices: 94 us -> 81 us  [move(): return lax.ppermute(value, AXES, pairs)]
    pallas_call x1 -> x4, Pallas kernels: 6.14 us -> 13.7 us  [the longest x2 9.66 us: exchange_device(): pl.pallas_call(functools.partial(lowrank_kernel, nf, nt, slots), out_shap...]
    select_n x1 -> x2, other arithmetic: 0.01 us -> 2.63 us  [exchange_device(): jnp.where(inner, got, move(got, df=2, only=(1, 2)))]
    unnamed x85 -> x87, local copies, waits for them, and re-layouts: 4.46 us -> 5.85 us
  transfers between devices with their start and end apart: 42 -> 45, of which waited for: 19 -> 20; matrix products, arithmetic and copies ran while one was open for 1% -> 4% of each run, Pallas kernels for 5% -> 8%
where the time goes in v2:
time: 222 us
  waiting for transfers between devices  81 us (36%)
  starting transfers between devices  75.6 us (34%)
  Pallas kernels  29.9 us (13%)
  blocking collectives  19.6 us (9%)
  local copies, waits for them, and re-layouts  7.65 us (3%)
  other arithmetic  6.62 us (3%)
    ppermute x45, waiting for transfers between devices, move(): return lax.ppermute(value, AXES, pairs)  81 us
    ppermute x45, starting transfers between devices, move(): return lax.ppermute(value, AXES, pairs)  75.6 us
    all_to_all x1, blocking collectives, exchange_device(): stack = lax.all_to_all(for_f, ('z', 'x'), 0, 0, tiled=True)  19.6 us
    pallas_call x2, Pallas kernels, exchange_device(): pl.pallas_call(functools.partial(lowrank_kernel, nf, nt, slots), out_shap...  9.66 us
    pallas_call x1, Pallas kernels, exchange_device(): pl.pallas_call(functools.partial(final_kernel, nf), out_shape=[jax.ShapeD...  6.72 us
    unnamed x87, local copies, waits for them, and re-layouts  5.85 us
    pallas_call x1, Pallas kernels, exchange_device(): pl.pallas_call(functools.partial(sparse_kernel, nf), out_shape=jax.ShapeD...  5.79 us
  transfers between devices with their start and end apart: 45, of which 20 were waited for; matrix products, arithmetic and copies ran while one was open for 4% of the time, Pallas kernels for 8%

profile of v2, /device:TPU:0, one launch (start us, length us, event | category | flops | bytes accessed | tf_op | source)
XLA Modules:
  0.0 221.6 jit_solution(6176086362840731708)
XLA Ops:
  0.7 3.0 %collective-permute-start.15 = (bf16[512,256]{1,0:T(8,128)(2,1)}, bf16[512,256]{1,0:T(8,128)(2,1)S(1)}, u32[]{:S(2)}, u32[]{:S(2)}) collective-permute-start(bf16[512,256]{1,0:T(8,128)(2,1)} %refs_6_.1), channel_id=1, source_target_pairs={{0,4},{1,5},{2,6},{3,7},{4,0},{5,1},{6,2},{7,3},{8,12},{9,13},{10,... | collective-permute-start | bytes 786440 | tf_op jit(solution)/shard_map/ppermute | solution.py:306
  5.0 4.1 %collective-permute-start.11 = (bf16[128,512]{1,0:T(8,128)(2,1)S(1)}, bf16[128,512]{1,0:T(8,128)(2,1)S(1)}, u32[]{:S(2)}, u32[]{:S(2)}) collective-permute-start(bf16[128,512]{1,0:T(8,128)(2,1)S(1)} %get-tuple-element.57), channel_id=1, source_target_pairs={{0,24},{1,25},{2,26},{3,27},{4,28},{5,29},{6,30},{7,31},{8,16},{9,... | collective-permute-start | bytes 393224 | tf_op jit(solution)/shard_map/ppermute | solution.py:306
  9.7 3.8 %collective-permute-done.11.refs_2_ = bf16[128,512]{1,0:T(8,128)(2,1)S(1)} collective-permute-done((bf16[128,512]{1,0:T(8,128)(2,1)S(1)}, bf16[128,512]{1,0:T(8,128)(2,1)S(1)}, u32[]{:S(2)}, u32[]{:S(2)}) %collective-permute-start.11) | collective-permute-done | bytes 131104 | tf_op jit(solution)/shard_map/ppermute | solution.py:306
  13.5 6.1 %collective-permute-done.10.refs_1_ = bf16[128,512]{1,0:T(8,128)(2,1)S(1)} collective-permute-done((bf16[128,512]{1,0:T(8,128)(2,1)S(1)}, bf16[128,512]{1,0:T(8,128)(2,1)S(1)}, u32[]{:S(2)}, u32[]{:S(2)}) %collective-permute-start.10) | collective-permute-done | bytes 131104 | tf_op jit(solution)/shard_map/ppermute | solution.py:306
  22.2 3.7 %rank_partial.1 = (f32[128,512]{1,0:T(8,128)}, bf16[128,512]{1,0:T(8,128)(2,1)}, bf16[128,512]{1,0:T(8,128)(2,1)}, bf16[128,512]{1,0:T(8,128)(2,1)}) custom-call(s32[5]{0:T(128)} %stack.23.idx, bf16[128,4096]{1,0:T(8,128)(2,1)} %refs_0_.1, bf16[128,512]{1,0:T(8,128)(2,1)} %copy-done.28, bf16[128,512]{1,0:T(8,128)(2,1)} %copy-done.27, ...), custom_call_target="tpu_custom_call" | custom-call | tf_op jit(solution)/shard_map/rank_partial/pallas_call | solution.py:315
  26.0 3.0 %collective-permute-start.18 = (bf16[128,512]{1,0:T(8,128)(2,1)}, bf16[128,512]{1,0:T(8,128)(2,1)S(1)}, u32[]{:S(2)}, u32[]{:S(2)}) collective-permute-start(bf16[128,512]{1,0:T(8,128)(2,1)} %get-tuple-element.28), channel_id=1, source_target_pairs={{0,16},{1,17},{2,18},{3,19},{4,20},{5,21},{6,22},{7,23},{8,24},{9,... | collective-permute-start | bytes 393224 | tf_op jit(solution)/shard_map/ppermute | solution.py:306
  30.4 3.7 %collective-permute-done.17.refs_0_ = bf16[128,512]{1,0:T(8,128)(2,1)S(1)} collective-permute-done((bf16[128,512]{1,0:T(8,128)(2,1)}, bf16[128,512]{1,0:T(8,128)(2,1)S(1)}, u32[]{:S(2)}, u32[]{:S(2)}) %collective-permute-start.17) | collective-permute-done | bytes 131104 | tf_op jit(solution)/shard_map/ppermute | solution.py:306
  34.1 5.2 %collective-permute-done.18.refs_1_ = bf16[128,512]{1,0:T(8,128)(2,1)S(1)} collective-permute-done((bf16[128,512]{1,0:T(8,128)(2,1)}, bf16[128,512]{1,0:T(8,128)(2,1)S(1)}, u32[]{:S(2)}, u32[]{:S(2)}) %collective-permute-start.18) | collective-permute-done | bytes 131104 | tf_op jit(solution)/shard_map/ppermute | solution.py:306
  41.9 19.6 %all_to_all.5.refs_0_ = bf16[8,128,256]{2,1,0:T(8,128)(2,1)S(1)} all-to-all(bf16[8,128,256]{2,1,0:T(8,128)(2,1)} %rank_round.1), channel_id=1, replica_groups=mesh['z'=4,'x'=2,'y'=2,'c'=2] {'z','x'}, dimensions={0} | all-to-all | bytes 1048576 | tf_op jit(solution)/shard_map/all_to_all | solution.py:336
  64.6 2.3 %collective-permute-start.1 = (bf16[54,16,128]{2,1,0:T(8,128)(2,1)S(1)}, bf16[54,16,128]{2,1,0:T(8,128)(2,1)}, u32[]{:S(2)}, u32[]{:S(2)}) collective-permute-start(bf16[54,16,128]{2,1,0:T(8,128)(2,1)S(1)} %slice.12.refs_0_), channel_id=1, source_target_pairs={{0,8},{1,9},{2,10},{3,11},{4,12},{5,13},{6,14},{7,15},{8,0},{9,1},... | collective-permute-start | bytes 663560 | tf_op jit(solution)/shard_map/ppermute | solution.py:306
  71.6 2.6 %collective-permute-done.1.refs_2_ = bf16[54,16,128]{2,1,0:T(8,128)(2,1)} collective-permute-done((bf16[54,16,128]{2,1,0:T(8,128)(2,1)S(1)}, bf16[54,16,128]{2,1,0:T(8,128)(2,1)}, u32[]{:S(2)}, u32[]{:S(2)}) %collective-permute-start.1) | collective-permute-done | bytes 221216 | tf_op jit(solution)/shard_map/ppermute | solution.py:306
  74.3 5.2 %collective-permute-start.26 = (bf16[128,896]{1,0:T(8,128)(2,1)S(1)}, bf16[128,896]{1,0:T(8,128)(2,1)S(1)}, u32[]{:S(2)}, u32[]{:S(2)}) collective-permute-start(bf16[128,896]{1,0:T(8,128)(2,1)S(1)} %get-tuple-element.53), channel_id=1, source_target_pairs={{0,16},{1,17},{2,18},{3,19},{4,20},{5,21},{6,22},{7,23},{8,24},{9,... | collective-permute-start | bytes 688136 | tf_op jit(solution)/shard_map/ppermute | solution.py:306
  80.0 2.5 %collective-permute-done.24.refs_6_ = bf16[128,896]{1,0:T(8,128)(2,1)S(1)} collective-permute-done((bf16[128,896]{1,0:T(8,128)(2,1)S(1)}, bf16[128,896]{1,0:T(8,128)(2,1)S(1)}, u32[]{:S(2)}, u32[]{:S(2)}) %collective-permute-start.24) | collective-permute-done | bytes 229408 | tf_op jit(solution)/shard_map/ppermute | solution.py:306
  82.5 13.1 %collective-permute-start.25 = (bf16[128,896]{1,0:T(8,128)(2,1)S(1)}, bf16[128,896]{1,0:T(8,128)(2,1)S(1)}, u32[]{:S(2)}, u32[]{:S(2)}) collective-permute-start(bf16[128,896]{1,0:T(8,128)(2,1)S(1)} %get-tuple-element.54), channel_id=1, source_target_pairs={{0,12},{1,13},{2,14},{3,15},{4,8},{5,9},{6,10},{7,11},{8,4},{9,5},... | collective-permute-start | bytes 688136 | tf_op jit(solution)/shard_map/ppermute | solution.py:306
  96.9 3.8 %collective-permute-done.26.refs_8_ = bf16[128,896]{1,0:T(8,128)(2,1)S(1)} collective-permute-done((bf16[128,896]{1,0:T(8,128)(2,1)S(1)}, bf16[128,896]{1,0:T(8,128)(2,1)S(1)}, u32[]{:S(2)}, u32[]{:S(2)}) %collective-permute-start.26) | collective-permute-done | bytes 229408 | tf_op jit(solution)/shard_map/ppermute | solution.py:306
  102.0 3.3 %collective-permute-done.25.refs_7_ = bf16[128,896]{1,0:T(8,128)(2,1)S(1)} collective-permute-done((bf16[128,896]{1,0:T(8,128)(2,1)S(1)}, bf16[128,896]{1,0:T(8,128)(2,1)S(1)}, u32[]{:S(2)}, u32[]{:S(2)}) %collective-permute-start.25) | collective-permute-done | bytes 229408 | tf_op jit(solution)/shard_map/ppermute | solution.py:306
  105.3 3.3 %collective-permute-done.4 = bf16[54,16,128]{2,1,0:T(8,128)(2,1)} collective-permute-done((bf16[54,16,128]{2,1,0:T(8,128)(2,1)}, bf16[54,16,128]{2,1,0:T(8,128)(2,1)}, u32[]{:S(2)}, u32[]{:S(2)}) %collective-permute-start.4) | collective-permute-done | bytes 221216 | tf_op jit(solution)/shard_map/ppermute | solution.py:306
  113.4 4.5 %collective-permute-done.27.refs_9_ = bf16[128,896]{1,0:T(8,128)(2,1)S(1)} collective-permute-done((bf16[128,896]{1,0:T(8,128)(2,1)}, bf16[128,896]{1,0:T(8,128)(2,1)S(1)}, u32[]{:S(2)}, u32[]{:S(2)}) %collective-permute-start.27) | collective-permute-done | bytes 229408 | tf_op jit(solution)/shard_map/ppermute | solution.py:306
  124.9 4.9 %lowrank.3 = (bf16[128,896]{1,0:T(8,128)(2,1)}, bf16[128,896]{1,0:T(8,128)(2,1)}, bf16[128,896]{1,0:T(8,128)(2,1)}, bf16[128,896]{1,0:T(8,128)(2,1)}) custom-call(s32[5]{0:T(128)} %stack.23.idx, bf16[8,128,256]{2,1,0:T(8,128)(2,1)} %copy-done, bf16[8,128,256]{2,1,0:T(8,128)(2,1)} %copy-done.2, bf16[8,128,256]{2,1,0:T(8,128)(2,1)} %copy-done.1, ...), custom_call_target="tpu_custom_call" | custom-call | tf_op jit(solution)/shard_map/lowrank/pallas_call | solution.py:380
  129.9 4.2 %collective-permute-start.34 = (bf16[128,896]{1,0:T(8,128)(2,1)}, bf16[128,896]{1,0:T(8,128)(2,1)S(1)}, u32[]{:S(2)}, u32[]{:S(2)}) collective-permute-start(bf16[128,896]{1,0:T(8,128)(2,1)} %get-tuple-element.35), channel_id=1, source_target_pairs={{0,20},{1,21},{2,22},{3,23},{4,16},{5,17},{6,18},{7,19},{8,28},{9,... | collective-permute-start | bytes 688136 | tf_op jit(solution)/shard_map/ppermute | solution.py:306
  135.3 4.8 %lowrank.2 = (bf16[128,896]{1,0:T(8,128)(2,1)}, bf16[128,896]{1,0:T(8,128)(2,1)}, bf16[128,896]{1,0:T(8,128)(2,1)}, bf16[128,896]{1,0:T(8,128)(2,1)}) custom-call(s32[5]{0:T(128)} %stack.23.idx, bf16[8,128,256]{2,1,0:T(8,128)(2,1)} %copy-done, bf16[8,128,256]{2,1,0:T(8,128)(2,1)} %copy-done.2, bf16[8,128,256]{2,1,0:T(8,128)(2,1)} %copy-done.1, ...), custom_call_target="tpu_custom_call" | custom-call | tf_op jit(solution)/shard_map/lowrank/pallas_call | solution.py:380
  141.7 3.6 %collective-permute-start.36 = (bf16[128,896]{1,0:T(8,128)(2,1)S(1)}, bf16[128,896]{1,0:T(8,128)(2,1)S(1)}, u32[]{:S(2)}, u32[]{:S(2)}) collective-permute-start(bf16[128,896]{1,0:T(8,128)(2,1)S(1)} %copy-done.39), channel_id=1, source_target_pairs={{0,28},{1,29},{2,30},{3,31},{4,24},{5,25},{6,26},{7,27},{8,20},{9,... | collective-permute-start | bytes 688136 | tf_op jit(solution)/shard_map/ppermute | solution.py:306
  145.5 9.8 %collective-permute-done.33.refs_7_ = bf16[128,896]{1,0:T(8,128)(2,1)S(1)} collective-permute-done((bf16[128,896]{1,0:T(8,128)(2,1)}, bf16[128,896]{1,0:T(8,128)(2,1)S(1)}, u32[]{:S(2)}, u32[]{:S(2)}) %collective-permute-start.33) | collective-permute-done | bytes 229408 | tf_op jit(solution)/shard_map/ppermute | solution.py:306
  155.4 5.4 %collective-permute-done.34.refs_8_ = bf16[128,896]{1,0:T(8,128)(2,1)S(1)} collective-permute-done((bf16[128,896]{1,0:T(8,128)(2,1)}, bf16[128,896]{1,0:T(8,128)(2,1)S(1)}, u32[]{:S(2)}, u32[]{:S(2)}) %collective-permute-start.34) | collective-permute-done | bytes 229408 | tf_op jit(solution)/shard_map/ppermute | solution.py:306
  161.3 5.8 %sparse_forward.1.refs_2_ = f32[2,128,3584]{2,1,0:T(8,128)} custom-call(s32[5]{0:T(128)} %stack.23.idx, s32[27]{0:T(128)} %gate_rows.3, s32[27]{0:T(128)} %get-tuple-element.61.gate_cols, s32[27]{0:T(128)} %up_rows.3, s32[27]{0:T(128)} %get-tuple-element.60.up_cols, bf16[128,4096]{1,0:T(8,128)(2,1)} %refs_0_.1, bf16[54,16,128]{2,1,0:T(8,128)(2,1)} %copy-done.13, ...), custom_call_target="tpu_custom_call" | custom-call | tf_op jit(solution)/shard_map/sparse_forward/pallas_call | solution.py:366
  167.2 3.2 %collective-permute-done.32.refs_6_ = bf16[128,896]{1,0:T(8,128)(2,1)S(1)} collective-permute-done((bf16[128,896]{1,0:T(8,128)(2,1)}, bf16[128,896]{1,0:T(8,128)(2,1)S(1)}, u32[]{:S(2)}, u32[]{:S(2)}) %collective-permute-start.32) | collective-permute-done | bytes 229408 | tf_op jit(solution)/shard_map/ppermute | solution.py:306
  171.1 6.7 %hidden_and_grads.1 = (bf16[128,3584]{1,0:T(8,128)(2,1)}, f32[4,27,16,128]{3,2,1,0:T(8,128)}, bf16[4,27,16,128]{3,2,1,0:T(8,128)(2,1)}, f32[2,27,16,128]{3,2,1,0...) custom-call(s32[5]{0:T(128)} %stack.23.idx, ...), custom_call_target="tpu_custom_call" | custom-call | tf_op jit(solution)/shard_map/hidden_and_grads/pallas_call | solution.py:396
  177.9 3.6 %collective-permute-start.41 = (bf16[2,27,16,128]{3,2,1,0:T(8,128)(2,1)}, bf16[2,27,16,128]{3,2,1,0:T(8,128)(2,1)S(1)}, u32[]{:S(2)}, u32[]{:S(2)}) collective-permute-start(bf16[2,27,16,128]{3,2,1,0:T(8,128)(2,1)} %get-tuple-element.46), channel_id=1, source_target_pairs={{0,8},{1,9},{2,10},{3,11},{4,12},{5,13},{6,14},{7,15},{8,0},{9,1},... | collective-permute-start | bytes 663560 | tf_op jit(solution)/shard_map/ppermute | solution.py:306
  185.4 5.9 %collective-permute-done.41 = bf16[2,27,16,128]{3,2,1,0:T(8,128)(2,1)S(1)} collective-permute-done((bf16[2,27,16,128]{3,2,1,0:T(8,128)(2,1)}, bf16[2,27,16,128]{3,2,1,0:T(8,128)(2,1)S(1)}, u32[]{:S(2)}, u32[]{:S(2)}) %collective-permute-start.41) | collective-permute-done | bytes 221216 | tf_op jit(solution)/shard_map/ppermute | solution.py:306
  191.2 9.1 %collective-permute-done.42 = bf16[2,27,16,128]{3,2,1,0:T(8,128)(2,1)S(1)} collective-permute-done((bf16[2,27,16,128]{3,2,1,0:T(8,128)(2,1)}, bf16[2,27,16,128]{3,2,1,0:T(8,128)(2,1)S(1)}, u32[]{:S(2)}, u32[]{:S(2)}) %collective-permute-start.42) | collective-permute-done | bytes 221216 | tf_op jit(solution)/shard_map/ppermute | solution.py:306
  205.7 3.9 %collective-permute-start.38 = (bf16[27,16,128]{2,1,0:T(8,128)(2,1)}, bf16[27,16,128]{2,1,0:T(8,128)(2,1)S(1)}, u32[]{:S(2)}, u32[]{:S(2)}) collective-permute-start(bf16[27,16,128]{2,1,0:T(8,128)(2,1)} %get-tuple-element.42), channel_id=1, source_target_pairs={{0,8},{1,9},{2,10},{3,11},{4,12},{5,13},{6,14},{7,15},{8,0},{9,1},... | collective-permute-start | bytes 331784 | tf_op jit(solution)/shard_map/ppermute | solution.py:306
  213.6 6.1 %collective-permute-done.39 = bf16[27,16,128]{2,1,0:T(8,128)(2,1)S(1)} collective-permute-done((bf16[27,16,128]{2,1,0:T(8,128)(2,1)}, bf16[27,16,128]{2,1,0:T(8,128)(2,1)S(1)}, u32[]{:S(2)}, u32[]{:S(2)}) %collective-permute-start.39) | collective-permute-done | bytes 110624 | tf_op jit(solution)/shard_map/ppermute | solution.py:306
  (165 shorter events, 50.7 us)
Async XLA Ops:
  0.7 20.1 %collective-permute-start.15 = (bf16[512,256]{1,0:T(8,128)(2,1)}, bf16[512,256]{1,0:T(8,128)(2,1)S(1)}, u32[]{:S(2)}, u32[]{:S(2)}) collective-permute-start(bf16[512,256]{1,0:T(8,128)(2,1)} %refs_6_.1), channel_id=1, source_target_pairs={{0,4},{1,5},{2,6},{3,7},{4,0},{5,1},{6,2},{7,3},{8,12},{9,13},{10,... | collective-permute-start | bytes 786440 | tf_op jit(solution)/shard_map/ppermute | solution.py:306
  3.7 17.0 %collective-permute-start.16 = (bf16[512,256]{1,0:T(8,128)(2,1)}, bf16[512,256]{1,0:T(8,128)(2,1)S(1)}, u32[]{:S(2)}, u32[]{:S(2)}) collective-permute-start(bf16[512,256]{1,0:T(8,128)(2,1)} %refs_7_.1), channel_id=1, source_target_pairs={{0,4},{1,5},{2,6},{3,7},{4,0},{5,1},{6,2},{7,3},{8,12},{9,13},{10,... | collective-permute-start | bytes 786440 | tf_op jit(solution)/shard_map/ppermute | solution.py:306
  9.1 10.5 %collective-permute-start.10 = (bf16[128,512]{1,0:T(8,128)(2,1)S(1)}, bf16[128,512]{1,0:T(8,128)(2,1)S(1)}, u32[]{:S(2)}, u32[]{:S(2)}) collective-permute-start(bf16[128,512]{1,0:T(8,128)(2,1)S(1)} %get-tuple-element.58), channel_id=1, source_target_pairs={{0,16},{1,17},{2,18},{3,19},{4,20},{5,21},{6,22},{7,23},{8,24},{9,... | collective-permute-start | bytes 393224 | tf_op jit(solution)/shard_map/ppermute | solution.py:306
  9.1 10.5 %collective-permute-start.9 = (bf16[128,512]{1,0:T(8,128)(2,1)S(1)}, bf16[128,512]{1,0:T(8,128)(2,1)S(1)}, u32[]{:S(2)}, u32[]{:S(2)}) collective-permute-start(bf16[128,512]{1,0:T(8,128)(2,1)S(1)} %get-tuple-element.59), channel_id=1, source_target_pairs={{0,8},{1,9},{2,10},{3,11},{4,12},{5,13},{6,14},{7,15},{8,0},{9,1},... | collective-permute-start | bytes 393224 | tf_op jit(solution)/shard_map/ppermute | solution.py:306
  26.0 13.2 %collective-permute-start.18 = (bf16[128,512]{1,0:T(8,128)(2,1)}, bf16[128,512]{1,0:T(8,128)(2,1)S(1)}, u32[]{:S(2)}, u32[]{:S(2)}) collective-permute-start(bf16[128,512]{1,0:T(8,128)(2,1)} %get-tuple-element.28), channel_id=1, source_target_pairs={{0,16},{1,17},{2,18},{3,19},{4,20},{5,21},{6,22},{7,23},{8,24},{9,... | collective-permute-start | bytes 393224 | tf_op jit(solution)/shard_map/ppermute | solution.py:306
  61.5 17.9 %collective-permute-start.21 = (bf16[8,128,256]{2,1,0:T(8,128)(2,1)S(1)}, bf16[8,128,256]{2,1,0:T(8,128)(2,1)S(1)}, u32[]{:S(2)}, u32[]{:S(2)}) collective-permute-start(bf16[8,128,256]{2,1,0:T(8,128)(2,1)S(1)} %all_to_all.5.refs_0_), channel_id=1, source_target_pairs={{0,2},{1,3},{2,0},{3,1},{4,6},{5,7},{6,4},{7,5},{8,10},{9,11},{10,... | collective-permute-start | bytes 1572872 | tf_op jit(solution)/shard_map/ppermute | solution.py:306
  68.0 11.5 %collective-permute-start.29 = (bf16[128,896]{1,0:T(8,128)(2,1)S(1)}, bf16[128,896]{1,0:T(8,128)(2,1)S(1)}, u32[]{:S(2)}, u32[]{:S(2)}) collective-permute-start(bf16[128,896]{1,0:T(8,128)(2,1)S(1)} %get-tuple-element.49), channel_id=1, source_target_pairs={{0,28},{1,29},{2,30},{3,31},{4,24},{5,25},{6,26},{7,27},{8,20},{9,... | collective-permute-start | bytes 688136 | tf_op jit(solution)/shard_map/ppermute | solution.py:306
  70.1 12.4 %collective-permute-start.24 = (bf16[128,896]{1,0:T(8,128)(2,1)S(1)}, bf16[128,896]{1,0:T(8,128)(2,1)S(1)}, u32[]{:S(2)}, u32[]{:S(2)}) collective-permute-start(bf16[128,896]{1,0:T(8,128)(2,1)S(1)} %get-tuple-element.50), channel_id=1, source_target_pairs={{0,8},{1,9},{2,10},{3,11},{4,12},{5,13},{6,14},{7,15},{8,0},{9,1},... | collective-permute-start | bytes 688136 | tf_op jit(solution)/shard_map/ppermute | solution.py:306
  70.1 25.5 %collective-permute-start.28 = (bf16[128,896]{1,0:T(8,128)(2,1)S(1)}, bf16[128,896]{1,0:T(8,128)(2,1)S(1)}, u32[]{:S(2)}, u32[]{:S(2)}) collective-permute-start(bf16[128,896]{1,0:T(8,128)(2,1)S(1)} %get-tuple-element.52), channel_id=1, source_target_pairs={{0,24},{1,25},{2,26},{3,27},{4,28},{5,29},{6,30},{7,31},{8,16},{9,... | collective-permute-start | bytes 688136 | tf_op jit(solution)/shard_map/ppermute | solution.py:306
  74.3 26.4 %collective-permute-start.26 = (bf16[128,896]{1,0:T(8,128)(2,1)S(1)}, bf16[128,896]{1,0:T(8,128)(2,1)S(1)}, u32[]{:S(2)}, u32[]{:S(2)}) collective-permute-start(bf16[128,896]{1,0:T(8,128)(2,1)S(1)} %get-tuple-element.53), channel_id=1, source_target_pairs={{0,16},{1,17},{2,18},{3,19},{4,20},{5,21},{6,22},{7,23},{8,24},{9,... | collective-permute-start | bytes 688136 | tf_op jit(solution)/shard_map/ppermute | solution.py:306
  79.5 44.4 %collective-permute-start.20 = (bf16[8,128,256]{2,1,0:T(8,128)(2,1)S(1)}, bf16[8,128,256]{2,1,0:T(8,128)(2,1)S(1)}, u32[]{:S(2)}, u32[]{:S(2)}) collective-permute-start(bf16[8,128,256]{2,1,0:T(8,128)(2,1)S(1)} %all_to_all.5.refs_0_), channel_id=1, source_target_pairs={{0,1},{1,0},{2,3},{3,2},{4,5},{5,4},{6,7},{7,6},{8,9},{9,8},{10,11... | collective-permute-start | bytes 1572872 | tf_op jit(solution)/shard_map/ppermute | solution.py:306
  79.5 44.5 %collective-permute-start.22 = (bf16[8,128,256]{2,1,0:T(8,128)(2,1)S(1)}, bf16[8,128,256]{2,1,0:T(8,128)(2,1)S(1)}, u32[]{:S(2)}, u32[]{:S(2)}) collective-permute-start(bf16[8,128,256]{2,1,0:T(8,128)(2,1)S(1)} %collective-permute-done.21.refs_2_), channel_id=1, source_target_pairs={{0,1},{1,0},{2,3},{3,2},{4,5},{5,4},{6,7},{7,6},{8,9},{9,8},{10,11... | collective-permute-start | bytes 1572872 | tf_op jit(solution)/shard_map/ppermute | solution.py:306
  82.5 22.8 %collective-permute-start.25 = (bf16[128,896]{1,0:T(8,128)(2,1)S(1)}, bf16[128,896]{1,0:T(8,128)(2,1)S(1)}, u32[]{:S(2)}, u32[]{:S(2)}) collective-permute-start(bf16[128,896]{1,0:T(8,128)(2,1)S(1)} %get-tuple-element.54), channel_id=1, source_target_pairs={{0,12},{1,13},{2,14},{3,15},{4,8},{5,9},{6,10},{7,11},{8,4},{9,5},... | collective-permute-start | bytes 688136 | tf_op jit(solution)/shard_map/ppermute | solution.py:306
  95.6 12.9 %collective-permute-start.4 = (bf16[54,16,128]{2,1,0:T(8,128)(2,1)}, bf16[54,16,128]{2,1,0:T(8,128)(2,1)}, u32[]{:S(2)}, u32[]{:S(2)}) collective-permute-start(bf16[54,16,128]{2,1,0:T(8,128)(2,1)} %collective-permute-done.3), channel_id=1, source_target_pairs={{8,0},{9,1},{10,2},{11,3},{12,4},{13,5},{14,6},{15,7},{16,24},{17,... | collective-permute-start | bytes 663560 | tf_op jit(solution)/shard_map/ppermute | solution.py:306
  105.3 12.6 %collective-permute-start.27 = (bf16[128,896]{1,0:T(8,128)(2,1)}, bf16[128,896]{1,0:T(8,128)(2,1)S(1)}, u32[]{:S(2)}, u32[]{:S(2)}) collective-permute-start(bf16[128,896]{1,0:T(8,128)(2,1)} %get-tuple-element.55), channel_id=1, source_target_pairs={{0,20},{1,21},{2,22},{3,23},{4,16},{5,17},{6,18},{7,19},{8,28},{9,... | collective-permute-start | bytes 688136 | tf_op jit(solution)/shard_map/ppermute | solution.py:306
  108.6 13.2 %collective-permute-start.23 = (bf16[128,896]{1,0:T(8,128)(2,1)}, bf16[128,896]{1,0:T(8,128)(2,1)S(1)}, u32[]{:S(2)}, u32[]{:S(2)}) collective-permute-start(bf16[128,896]{1,0:T(8,128)(2,1)} %get-tuple-element.56), channel_id=1, source_target_pairs={{0,4},{1,5},{2,6},{3,7},{4,0},{5,1},{6,2},{7,3},{8,12},{9,13},{10,... | collective-permute-start | bytes 688136 | tf_op jit(solution)/shard_map/ppermute | solution.py:306
  110.4 19.5 %collective-permute-start.7 = (bf16[54,16,128]{2,1,0:T(8,128)(2,1)}, bf16[54,16,128]{2,1,0:T(8,128)(2,1)}, u32[]{:S(2)}, u32[]{:S(2)}) collective-permute-start(bf16[54,16,128]{2,1,0:T(8,128)(2,1)} %collective-permute-done.6), channel_id=1, source_target_pairs={{8,0},{9,1},{10,2},{11,3},{12,4},{13,5},{14,6},{15,7},{16,24},{17,... | collective-permute-start | bytes 663560 | tf_op jit(solution)/shard_map/ppermute | solution.py:306
  117.9 17.1 %collective-permute-start = (bf16[54,16,128]{2,1,0:T(8,128)(2,1)}, bf16[54,16,128]{2,1,0:T(8,128)(2,1)}, u32[]{:S(2)}, u32[]{:S(2)}) collective-permute-start(bf16[54,16,128]{2,1,0:T(8,128)(2,1)} %copy-done.13), channel_id=1, source_target_pairs={{0,4},{1,5},{2,6},{3,7},{4,0},{5,1},{6,2},{7,3},{8,12},{9,13},{10,... | collective-permute-start | bytes 663560 | tf_op jit(solution)/shard_map/ppermute | solution.py:306
  121.8 18.4 %collective-permute-start.2 = (bf16[54,16,128]{2,1,0:T(8,128)(2,1)}, bf16[54,16,128]{2,1,0:T(8,128)(2,1)}, u32[]{:S(2)}, u32[]{:S(2)}) collective-permute-start(bf16[54,16,128]{2,1,0:T(8,128)(2,1)} %collective-permute-done.1.refs_2_), channel_id=1, source_target_pairs={{0,4},{1,5},{2,6},{3,7},{4,0},{5,1},{6,2},{7,3},{8,12},{9,13},{10,... | collective-permute-start | bytes 663560 | tf_op jit(solution)/shard_map/ppermute | solution.py:306
  123.9 17.8 %collective-permute-start.5 = (bf16[54,16,128]{2,1,0:T(8,128)(2,1)}, bf16[54,16,128]{2,1,0:T(8,128)(2,1)}, u32[]{:S(2)}, u32[]{:S(2)}) collective-permute-start(bf16[54,16,128]{2,1,0:T(8,128)(2,1)} %broadcast_select_fusion.9.refs_4_), channel_id=1, source_target_pairs={{0,4},{1,5},{2,6},{3,7},{4,0},{5,1},{6,2},{7,3},{8,12},{9,13},{10,... | collective-permute-start | bytes 663560 | tf_op jit(solution)/shard_map/ppermute | solution.py:306
  129.8 25.5 %collective-permute-start.33 = (bf16[128,896]{1,0:T(8,128)(2,1)}, bf16[128,896]{1,0:T(8,128)(2,1)S(1)}, u32[]{:S(2)}, u32[]{:S(2)}) collective-permute-start(bf16[128,896]{1,0:T(8,128)(2,1)} %get-tuple-element.34), channel_id=1, source_target_pairs={{0,16},{1,17},{2,18},{3,19},{4,20},{5,21},{6,22},{7,23},{8,24},{9,... | collective-permute-start | bytes 688136 | tf_op jit(solution)/shard_map/ppermute | solution.py:306
  129.9 30.8 %collective-permute-start.34 = (bf16[128,896]{1,0:T(8,128)(2,1)}, bf16[128,896]{1,0:T(8,128)(2,1)S(1)}, u32[]{:S(2)}, u32[]{:S(2)}) collective-permute-start(bf16[128,896]{1,0:T(8,128)(2,1)} %get-tuple-element.35), channel_id=1, source_target_pairs={{0,20},{1,21},{2,22},{3,23},{4,16},{5,17},{6,18},{7,19},{8,28},{9,... | collective-permute-start | bytes 688136 | tf_op jit(solution)/shard_map/ppermute | solution.py:306
  135.1 10.2 %collective-permute-start.8 = (bf16[54,16,128]{2,1,0:T(8,128)(2,1)S(1)}, bf16[54,16,128]{2,1,0:T(8,128)(2,1)S(1)}, u32[]{:S(2)}, u32[]{:S(2)}) collective-permute-start(bf16[54,16,128]{2,1,0:T(8,128)(2,1)S(1)} %broadcast_select_fusion.8.refs_6_), channel_id=1, source_target_pairs={{0,4},{1,5},{2,6},{3,7},{4,0},{5,1},{6,2},{7,3},{8,12},{9,13},{10,... | collective-permute-start | bytes 663560 | tf_op jit(solution)/shard_map/ppermute | solution.py:306
  140.2 27.0 %collective-permute-start.35 = (bf16[128,896]{1,0:T(8,128)(2,1)S(1)}, bf16[128,896]{1,0:T(8,128)(2,1)S(1)}, u32[]{:S(2)}, u32[]{:S(2)}) collective-permute-start(bf16[128,896]{1,0:T(8,128)(2,1)S(1)} %copy-done.40), channel_id=1, source_target_pairs={{0,24},{1,25},{2,26},{3,27},{4,28},{5,29},{6,30},{7,31},{8,16},{9,... | collective-permute-start | bytes 688136 | tf_op jit(solution)/shard_map/ppermute | solution.py:306
  141.7 25.4 %collective-permute-start.36 = (bf16[128,896]{1,0:T(8,128)(2,1)S(1)}, bf16[128,896]{1,0:T(8,128)(2,1)S(1)}, u32[]{:S(2)}, u32[]{:S(2)}) collective-permute-start(bf16[128,896]{1,0:T(8,128)(2,1)S(1)} %copy-done.39), channel_id=1, source_target_pairs={{0,28},{1,29},{2,30},{3,31},{4,24},{5,25},{6,26},{7,27},{8,20},{9,... | collective-permute-start | bytes 688136 | tf_op jit(solution)/shard_map/ppermute | solution.py:306
  145.3 21.9 %collective-permute-start.30 = (bf16[128,896]{1,0:T(8,128)(2,1)}, bf16[128,896]{1,0:T(8,128)(2,1)S(1)}, u32[]{:S(2)}, u32[]{:S(2)}) collective-permute-start(bf16[128,896]{1,0:T(8,128)(2,1)} %get-tuple-element.31), channel_id=1, source_target_pairs={{0,4},{1,5},{2,6},{3,7},{4,0},{5,1},{6,2},{7,3},{8,12},{9,13},{10,... | collective-permute-start | bytes 688136 | tf_op jit(solution)/shard_map/ppermute | solution.py:306
  155.4 11.8 %collective-permute-start.31 = (bf16[128,896]{1,0:T(8,128)(2,1)}, bf16[128,896]{1,0:T(8,128)(2,1)S(1)}, u32[]{:S(2)}, u32[]{:S(2)}) collective-permute-start(bf16[128,896]{1,0:T(8,128)(2,1)} %get-tuple-element.32), channel_id=1, source_target_pairs={{0,8},{1,9},{2,10},{3,11},{4,12},{5,13},{6,14},{7,15},{8,0},{9,1},... | collective-permute-start | bytes 688136 | tf_op jit(solution)/shard_map/ppermute | solution.py:306
  177.9 13.3 %collective-permute-start.41 = (bf16[2,27,16,128]{3,2,1,0:T(8,128)(2,1)}, bf16[2,27,16,128]{3,2,1,0:T(8,128)(2,1)S(1)}, u32[]{:S(2)}, u32[]{:S(2)}) collective-permute-start(bf16[2,27,16,128]{3,2,1,0:T(8,128)(2,1)} %get-tuple-element.46), channel_id=1, source_target_pairs={{0,8},{1,9},{2,10},{3,11},{4,12},{5,13},{6,14},{7,15},{8,0},{9,1},... | collective-permute-start | bytes 663560 | tf_op jit(solution)/shard_map/ppermute | solution.py:306
  181.5 18.9 %collective-permute-start.42 = (bf16[2,27,16,128]{3,2,1,0:T(8,128)(2,1)}, bf16[2,27,16,128]{3,2,1,0:T(8,128)(2,1)S(1)}, u32[]{:S(2)}, u32[]{:S(2)}) collective-permute-start(bf16[2,27,16,128]{3,2,1,0:T(8,128)(2,1)} %get-tuple-element.47), channel_id=1, source_target_pairs={{0,16},{1,17},{2,18},{3,19},{4,20},{5,21},{6,22},{7,23},{8,24},{9,... | collective-permute-start | bytes 663560 | tf_op jit(solution)/shard_map/ppermute | solution.py:306
  182.4 17.9 %collective-permute-start.43 = (bf16[2,27,16,128]{3,2,1,0:T(8,128)(2,1)}, bf16[2,27,16,128]{3,2,1,0:T(8,128)(2,1)S(1)}, u32[]{:S(2)}, u32[]{:S(2)}) collective-permute-start(bf16[2,27,16,128]{3,2,1,0:T(8,128)(2,1)} %get-tuple-element.48), channel_id=1, source_target_pairs={{0,24},{1,25},{2,26},{3,27},{4,28},{5,29},{6,30},{7,31},{8,16},{9,... | collective-permute-start | bytes 663560 | tf_op jit(solution)/shard_map/ppermute | solution.py:306
  183.9 19.0 %collective-permute-start.37 = (bf16[4,27,16,128]{3,2,1,0:T(8,128)(2,1)}, bf16[4,27,16,128]{3,2,1,0:T(8,128)(2,1)S(1)}, u32[]{:S(2)}, u32[]{:S(2)}) collective-permute-start(bf16[4,27,16,128]{3,2,1,0:T(8,128)(2,1)} %get-tuple-element.40), channel_id=1, source_target_pairs={{0,4},{1,5},{2,6},{3,7},{4,0},{5,1},{6,2},{7,3},{8,12},{9,13},{10,... | collective-permute-start | bytes 1327112 | tf_op jit(solution)/shard_map/ppermute | solution.py:306
  201.5 10.6 %collective-permute-start.44 = (bf16[27,16,128]{2,1,0:T(8,128)(2,1)S(1)}, bf16[27,16,128]{2,1,0:T(8,128)(2,1)S(1)}, u32[]{:S(2)}, u32[]{:S(2)}) collective-permute-start(bf16[27,16,128]{2,1,0:T(8,128)(2,1)S(1)} %fusion), channel_id=1, source_target_pairs={{0,4},{1,5},{2,6},{3,7},{4,0},{5,1},{6,2},{7,3},{8,12},{9,13},{10,... | collective-permute-start | bytes 331784 | tf_op jit(solution)/shard_map/ppermute | solution.py:306
  (54 other events, 831.9 us)

commit v3 on v2

--- a/solution.py
+++ b/solution.py
@@ -99,6 +99,10 @@
 AXES = ("z", "x", "y", "c")
 
 
+def grant(mib):
+    return pltpu.CompilerParams(vmem_limit_bytes=mib << 20)
+
+
 def at(start, size):
     return pl.ds(pl.multiple_of(start, BLK), size)
 
@@ -111,24 +115,20 @@
 
 
 def partial_kernel(nz, idx, tokens, *refs):
-    mine, other = refs[: nz - 1], refs[nz - 1 : 2 * nz - 2]
-    left_g, left_u, recv_g, recv_u = refs[2 * nz - 2 : 2 * nz + 2]
-    own_out, outs = refs[2 * nz + 2], refs[2 * nz + 3 : 3 * nz + 2]
-    left, toks, sems = refs[3 * nz + 2 :]
-    z, x, c = idx[0], idx[1], idx[2]
+    n = nz - 1
+    quarters, (left_g, left_u, recv_g, recv_u) = refs[: 4 * n], refs[4 * n : 4 * nz]
+    own_out, outs = refs[4 * nz], refs[4 * nz + 1 : 5 * nz]
+    left, toks = refs[5 * nz :]
+    z, x, c, y = idx[0], idx[1], idx[2], idx[5]
     depth, width = left_g.shape
-    pairs = [
-        (left_g, left.at[x, :, pl.ds(0, width)]),
-        (left_u, left.at[x, :, pl.ds(width, width)]),
-        (recv_g, left.at[1 - x, :, pl.ds(0, width)]),
-        (recv_u, left.at[1 - x, :, pl.ds(width, width)]),
-        (tokens.at[:, at(z * 2 * depth, 2 * depth)], toks.at[0]),
-    ]
-    for j in range(1, nz):
-        pairs.append((mine[j - 1], toks.at[j, :, at(c * depth, depth)]))
-        pairs.append((other[j - 1], toks.at[j, :, at((1 - c) * depth, depth)]))
-    for copy in run_copies(pairs, sems):
-        copy.wait()
+    left[x, :, :width], left[x, :, width:] = left_g[...], left_u[...]
+    left[1 - x, :, :width], left[1 - x, :, width:] = recv_g[...], recv_u[...]
+    toks[0] = tokens[:, at(z * 2 * depth, 2 * depth)]
+    quarter = depth // 2
+    for i, (dc, dy) in enumerate(((0, 0), (0, 1), (1, 0), (1, 1))):
+        start = (c ^ dc) * depth + (y ^ dy) * quarter
+        for j in range(1, nz):
+            toks[j, :, at(start, quarter)] = quarters[i * n + j - 1][...]
     weights = left[...].reshape(2 * depth, 2 * width)
     rows = toks.shape[1]
     total = jnp.dot(
@@ -149,24 +149,47 @@
         out[k] = total[:, k % 2 * width : (k % 2 + 1) * width].astype(BF16)
 
 
+def load_ranks(nf, slots, idx, ranks, rank):
+    f, t = idx[3], idx[4]
+    depth = rank.shape[2] // nf
+    parts = ranks[0].shape[2] // depth
+    for s, source in enumerate(ranks):
+        for h in range(parts):
+            lanes = at((f ^ ((t ^ s) * parts + h)) * depth, depth)
+            for i, m in enumerate(slots):
+                rank[i, :, lanes] = source[f ^ m, :, h * depth : (h + 1) * depth]
+
+
+def product(rank, rights):
+    count, rows, _ = rank.shape
+    weights = jnp.concatenate([right[...] for right in rights], axis=0)
+    lhs = rank[:, :, : weights.shape[0]].reshape(count * rows, weights.shape[0])
+    return jnp.dot(lhs, weights, preferred_element_type=F32)
+
+
 def lowrank_kernel(nf, nt, slots, idx, *refs):
     ranks, rights = refs[:nt], refs[nt : nt + nf]
-    outs = refs[nt + nf : nt + nf + len(slots)]
-    rank, weight, sems = refs[nt + nf + len(slots) :]
-    f, t = idx[3], idx[4]
-    slice_width = ranks[0].shape[2]
-    pairs = [(rights[k], weight.at[f ^ k]) for k in range(nf)]
-    for s in range(nt):
-        lanes = at((t ^ s) * slice_width, slice_width)
-        pairs += [(ranks[s].at[f ^ m], rank.at[i, :, lanes]) for i, m in enumerate(slots)]
-    for copy in run_copies(pairs, sems):
-        copy.wait()
-    count, rows, depth = rank.shape
-    cols = weight.shape[2]
-    weights = weight[...].reshape(depth, cols)
-    total = jnp.dot(rank[...].reshape(count * rows, depth), weights, preferred_element_type=F32)
-    for i in range(count):
+    outs, rank = refs[nt + nf : nt + nf + len(slots)], refs[-1]
+    load_ranks(nf, slots, idx, ranks, rank)
+    total = product(rank, rights)
+    rows = rank.shape[1]
+    for i in range(len(slots)):
         outs[i][...] = total[i * rows : (i + 1) * rows].astype(BF16)
+
+
+def lowrank_first_kernel(nf, nt, slots, idx, *refs):
+    ranks, rights = refs[:nt], refs[nt : nt + nf - 1]
+    total, columns, rank = refs[nt + nf - 1 :]
+    load_ranks(nf, slots, idx, ranks, rank)
+    total[...] = product(rank, rights)
+    columns[...] = rank[:, :, -columns.shape[1] :].reshape(columns.shape)
+
+
+def lowrank_last_kernel(total, columns, right, *outs):
+    rows = outs[0].shape[0]
+    value = total[...] + jnp.dot(columns[...], right[...], preferred_element_type=F32)
+    for i, out in enumerate(outs):
+        out[...] = value[i * rows : (i + 1) * rows].astype(BF16)
 
 
 def sparse_kernel(nf, idx, gate_rows, gate_cols, up_rows, up_cols, tokens, *refs):
@@ -192,81 +215,69 @@
         lax.fori_loop(0, count, step, 0, unroll=True)
 
 
-def final_kernel(nf, idx, gate_rows, gate_cols, up_rows, up_cols, *refs):
+def support_grads(nf, tokens, dpre, rows, cols, k):
+    source = tokens[:, at(rows[k] * BLK, BLK)]
+    picked = dpre[:, at(cols[k] * BLK, BLK)]
+    value = lax.dot_general(source, picked, (((0,), (0,)), ((), ())), preferred_element_type=F32)
+    return value.reshape(nf // 2, 2, BLK // nf, BLK)
+
+
+def final_kernel(nf, idx, up_rows, up_cols, tokens, grad, sparse, *refs):
     nz = nf // 2
-    tokens_in, grad_in, sparse_in = refs[:3]
-    pieces = refs[3 : nf + 3]
-    hidden_out, gate_keep_out, gate_send_out, up_keep_out = refs[nf + 3 : nf + 7]
-    up_send_outs = refs[nf + 7 : nf + 6 + nz]
-    tokens, grad, sparse, pre, dpre, hidden = refs[nf + 6 + nz : nf + 12 + nz]
-    gate_keep, gate_send, up_keep, up_send, sems, out_sems = refs[nf + 12 + nz :]
-    z, x, f = idx[0], idx[1], idx[3]
-    width = pre.shape[3]
-    pairs = [(pieces[k], pre.at[(f ^ k) % 2, (f ^ k) // 2]) for k in range(nf)]
+    pieces = refs[:nf]
+    hidden, dpre_gate, up_keep = refs[nf : nf + 3]
+    up_sends = refs[nf + 3 : nf + 2 + nz]
+    dpre_up, keep, send = refs[nf + 2 + nz :]
+    z, x = idx[0], idx[1]
+    rows, width = pieces[0].shape
+    tall = rows // 2
     for j in range(nz):
-        here = pl.ds(j * width, width)
-        pairs.append((sparse_in.at[:, :, here], sparse.at[:, :, here]))
-        pairs.append((grad_in.at[:, here], grad.at[:, here]))
-    pairs.append((tokens_in, tokens))
-    copies = run_copies(pairs, sems)
-    for copy in copies[:nf]:
-        copy.wait()
-    sent = []
-
-    def send(source, target):
-        copy = pltpu.make_async_copy(source, target, out_sems.at[len(sent)])
-        copy.start()
-        sent.append(copy)
-
-    for j in range(nz):
-        here = pl.ds(j * width, width)
-        copies[nf + 2 * j].wait()
-        copies[nf + 2 * j + 1].wait()
-        gate = pre[0, j].astype(F32) + sparse[0, :, here]
-        up = pre[1, j].astype(F32) + sparse[1, :, here]
-        sigma = jax.nn.sigmoid(gate)
-        silu = gate * sigma
-        upstream = grad[:, here].astype(F32)
-        dpre[0, :, here] = (upstream * up * sigma * (1.0 + gate * (1.0 - sigma))).astype(BF16)
-        dpre[1, :, here] = (upstream * silu).astype(BF16)
-        hidden[:, here] = (silu * up).astype(BF16)
-        send(hidden.at[:, here], hidden_out.at[:, here])
-    copies[-1].wait()
-    count = gate_rows.shape[0]
-
-    def partial(p, rows, cols, k):
-        source = tokens[:, at(rows[k] * BLK, BLK)]
-        picked = dpre[p, :, at(cols[k] * BLK, BLK)]
-        value = lax.dot_general(
-            source, picked, (((0,), (0,)), ((), ())), preferred_element_type=F32
-        )
-        return value.reshape(nz, 2, BLK // nf, BLK)
-
-    def up_step(k, carry):
-        value = partial(1, up_rows, up_cols, k)
+        mine, other = pieces[2 * j], pieces[2 * j + 1]
+
+        def chunk(i, carry, j=j, mine=mine, other=other):
+            down = pl.ds(pl.multiple_of(i % 2 * tall, tall), tall)
+            local = at(i // 2 * BLK, BLK)
+            here = at((z ^ j) * width + i // 2 * BLK, BLK)
+            a, b = mine[down, local].astype(F32), other[down, local].astype(F32)
+            gate = jnp.where(x == 0, a, b) + sparse[0, down, here]
+            up = jnp.where(x == 0, b, a) + sparse[1, down, here]
+            sigma = jax.nn.sigmoid(gate)
+            silu = gate * sigma
+            upstream = grad[down, here].astype(F32)
+            slope = upstream * up * sigma * (1.0 + gate * (1.0 - sigma))
+            dpre_gate[down, here] = slope.astype(BF16)
+            dpre_up[down, here] = (upstream * silu).astype(BF16)
+            hidden[down, here] = (silu * up).astype(BF16)
+            return carry
+
+        lax.fori_loop(0, 2 * width // BLK, chunk, 0, unroll=True)
+
+    def step(k, carry):
+        value = support_grads(nf, tokens, dpre_up, up_rows, up_cols, k)
         for j in range(nz):
-            up_keep[z ^ j, :, k] = value[j]
-            up_send[z ^ j, :, k] = value[j].astype(BF16)
+            keep[z ^ j, :, k] = value[j]
+            send[z ^ j, :, k] = value[j].astype(BF16)
         return carry
 
-    def gate_step(k, carry):
-        value = partial(0, gate_rows, gate_cols, k)
+    lax.fori_loop(0, up_rows.shape[0], step, 0, unroll=True)
+    up_keep[...] = keep[0]
+    for j in range(1, nz):
+        up_sends[j - 1][...] = send[j]
+
+
+def gate_grads_kernel(nf, idx, rows, cols, tokens, dpre, keep_out, send_out):
+    z, x = idx[0], idx[1]
+
+    def step(k, carry):
+        value = support_grads(nf, tokens, dpre, rows, cols, k)
         keep = jnp.where(x == 0, value[:, 0], value[:, 1])
         other = jnp.where(x == 0, value[:, 1], value[:, 0]).astype(BF16)
-        for j in range(nz):
-            gate_keep[z ^ j, k] = keep[j]
-            gate_send[z ^ j, k] = other[j]
+        for j in range(nf // 2):
+            keep_out[z ^ j, k] = keep[j]
+            send_out[z ^ j, k] = other[j]
         return carry
 
-    lax.fori_loop(0, count, up_step, 0, unroll=True)
-    for j in range(1, nz):
-        send(up_send.at[j], up_send_outs[j - 1])
-    send(up_keep.at[0], up_keep_out)
-    lax.fori_loop(0, count, gate_step, 0, unroll=True)
-    send(gate_send, gate_send_out)
-    send(gate_keep, gate_keep_out)
-    for copy in sent:
-        copy.wait()
+    lax.fori_loop(0, rows.shape[0], step, 0, unroll=True)
 
 
 def gate_add_kernel(keep, got, own, *sends):
@@ -298,33 +309,39 @@
     count = gate_values.shape[0]
     share = BLK // nf
     z, x, c = lax.axis_index("z"), lax.axis_index("x"), lax.axis_index("c")
-    f, t = 2 * z + x, 2 * lax.axis_index("y") + c
-    idx = jnp.stack([z, x, c, f, t]).astype(jnp.int32)
+    y = lax.axis_index("y")
+    f, t = 2 * z + x, 2 * y + c
+    idx = jnp.stack([z, x, c, f, t, y]).astype(jnp.int32)
 
     def move(value, df=0, dt=0, only=range(nf)):
         pairs = [(i, i ^ (df * nt + dt)) for i in range(nf * nt) if i // (2 * nt) in only]
         return lax.ppermute(value, AXES, pairs)
 
-    halves = [
-        lax.dynamic_slice(tokens, (0, (z ^ j) * 2 * depth + c * depth), (rows, depth))
+    quarter = depth // 2
+    fetched = [
+        lax.dynamic_slice(
+            tokens, (0, (z ^ j) * 2 * depth + c * depth + y * quarter), (rows, quarter)
+        )
         for j in range(1, nz)
     ]
-    mine = [move(h, df=2 * j) for j, h in enumerate(halves, 1)]
+    fetched = [move(part, df=2 * j) for j, part in enumerate(fetched, 1)]
     recv_g, recv_u = move(gate_left, df=1), move(up_left, df=1)
-    other = [move(h, dt=1) for h in mine]
+    across_y = [move(part, dt=2) for part in fetched]
+    half = [*fetched, *across_y]
+    half += [move(part, dt=1) for part in half]
     sums = pl.pallas_call(
         functools.partial(partial_kernel, nz),
         out_shape=[jax.ShapeDtypeStruct((rows, 2 * slice_width), F32)]
         + [jax.ShapeDtypeStruct((rows, 2 * slice_width), BF16)] * (nz - 1),
-        in_specs=[SMEM] + [ANY] * (2 * nz + 3),
+        in_specs=[SMEM] + [VMEM] * (4 * nz + 1),
         out_specs=[VMEM] * nz,
         scratch_shapes=[
             pltpu.VMEM((2, depth, 2 * slice_width), BF16),
             pltpu.VMEM((nz, rows, 2 * depth), BF16),
-            pltpu.SemaphoreType.DMA((2 * nz + 3,)),
         ],
         name="rank_partial",
-    )(idx, tokens, *mine, *other, gate_left, up_left, recv_g, recv_u)
+            compiler_params=grant(10),
+    )(idx, tokens, *half, gate_left, up_left, recv_g, recv_u)
     got = [move(sums[j], df=2 * j) for j in range(1, nz)]
     for_f = pl.pallas_call(
         rank_round_kernel,
@@ -332,20 +349,23 @@
         in_specs=[VMEM] * nz,
         out_specs=VMEM,
         name="rank_round",
+        compiler_params=grant(4),
     )(sums[0], *got)
     stack = lax.all_to_all(for_f, ("z", "x"), 0, 0, tiled=True)
     ranks = [stack, move(stack, dt=1), move(stack, dt=2)]
     ranks.append(move(ranks[2], dt=1))
 
     rights = []
+    later_gate, later_up, _ = lax.optimization_barrier((gate_right, up_right, fetched[0]))
     for k in range(nf):
+        gate_k, up_k = (gate_right, up_right) if k in (4, 5) else (later_gate, later_up)
         start = (0, (z ^ (k // 2)) * cols)
         size = (gate_right.shape[0], cols)
         rights.append(
             jnp.where(
                 (x ^ (k % 2)) == 0,
-                lax.dynamic_slice(gate_right, start, size),
-                lax.dynamic_slice(up_right, start, size),
+                lax.dynamic_slice(gate_k, start, size),
+                lax.dynamic_slice(up_k, start, size),
             )
         )
     rights = [rights[0]] + [move(rights[k], df=k) for k in range(1, nf)]
@@ -373,54 +393,76 @@
             pltpu.SemaphoreType.DMA((nf,)),
         ],
         name="sparse_forward",
+        compiler_params=grant(14),
     )(*index, tokens, *values)
 
-    pieces = [None] * nf
-    for slots in (range(nf // 2, nf), range(nf // 2)):
-        lowrank = pl.pallas_call(
-            functools.partial(lowrank_kernel, nf, nt, slots),
-            out_shape=[jax.ShapeDtypeStruct((rows, cols), BF16)] * len(slots),
-            in_specs=[SMEM] + [ANY] * (nt + nf),
-            out_specs=[VMEM] * len(slots),
-            scratch_shapes=[
-                pltpu.VMEM((len(slots), rows, nt * slice_width), BF16),
-                pltpu.VMEM((nf, gate_right.shape[0], cols), BF16),
-                pltpu.SemaphoreType.DMA((nt * len(slots) + nf,)),
-            ],
-            name="lowrank",
-        )(idx, *ranks, *rights)
-        for k, product in zip(slots, lowrank):
-            pieces[k] = move(product, df=k) if k else product
+    depth_k, far, near_slots = gate_right.shape[0], range(nf // 2, nf), range(nf // 2)
+    scratch = [pltpu.VMEM((nf // 2, rows, nt * slice_width), BF16)]
+    blocks = [jax.ShapeDtypeStruct((rows, cols), BF16)] * (nf // 2)
+    first, columns = pl.pallas_call(
+        functools.partial(lowrank_first_kernel, nf, nt, far),
+        out_shape=[
+            jax.ShapeDtypeStruct((nf // 2 * rows, cols), F32),
+            jax.ShapeDtypeStruct((nf // 2 * rows, depth_k), BF16),
+        ],
+        in_specs=[SMEM] + [VMEM] * (nt + nf - 1),
+        out_specs=[VMEM] * 2,
+        scratch_shapes=scratch,
+        name="lowrank_first",
+        compiler_params=grant(14),
+    )(idx, *ranks, *rights[:-1])
+    far_products = pl.pallas_call(
+        lowrank_last_kernel,
+        out_shape=blocks,
+        in_specs=[VMEM] * 3,
+        out_specs=[VMEM] * (nf // 2),
+        name="lowrank_last",
+            compiler_params=grant(10),
+    )(first, columns, rights[-1])
+    near_products = pl.pallas_call(
+        functools.partial(lowrank_kernel, nf, nt, near_slots),
+        out_shape=blocks,
+        in_specs=[SMEM] + [VMEM] * (nt + nf),
+        out_specs=[VMEM] * (nf // 2),
+        scratch_shapes=scratch,
+        name="lowrank_near",
+            compiler_params=grant(14),
+    )(idx, *ranks, *rights)
+    pieces = [near_products[0]]
+    pieces += [move(near_products[k], df=k) for k in near_slots[1:]]
+    pieces += [move(far_products[k - far[0]], df=k) for k in far]
 
     support = (count, share, BLK)
     outs = pl.pallas_call(
         functools.partial(final_kernel, nf),
         out_shape=[
             jax.ShapeDtypeStruct((rows, width), BF16),
-            jax.ShapeDtypeStruct((nz,) + support, F32),
-            jax.ShapeDtypeStruct((nz,) + support, BF16),
+            jax.ShapeDtypeStruct((rows, width), BF16),
             jax.ShapeDtypeStruct((2,) + support, F32),
         ]
         + [jax.ShapeDtypeStruct((2,) + support, BF16)] * (nz - 1),
-        in_specs=[SMEM] * 5 + [ANY] * (nf + 3),
-        out_specs=[ANY] * (nz + 3),
+        in_specs=[SMEM] * 3 + [VMEM] * (nf + 3),
+        out_specs=[VMEM] * (nz + 2),
         scratch_shapes=[
-            pltpu.VMEM(tokens.shape, BF16),
             pltpu.VMEM((rows, width), BF16),
-            pltpu.VMEM((2, rows, width), F32),
-            pltpu.VMEM((2, nz, rows, cols), BF16),
-            pltpu.VMEM((2, rows, width), BF16),
-            pltpu.VMEM((rows, width), BF16),
-            pltpu.VMEM((nz,) + support, F32),
-            pltpu.VMEM((nz,) + support, BF16),
             pltpu.VMEM((nz, 2) + support, F32),
             pltpu.VMEM((nz, 2) + support, BF16),
-            pltpu.SemaphoreType.DMA((nf + 2 * nz + 1,)),
-            pltpu.SemaphoreType.DMA((2 * nz + 2,)),
         ],
-        name="hidden_and_grads",
-    )(*index, tokens, grad_hidden, sparse, *pieces)
-    hidden, gate_keep, gate_send, up_keep, *up_sends = outs
+        name="hidden_and_up_grads",
+            compiler_params=grant(24),
+    )(idx, up_rows, up_cols - base, tokens, grad_hidden, sparse, *pieces)
+    hidden, dpre_gate, up_keep, *up_sends = outs
+    gate_keep, gate_send = pl.pallas_call(
+        functools.partial(gate_grads_kernel, nf),
+        out_shape=[
+            jax.ShapeDtypeStruct((nz,) + support, F32),
+            jax.ShapeDtypeStruct((nz,) + support, BF16),
+        ],
+        in_specs=[SMEM] * 3 + [VMEM] * 2,
+        out_specs=[VMEM] * 2,
+        name="gate_grads",
+        compiler_params=grant(10),
+    )(idx, gate_rows, gate_cols - base, tokens, dpre_gate)
 
     up_sum = up_keep
     for j in range(1, nz):
@@ -433,6 +475,7 @@
         in_specs=[VMEM] * 2,
         out_specs=[VMEM] * nz,
         name="gate_add",
+        compiler_params=grant(6),
     )(gate_keep, gate_got)
     for j in range(1, nz):
         gate_total = gate_total + move(gate_sums[j - 1], df=2 * j).astype(F32)

time: 222 us -> 204 us (0.919)
  waiting for transfers between devices: 81 us -> 62.4 us
  local copies, waits for them, and re-layouts: 7.65 us -> 22.5 us
  Pallas kernels: 29.9 us -> 15.8 us
    ppermute x45 -> x51, waiting for transfers between devices: 81 us -> 62.4 us  [move(): return lax.ppermute(value, AXES, pairs)]
    unnamed x87 -> x85, local copies, waits for them, and re-layouts: 5.85 us -> 21.4 us
    pallas_call x1, Pallas kernels: 6.72 us -> 3.39 us  [exchange_device(): pl.pallas_call(functools.partial(final_kernel, nf), out_shape=[jax.ShapeD...]
    select_n x1 -> x2, other arithmetic: 1.16 us -> 4.38 us  [exchange_device(): jnp.where(x ^ k % 2 == 0, lax.dynamic_slice(gate_k, start, size), lax.dyn...]
    pallas_call x1, Pallas kernels: 5.79 us -> 2.74 us  [exchange_device(): pl.pallas_call(functools.partial(sparse_kernel, nf), out_shape=jax.ShapeD...]
    pallas_call x1, Pallas kernels: 3.69 us -> 1.43 us  [exchange_device(): pl.pallas_call(functools.partial(partial_kernel, nz), out_shape=[jax.Shap...]
    pallas_call x2 -> x4, Pallas kernels: 9.66 us -> 8.02 us  [the longest x1 3.27 us: exchange_device(): pl.pallas_call(functools.partial(lowrank_kernel, nf, nt, near_slots), out...]
    ppermute x45 -> x51, starting transfers between devices: 75.6 us -> 76.7 us  [move(): return lax.ppermute(value, AXES, pairs)]
  transfers between devices with their start and end apart: 45 -> 51, of which waited for: 20 -> 19; matrix products, arithmetic and copies ran while one was open for 4% -> 3% of each run, Pallas kernels for 8% -> 5%
where the time goes in v3:
time: 204 us; the launch traced here: 203 us
  starting transfers between devices  76.7 us (38%)
  waiting for transfers between devices  62.4 us (31%)
  local copies, waits for them, and re-layouts  22.5 us (11%)
  blocking collectives  18.6 us (9%)
  Pallas kernels  15.8 us (8%)
  other arithmetic  5.67 us (3%)
    ppermute x51, starting transfers between devices, move(): return lax.ppermute(value, AXES, pairs)  76.7 us
    ppermute x51, waiting for transfers between devices, move(): return lax.ppermute(value, AXES, pairs)  62.4 us
    unnamed x85, local copies, waits for them, and re-layouts  21.4 us
    all_to_all x1, blocking collectives, exchange_device(): stack = lax.all_to_all(for_f, ('z', 'x'), 0, 0, tiled=True)  18.6 us
    select_n x2, other arithmetic, exchange_device(): jnp.where(x ^ k % 2 == 0, lax.dynamic_slice(gate_k, start, size), lax.dyn...  4.38 us
  transfers between devices with their start and end apart: 51, of which 19 were waited for; matrix products, arithmetic and copies ran while one was open for 3% of the time, Pallas kernels for 5%

profile of v3, /device:TPU:0, one launch (start us, length us, event | category | flops | bytes accessed | tf_op | source)
XLA Modules:
  0.0 202.8 jit_solution(3574099698561778621)
XLA Ops:
  1.7 3.1 %collective-permute-start.9 = (bf16[128,256]{1,0:T(8,128)(2,1)S(1)}, bf16[128,256]{1,0:T(8,128)(2,1)S(1)}, u32[]{:S(2)}, u32[]{:S(2)}) collective-permute-start(bf16[128,256]{1,0:T(8,128)(2,1)S(1)} %get-tuple-element.69), channel_id=1, source_target_pairs={{0,8},{1,9},{2,10},{3,11},{4,12},{5,13},{6,14},{7,15},{8,0},{9,1},... | collective-permute-start | bytes 196616 | tf_op jit(solution)/shard_map/ppermute | solution.py:318
  4.8 2.6 %collective-permute-start.10 = (bf16[128,256]{1,0:T(8,128)(2,1)S(1)}, bf16[128,256]{1,0:T(8,128)(2,1)S(1)}, u32[]{:S(2)}, u32[]{:S(2)}) collective-permute-start(bf16[128,256]{1,0:T(8,128)(2,1)S(1)} %get-tuple-element.68), channel_id=1, source_target_pairs={{0,16},{1,17},{2,18},{3,19},{4,20},{5,21},{6,22},{7,23},{8,24},{9,... | collective-permute-start | bytes 196616 | tf_op jit(solution)/shard_map/ppermute | solution.py:318
  25.9 3.5 %collective-permute-start.24 = (bf16[128,512]{1,0:T(8,128)(2,1)S(1)}, bf16[128,512]{1,0:T(8,128)(2,1)S(1)}, u32[]{:S(2)}, u32[]{:S(2)}) collective-permute-start(bf16[128,512]{1,0:T(8,128)(2,1)S(1)} %get-tuple-element.33), channel_id=1, source_target_pairs={{0,16},{1,17},{2,18},{3,19},{4,20},{5,21},{6,22},{7,23},{8,24},{9,... | collective-permute-start | bytes 393224 | tf_op jit(solution)/shard_map/ppermute | solution.py:318
  29.7 2.6 %collective-permute-done.23.refs_0_ = bf16[128,512]{1,0:T(8,128)(2,1)S(1)} collective-permute-done((bf16[128,512]{1,0:T(8,128)(2,1)S(1)}, bf16[128,512]{1,0:T(8,128)(2,1)S(1)}, u32[]{:S(2)}, u32[]{:S(2)}) %collective-permute-start.23) | collective-permute-done | bytes 131104 | tf_op jit(solution)/shard_map/ppermute | solution.py:318
  32.3 7.0 %collective-permute-done.24.refs_1_ = bf16[128,512]{1,0:T(8,128)(2,1)S(1)} collective-permute-done((bf16[128,512]{1,0:T(8,128)(2,1)S(1)}, bf16[128,512]{1,0:T(8,128)(2,1)S(1)}, u32[]{:S(2)}, u32[]{:S(2)}) %collective-permute-start.24) | collective-permute-done | bytes 131104 | tf_op jit(solution)/shard_map/ppermute | solution.py:318
  39.4 18.6 %all_to_all.5.refs_0_ = bf16[8,128,256]{2,1,0:T(8,128)(2,1)S(1)} all-to-all(bf16[8,128,256]{2,1,0:T(8,128)(2,1)S(1)} %rank_round.1), channel_id=1, replica_groups=mesh['z'=4,'x'=2,'y'=2,'c'=2] {'z','x'}, dimensions={0} | all-to-all | bytes 1048576 | tf_op jit(solution)/shard_map/all_to_all | solution.py:354
  62.0 3.6 %collective-permute-start.32 = (bf16[128,896]{1,0:T(8,128)(2,1)S(1)}, bf16[128,896]{1,0:T(8,128)(2,1)S(1)}, u32[]{:S(2)}, u32[]{:S(2)}) collective-permute-start(bf16[128,896]{1,0:T(8,128)(2,1)S(1)} %get-tuple-element.66), channel_id=1, source_target_pairs={{0,16},{1,17},{2,18},{3,19},{4,20},{5,21},{6,22},{7,23},{8,24},{9,... | collective-permute-start | bytes 688136 | tf_op jit(solution)/shard_map/ppermute | solution.py:318
  66.5 2.6 %broadcast_select_fusion = (bf16[128,896]{1,0:T(8,128)(2,1)}, bf16[128,896]{1,0:T(8,128)(2,1)}, bf16[128,896]{1,0:T(8,128)(2,1)S(1)}, bf16[128,896]{1,0:T(8,128)...) fusion(pred[]{:T(512)S(6)} %eq.11, bf16[128,3584]{1,0:T(8,128)(2,1)} %param.19, s32[]{:T(128)S(6)} %select_n.116, ...), kind=kLoop, calls=%fused_computation.2 | loop fusion | flops 688128 | bytes 2752526 | tf_op jit(solution)/shard_map/jit(_where)/select_n | solution.py:365
  69.6 10.8 %collective-permute-start.30 = (bf16[128,896]{1,0:T(8,128)(2,1)S(1)}, bf16[128,896]{1,0:T(8,128)(2,1)S(1)}, u32[]{:S(2)}, u32[]{:S(2)}) collective-permute-start(bf16[128,896]{1,0:T(8,128)(2,1)S(1)} %get-tuple-element.61), channel_id=1, source_target_pairs={{0,8},{1,9},{2,10},{3,11},{4,12},{5,13},{6,14},{7,15},{8,0},{9,1},... | collective-permute-start | bytes 688136 | tf_op jit(solution)/shard_map/ppermute | solution.py:318
  80.4 4.0 %collective-permute-done.32.refs_8_ = bf16[128,896]{1,0:T(8,128)(2,1)S(1)} collective-permute-done((bf16[128,896]{1,0:T(8,128)(2,1)S(1)}, bf16[128,896]{1,0:T(8,128)(2,1)S(1)}, u32[]{:S(2)}, u32[]{:S(2)}) %collective-permute-start.32) | collective-permute-done | bytes 229408 | tf_op jit(solution)/shard_map/ppermute | solution.py:318
  84.9 2.9 %collective-permute-done.33.refs_9_ = bf16[128,896]{1,0:T(8,128)(2,1)S(1)} collective-permute-done((bf16[128,896]{1,0:T(8,128)(2,1)}, bf16[128,896]{1,0:T(8,128)(2,1)S(1)}, u32[]{:S(2)}, u32[]{:S(2)}) %collective-permute-start.33) | collective-permute-done | bytes 229408 | tf_op jit(solution)/shard_map/ppermute | solution.py:318
  90.9 5.4 %collective-permute-done.31.refs_7_ = bf16[128,896]{1,0:T(8,128)(2,1)} collective-permute-done((bf16[128,896]{1,0:T(8,128)(2,1)}, bf16[128,896]{1,0:T(8,128)(2,1)}, u32[]{:S(2)}, u32[]{:S(2)}) %collective-permute-start.31) | collective-permute-done | bytes 229408 | tf_op jit(solution)/shard_map/ppermute | solution.py:318
  96.4 3.4 %collective-permute-start.34 = (bf16[128,896]{1,0:T(8,128)(2,1)}, bf16[128,896]{1,0:T(8,128)(2,1)S(1)}, u32[]{:S(2)}, u32[]{:S(2)}) collective-permute-start(bf16[128,896]{1,0:T(8,128)(2,1)} %get-tuple-element.60), channel_id=1, source_target_pairs={{0,24},{1,25},{2,26},{3,27},{4,28},{5,29},{6,30},{7,31},{8,16},{9,... | collective-permute-start | bytes 688136 | tf_op jit(solution)/shard_map/ppermute | solution.py:318
  100.4 9.6 %collective-permute-done.4 = bf16[54,16,128]{2,1,0:T(8,128)(2,1)} collective-permute-done((bf16[54,16,128]{2,1,0:T(8,128)(2,1)}, bf16[54,16,128]{2,1,0:T(8,128)(2,1)}, u32[]{:S(2)}, u32[]{:S(2)}) %collective-permute-start.4) | collective-permute-done | bytes 221216 | tf_op jit(solution)/shard_map/ppermute | solution.py:318
  112.4 2.2 %collective-permute-start = (bf16[54,16,128]{2,1,0:T(8,128)(2,1)}, bf16[54,16,128]{2,1,0:T(8,128)(2,1)S(1)}, u32[]{:S(2)}, u32[]{:S(2)}) collective-permute-start(bf16[54,16,128]{2,1,0:T(8,128)(2,1)} %copy-done.11), channel_id=1, source_target_pairs={{0,4},{1,5},{2,6},{3,7},{4,0},{5,1},{6,2},{7,3},{8,12},{9,13},{10,... | collective-permute-start | bytes 663560 | tf_op jit(solution)/shard_map/ppermute | solution.py:318
  114.7 1.9 collective-permute-start.5
  116.7 2.5 %lowrank_first.1 = (f32[512,896]{1,0:T(8,128)S(1)}, bf16[512,128]{1,0:T(8,128)(2,1)S(1)}) custom-call(s32[6]{0:T(128)S(1)} %stack.27.idx, bf16[8,128,256]{2,1,0:T(8,128)(2,1)S(1)} %all_to_all.5.refs_0_, bf16[8,128,256]{2,1,0:T(8,128)(2,1)S(1)} %collective-permute-done.26.refs_1_, bf16[8,128,256]{2,1,0:T(8,128)(2,1)S(1)} %collective-permute-done.27.refs_2_, ...), custom_call_target="tpu_custom_call" | custom-call | tf_op jit(solution)/shard_map/lowrank_first/pallas_call | solution.py:402
  121.7 1.9 collective-permute-start.39
  124.9 2.0 collective-permute-start.8
  130.6 3.3 %lowrank_near.1 = (bf16[128,896]{1,0:T(8,128)(2,1)S(1)}, bf16[128,896]{1,0:T(8,128)(2,1)}, bf16[128,896]{1,0:T(8,128)(2,1)}, bf16[128,896]{1,0:T(8,128)(2,1)}) custom-call(s32[6]{0:T(128)S(1)} %stack.27.idx, bf16[8,128,256]{2,1,0:T(8,128)(2,1)S(1)} %all_to_all.5.refs_0_, bf16[8,128,256]{2,1,0:T(8,128)(2,1)S(1)} %collective-permute-done.26.refs_1_, ...), custom_call_target="tpu_custom_call" | custom-call | tf_op jit(solution)/shard_map/lowrank_near/pallas_call | solution.py:422
  135.3 2.1 %collective-permute-start.41 = (bf16[128,896]{1,0:T(8,128)(2,1)}, bf16[128,896]{1,0:T(8,128)(2,1)S(1)}, u32[]{:S(2)}, u32[]{:S(2)}) collective-permute-start(bf16[128,896]{1,0:T(8,128)(2,1)} %get-tuple-element.45), channel_id=1, source_target_pairs={{0,24},{1,25},{2,26},{3,27},{4,28},{5,29},{6,30},{7,31},{8,16},{9,... | collective-permute-start | bytes 688136 | tf_op jit(solution)/shard_map/ppermute | solution.py:318
  140.0 2.0 collective-permute-start.36
  142.7 3.2 %collective-permute-start.37 = (bf16[128,896]{1,0:T(8,128)(2,1)}, bf16[128,896]{1,0:T(8,128)(2,1)S(1)}, u32[]{:S(2)}, u32[]{:S(2)}) collective-permute-start(bf16[128,896]{1,0:T(8,128)(2,1)} %get-tuple-element.39), channel_id=1, source_target_pairs={{0,8},{1,9},{2,10},{3,11},{4,12},{5,13},{6,14},{7,15},{8,0},{9,1},... | collective-permute-start | bytes 688136 | tf_op jit(solution)/shard_map/ppermute | solution.py:318
  145.9 4.5 %collective-permute-done.40.refs_5_ = bf16[128,896]{1,0:T(8,128)(2,1)S(1)} collective-permute-done((bf16[128,896]{1,0:T(8,128)(2,1)S(1)}, bf16[128,896]{1,0:T(8,128)(2,1)S(1)}, u32[]{:S(2)}, u32[]{:S(2)}) %collective-permute-start.40) | collective-permute-done | bytes 229408 | tf_op jit(solution)/shard_map/ppermute | solution.py:318
  158.4 2.7 %sparse_forward.1.sparse = f32[2,128,3584]{2,1,0:T(8,128)S(1)} custom-call(s32[6]{0:T(128)S(1)} %stack.27.idx, s32[27]{0:T(128)S(1)} %copy-done.34, s32[27]{0:T(128)S(1)} %get-tuple-element.70.gate_cols.cols, s32[27]{0:T(128)S(1)} %copy-done.33, s32[27]{0:T(128)S(1)} %get-tuple-element.71.up_cols, bf16[128,4096]{1,0:T(8,128)(2,1)S(1)} %copy-done.1, ...), custom_call_target="tpu_custom_call" | custom-call | tf_op jit(solution)/shard_map/sparse_forward/pallas_call | solution.py:386
  161.2 3.4 %hidden_and_up_grads.1 = (bf16[128,3584]{1,0:T(8,128)(2,1)}, bf16[128,3584]{1,0:T(8,128)(2,1)S(1)}, f32[2,27,16,128]{3,2,1,0:T(8,128)S(1)}, bf16[2,27,16,128]{3,...) custom-call(s32[6]{0:T(128)S(1)} %stack.27.idx, s32[27]{0:T(128)S(1)} %copy-done.33, ...), custom_call_target="tpu_custom_call" | custom-call | tf_op jit(solution)/shard_map/hidden_and_up_grads/pallas_call | solution.py:436
  164.6 3.6 %collective-permute-start.47 = (bf16[2,27,16,128]{3,2,1,0:T(8,128)(2,1)S(1)}, bf16[2,27,16,128]{3,2,1,0:T(8,128)(2,1)S(1)}, u32[]{:S(2)}, u32[]{:S(2)}) collective-permute-start(bf16[2,27,16,128]{3,2,1,0:T(8,128)(2,1)S(1)} %get-tuple-element.56), channel_id=1, source_target_pairs={{0,8},{1,9},{2,10},{3,11},{4,12},{5,13},{6,14},{7,15},{8,0},{9,1},... | collective-permute-start | bytes 663560 | tf_op jit(solution)/shard_map/ppermute | solution.py:318
  172.2 5.2 %collective-permute-done.47 = bf16[2,27,16,128]{3,2,1,0:T(8,128)(2,1)S(1)} collective-permute-done((bf16[2,27,16,128]{3,2,1,0:T(8,128)(2,1)S(1)}, bf16[2,27,16,128]{3,2,1,0:T(8,128)(2,1)S(1)}, u32[]{:S(2)}, u32[]{:S(2)}) %collective-permute-start.47) | collective-permute-done | bytes 221216 | tf_op jit(solution)/shard_map/ppermute | solution.py:318
  177.4 7.8 %collective-permute-done.48 = bf16[2,27,16,128]{3,2,1,0:T(8,128)(2,1)S(1)} collective-permute-done((bf16[2,27,16,128]{3,2,1,0:T(8,128)(2,1)S(1)}, bf16[2,27,16,128]{3,2,1,0:T(8,128)(2,1)S(1)}, u32[]{:S(2)}, u32[]{:S(2)}) %collective-permute-start.48) | collective-permute-done | bytes 221216 | tf_op jit(solution)/shard_map/ppermute | solution.py:318
  186.6 4.9 %collective-permute-start.44 = (bf16[27,16,128]{2,1,0:T(8,128)(2,1)S(1)}, bf16[27,16,128]{2,1,0:T(8,128)(2,1)S(1)}, u32[]{:S(2)}, u32[]{:S(2)}) collective-permute-start(bf16[27,16,128]{2,1,0:T(8,128)(2,1)S(1)} %get-tuple-element.52), channel_id=1, source_target_pairs={{0,8},{1,9},{2,10},{3,11},{4,12},{5,13},{6,14},{7,15},{8,0},{9,1},... | collective-permute-start | bytes 331784 | tf_op jit(solution)/shard_map/ppermute | solution.py:318
  191.5 2.4 %collective-permute-start.46 = (bf16[27,16,128]{2,1,0:T(8,128)(2,1)S(1)}, bf16[27,16,128]{2,1,0:T(8,128)(2,1)S(1)}, u32[]{:S(2)}, u32[]{:S(2)}) collective-permute-start(bf16[27,16,128]{2,1,0:T(8,128)(2,1)S(1)} %get-tuple-element.54), channel_id=1, source_target_pairs={{0,24},{1,25},{2,26},{3,27},{4,28},{5,29},{6,30},{7,31},{8,16},{9,... | collective-permute-start | bytes 331784 | tf_op jit(solution)/shard_map/ppermute | solution.py:318
  195.0 6.9 %collective-permute-done.45 = bf16[27,16,128]{2,1,0:T(8,128)(2,1)S(1)} collective-permute-done((bf16[27,16,128]{2,1,0:T(8,128)(2,1)S(1)}, bf16[27,16,128]{2,1,0:T(8,128)(2,1)S(1)}, u32[]{:S(2)}, u32[]{:S(2)}) %collective-permute-start.45) | collective-permute-done | bytes 110624 | tf_op jit(solution)/shard_map/ppermute | solution.py:318
  (178 shorter events, 59.4 us)
Async XLA Ops:
  7.4 13.0 %collective-permute-start.21 = (bf16[512,256]{1,0:T(8,128)(2,1)}, bf16[512,256]{1,0:T(8,128)(2,1)S(1)}, u32[]{:S(2)}, u32[]{:S(2)}) collective-permute-start(bf16[512,256]{1,0:T(8,128)(2,1)} %refs_12_.1), channel_id=1, source_target_pairs={{0,4},{1,5},{2,6},{3,7},{4,0},{5,1},{6,2},{7,3},{8,12},{9,13},{10,... | collective-permute-start | bytes 786440 | tf_op jit(solution)/shard_map/ppermute | solution.py:318
  9.1 11.6 %collective-permute-start.22 = (bf16[512,256]{1,0:T(8,128)(2,1)}, bf16[512,256]{1,0:T(8,128)(2,1)S(1)}, u32[]{:S(2)}, u32[]{:S(2)}) collective-permute-start(bf16[512,256]{1,0:T(8,128)(2,1)} %refs_13_.1), channel_id=1, source_target_pairs={{0,4},{1,5},{2,6},{3,7},{4,0},{5,1},{6,2},{7,3},{8,12},{9,13},{10,... | collective-permute-start | bytes 786440 | tf_op jit(solution)/shard_map/ppermute | solution.py:318
  25.9 13.3 %collective-permute-start.24 = (bf16[128,512]{1,0:T(8,128)(2,1)S(1)}, bf16[128,512]{1,0:T(8,128)(2,1)S(1)}, u32[]{:S(2)}, u32[]{:S(2)}) collective-permute-start(bf16[128,512]{1,0:T(8,128)(2,1)S(1)} %get-tuple-element.33), channel_id=1, source_target_pairs={{0,16},{1,17},{2,18},{3,19},{4,20},{5,21},{6,22},{7,23},{8,24},{9,... | collective-permute-start | bytes 393224 | tf_op jit(solution)/shard_map/ppermute | solution.py:318
  58.0 26.4 %collective-permute-start.27 = (bf16[8,128,256]{2,1,0:T(8,128)(2,1)S(1)}, bf16[8,128,256]{2,1,0:T(8,128)(2,1)S(1)}, u32[]{:S(2)}, u32[]{:S(2)}) collective-permute-start(bf16[8,128,256]{2,1,0:T(8,128)(2,1)S(1)} %all_to_all.5.refs_0_), channel_id=1, source_target_pairs={{0,2},{1,3},{2,0},{3,1},{4,6},{5,7},{6,4},{7,5},{8,10},{9,11},{10,... | collective-permute-start | bytes 1572872 | tf_op jit(solution)/shard_map/ppermute | solution.py:318
  58.3 10.8 %collective-permute-start.1 = (bf16[54,16,128]{2,1,0:T(8,128)(2,1)S(1)}, bf16[54,16,128]{2,1,0:T(8,128)(2,1)}, u32[]{:S(2)}, u32[]{:S(2)}) collective-permute-start(bf16[54,16,128]{2,1,0:T(8,128)(2,1)S(1)} %slice.12.refs_0_), channel_id=1, source_target_pairs={{0,8},{1,9},{2,10},{3,11},{4,12},{5,13},{6,14},{7,15},{8,0},{9,1},... | collective-permute-start | bytes 663560 | tf_op jit(solution)/shard_map/ppermute | solution.py:318
  62.0 22.4 %collective-permute-start.32 = (bf16[128,896]{1,0:T(8,128)(2,1)S(1)}, bf16[128,896]{1,0:T(8,128)(2,1)S(1)}, u32[]{:S(2)}, u32[]{:S(2)}) collective-permute-start(bf16[128,896]{1,0:T(8,128)(2,1)S(1)} %get-tuple-element.66), channel_id=1, source_target_pairs={{0,16},{1,17},{2,18},{3,19},{4,20},{5,21},{6,22},{7,23},{8,24},{9,... | collective-permute-start | bytes 688136 | tf_op jit(solution)/shard_map/ppermute | solution.py:318
  65.6 22.2 %collective-permute-start.33 = (bf16[128,896]{1,0:T(8,128)(2,1)}, bf16[128,896]{1,0:T(8,128)(2,1)S(1)}, u32[]{:S(2)}, u32[]{:S(2)}) collective-permute-start(bf16[128,896]{1,0:T(8,128)(2,1)} %get-tuple-element.65), channel_id=1, source_target_pairs={{0,20},{1,21},{2,22},{3,23},{4,16},{5,17},{6,18},{7,19},{8,28},{9,... | collective-permute-start | bytes 688136 | tf_op jit(solution)/shard_map/ppermute | solution.py:318
  69.0 18.8 %collective-permute-start.29 = (bf16[128,896]{1,0:T(8,128)(2,1)S(1)}, bf16[128,896]{1,0:T(8,128)(2,1)S(1)}, u32[]{:S(2)}, u32[]{:S(2)}) collective-permute-start(bf16[128,896]{1,0:T(8,128)(2,1)S(1)} %get-tuple-element.64), channel_id=1, source_target_pairs={{0,4},{1,5},{2,6},{3,7},{4,0},{5,1},{6,2},{7,3},{8,12},{9,13},{10,... | collective-permute-start | bytes 688136 | tf_op jit(solution)/shard_map/ppermute | solution.py:318
  69.6 20.0 %collective-permute-start.30 = (bf16[128,896]{1,0:T(8,128)(2,1)S(1)}, bf16[128,896]{1,0:T(8,128)(2,1)S(1)}, u32[]{:S(2)}, u32[]{:S(2)}) collective-permute-start(bf16[128,896]{1,0:T(8,128)(2,1)S(1)} %get-tuple-element.61), channel_id=1, source_target_pairs={{0,8},{1,9},{2,10},{3,11},{4,12},{5,13},{6,14},{7,15},{8,0},{9,1},... | collective-permute-start | bytes 688136 | tf_op jit(solution)/shard_map/ppermute | solution.py:318
  84.4 30.2 %collective-permute-start.26 = (bf16[8,128,256]{2,1,0:T(8,128)(2,1)S(1)}, bf16[8,128,256]{2,1,0:T(8,128)(2,1)S(1)}, u32[]{:S(2)}, u32[]{:S(2)}) collective-permute-start(bf16[8,128,256]{2,1,0:T(8,128)(2,1)S(1)} %all_to_all.5.refs_0_), channel_id=1, source_target_pairs={{0,1},{1,0},{2,3},{3,2},{4,5},{5,4},{6,7},{7,6},{8,9},{9,8},{10,11... | collective-permute-start | bytes 1572872 | tf_op jit(solution)/shard_map/ppermute | solution.py:318
  84.4 30.3 %collective-permute-start.28 = (bf16[8,128,256]{2,1,0:T(8,128)(2,1)S(1)}, bf16[8,128,256]{2,1,0:T(8,128)(2,1)S(1)}, u32[]{:S(2)}, u32[]{:S(2)}) collective-permute-start(bf16[8,128,256]{2,1,0:T(8,128)(2,1)S(1)} %collective-permute-done.27.refs_2_), channel_id=1, source_target_pairs={{0,1},{1,0},{2,3},{3,2},{4,5},{5,4},{6,7},{7,6},{8,9},{9,8},{10,11... | collective-permute-start | bytes 1572872 | tf_op jit(solution)/shard_map/ppermute | solution.py:318
  87.8 12.0 %collective-permute-start.6 = (bf16[54,16,128]{2,1,0:T(8,128)(2,1)}, bf16[54,16,128]{2,1,0:T(8,128)(2,1)}, u32[]{:S(2)}, u32[]{:S(2)}) collective-permute-start(bf16[54,16,128]{2,1,0:T(8,128)(2,1)} %collective-permute-done.1.refs_2_), channel_id=1, source_target_pairs={{8,16},{9,17},{10,18},{11,19},{12,20},{13,21},{14,22},{15,23},{16,... | collective-permute-start | bytes 663560 | tf_op jit(solution)/shard_map/ppermute | solution.py:318
  89.6 20.3 %collective-permute-start.4 = (bf16[54,16,128]{2,1,0:T(8,128)(2,1)}, bf16[54,16,128]{2,1,0:T(8,128)(2,1)}, u32[]{:S(2)}, u32[]{:S(2)}) collective-permute-start(bf16[54,16,128]{2,1,0:T(8,128)(2,1)} %copy-done.35), channel_id=1, source_target_pairs={{8,0},{9,1},{10,2},{11,3},{12,4},{13,5},{14,6},{15,7},{16,24},{17,... | collective-permute-start | bytes 663560 | tf_op jit(solution)/shard_map/ppermute | solution.py:318
  96.4 16.0 %collective-permute-start.34 = (bf16[128,896]{1,0:T(8,128)(2,1)}, bf16[128,896]{1,0:T(8,128)(2,1)S(1)}, u32[]{:S(2)}, u32[]{:S(2)}) collective-permute-start(bf16[128,896]{1,0:T(8,128)(2,1)} %get-tuple-element.60), channel_id=1, source_target_pairs={{0,24},{1,25},{2,26},{3,27},{4,28},{5,29},{6,30},{7,31},{8,16},{9,... | collective-permute-start | bytes 688136 | tf_op jit(solution)/shard_map/ppermute | solution.py:318
  99.8 20.7 %collective-permute-start.35 = (bf16[128,896]{1,0:T(8,128)(2,1)}, bf16[128,896]{1,0:T(8,128)(2,1)S(1)}, u32[]{:S(2)}, u32[]{:S(2)}) collective-permute-start(bf16[128,896]{1,0:T(8,128)(2,1)} %get-tuple-element.59), channel_id=1, source_target_pairs={{0,28},{1,29},{2,30},{3,31},{4,24},{5,25},{6,26},{7,27},{8,20},{9,... | collective-permute-start | bytes 688136 | tf_op jit(solution)/shard_map/ppermute | solution.py:318
  110.0 13.6 %collective-permute-start.7 = (bf16[54,16,128]{2,1,0:T(8,128)(2,1)}, bf16[54,16,128]{2,1,0:T(8,128)(2,1)S(1)}, u32[]{:S(2)}, u32[]{:S(2)}) collective-permute-start(bf16[54,16,128]{2,1,0:T(8,128)(2,1)} %collective-permute-done.6), channel_id=1, source_target_pairs={{8,0},{9,1},{10,2},{11,3},{12,4},{13,5},{14,6},{15,7},{16,24},{17,... | collective-permute-start | bytes 663560 | tf_op jit(solution)/shard_map/ppermute | solution.py:318
  112.4 11.7 %collective-permute-start = (bf16[54,16,128]{2,1,0:T(8,128)(2,1)}, bf16[54,16,128]{2,1,0:T(8,128)(2,1)S(1)}, u32[]{:S(2)}, u32[]{:S(2)}) collective-permute-start(bf16[54,16,128]{2,1,0:T(8,128)(2,1)} %copy-done.11), channel_id=1, source_target_pairs={{0,4},{1,5},{2,6},{3,7},{4,0},{5,1},{6,2},{7,3},{8,12},{9,13},{10,... | collective-permute-start | bytes 663560 | tf_op jit(solution)/shard_map/ppermute | solution.py:318
  114.6 20.0 %collective-permute-start.2 = (bf16[54,16,128]{2,1,0:T(8,128)(2,1)}, bf16[54,16,128]{2,1,0:T(8,128)(2,1)S(1)}, u32[]{:S(2)}, u32[]{:S(2)}) collective-permute-start(bf16[54,16,128]{2,1,0:T(8,128)(2,1)} %collective-permute-done.1.refs_2_), channel_id=1, source_target_pairs={{0,4},{1,5},{2,6},{3,7},{4,0},{5,1},{6,2},{7,3},{8,12},{9,13},{10,... | collective-permute-start | bytes 663560 | tf_op jit(solution)/shard_map/ppermute | solution.py:318
  114.7 22.7 %collective-permute-start.5 = (bf16[54,16,128]{2,1,0:T(8,128)(2,1)S(1)}, bf16[54,16,128]{2,1,0:T(8,128)(2,1)S(1)}, u32[]{:S(2)}, u32[]{:S(2)}) collective-permute-start(bf16[54,16,128]{2,1,0:T(8,128)(2,1)S(1)} %broadcast_select_fusion.9.refs_4_), channel_id=1, source_target_pairs={{0,4},{1,5},{2,6},{3,7},{4,0},{5,1},{6,2},{7,3},{8,12},{9,13},{10,... | collective-permute-start | bytes 663560 | tf_op jit(solution)/shard_map/ppermute | solution.py:318
  121.7 20.3 %collective-permute-start.39 = (bf16[128,896]{1,0:T(8,128)(2,1)S(1)}, bf16[128,896]{1,0:T(8,128)(2,1)S(1)}, u32[]{:S(2)}, u32[]{:S(2)}) collective-permute-start(bf16[128,896]{1,0:T(8,128)(2,1)S(1)} %get-tuple-element.43), channel_id=1, source_target_pairs={{0,16},{1,17},{2,18},{3,19},{4,20},{5,21},{6,22},{7,23},{8,24},{9,... | collective-permute-start | bytes 688136 | tf_op jit(solution)/shard_map/ppermute | solution.py:318
  123.6 26.9 %collective-permute-start.40 = (bf16[128,896]{1,0:T(8,128)(2,1)S(1)}, bf16[128,896]{1,0:T(8,128)(2,1)S(1)}, u32[]{:S(2)}, u32[]{:S(2)}) collective-permute-start(bf16[128,896]{1,0:T(8,128)(2,1)S(1)} %get-tuple-element.44), channel_id=1, source_target_pairs={{0,20},{1,21},{2,22},{3,23},{4,16},{5,17},{6,18},{7,19},{8,28},{9,... | collective-permute-start | bytes 688136 | tf_op jit(solution)/shard_map/ppermute | solution.py:318
  124.9 14.4 %collective-permute-start.8 = (bf16[54,16,128]{2,1,0:T(8,128)(2,1)S(1)}, bf16[54,16,128]{2,1,0:T(8,128)(2,1)S(1)}, u32[]{:S(2)}, u32[]{:S(2)}) collective-permute-start(bf16[54,16,128]{2,1,0:T(8,128)(2,1)S(1)} %broadcast_select_fusion.8.refs_6_), channel_id=1, source_target_pairs={{0,4},{1,5},{2,6},{3,7},{4,0},{5,1},{6,2},{7,3},{8,12},{9,13},{10,... | collective-permute-start | bytes 663560 | tf_op jit(solution)/shard_map/ppermute | solution.py:318
  135.3 25.8 %collective-permute-start.41 = (bf16[128,896]{1,0:T(8,128)(2,1)}, bf16[128,896]{1,0:T(8,128)(2,1)S(1)}, u32[]{:S(2)}, u32[]{:S(2)}) collective-permute-start(bf16[128,896]{1,0:T(8,128)(2,1)} %get-tuple-element.45), channel_id=1, source_target_pairs={{0,24},{1,25},{2,26},{3,27},{4,28},{5,29},{6,30},{7,31},{8,16},{9,... | collective-permute-start | bytes 688136 | tf_op jit(solution)/shard_map/ppermute | solution.py:318
  138.1 23.0 %collective-permute-start.42 = (bf16[128,896]{1,0:T(8,128)(2,1)}, bf16[128,896]{1,0:T(8,128)(2,1)S(1)}, u32[]{:S(2)}, u32[]{:S(2)}) collective-permute-start(bf16[128,896]{1,0:T(8,128)(2,1)} %get-tuple-element.46), channel_id=1, source_target_pairs={{0,28},{1,29},{2,30},{3,31},{4,24},{5,25},{6,26},{7,27},{8,20},{9,... | collective-permute-start | bytes 688136 | tf_op jit(solution)/shard_map/ppermute | solution.py:318
  140.0 21.1 %collective-permute-start.36 = (bf16[128,896]{1,0:T(8,128)(2,1)}, bf16[128,896]{1,0:T(8,128)(2,1)S(1)}, u32[]{:S(2)}, u32[]{:S(2)}) collective-permute-start(bf16[128,896]{1,0:T(8,128)(2,1)} %get-tuple-element.38), channel_id=1, source_target_pairs={{0,4},{1,5},{2,6},{3,7},{4,0},{5,1},{6,2},{7,3},{8,12},{9,13},{10,... | collective-permute-start | bytes 688136 | tf_op jit(solution)/shard_map/ppermute | solution.py:318
  142.7 18.5 %collective-permute-start.37 = (bf16[128,896]{1,0:T(8,128)(2,1)}, bf16[128,896]{1,0:T(8,128)(2,1)S(1)}, u32[]{:S(2)}, u32[]{:S(2)}) collective-permute-start(bf16[128,896]{1,0:T(8,128)(2,1)} %get-tuple-element.39), channel_id=1, source_target_pairs={{0,8},{1,9},{2,10},{3,11},{4,12},{5,13},{6,14},{7,15},{8,0},{9,1},... | collective-permute-start | bytes 688136 | tf_op jit(solution)/shard_map/ppermute | solution.py:318
  164.6 12.8 %collective-permute-start.47 = (bf16[2,27,16,128]{3,2,1,0:T(8,128)(2,1)S(1)}, bf16[2,27,16,128]{3,2,1,0:T(8,128)(2,1)S(1)}, u32[]{:S(2)}, u32[]{:S(2)}) collective-permute-start(bf16[2,27,16,128]{3,2,1,0:T(8,128)(2,1)S(1)} %get-tuple-element.56), channel_id=1, source_target_pairs={{0,8},{1,9},{2,10},{3,11},{4,12},{5,13},{6,14},{7,15},{8,0},{9,1},... | collective-permute-start | bytes 663560 | tf_op jit(solution)/shard_map/ppermute | solution.py:318
  168.2 17.0 %collective-permute-start.48 = (bf16[2,27,16,128]{3,2,1,0:T(8,128)(2,1)S(1)}, bf16[2,27,16,128]{3,2,1,0:T(8,128)(2,1)S(1)}, u32[]{:S(2)}, u32[]{:S(2)}) collective-permute-start(bf16[2,27,16,128]{3,2,1,0:T(8,128)(2,1)S(1)} %get-tuple-element.57), channel_id=1, source_target_pairs={{0,16},{1,17},{2,18},{3,19},{4,20},{5,21},{6,22},{7,23},{8,24},{9,... | collective-permute-start | bytes 663560 | tf_op jit(solution)/shard_map/ppermute | solution.py:318
  169.2 16.0 %collective-permute-start.49 = (bf16[2,27,16,128]{3,2,1,0:T(8,128)(2,1)S(1)}, bf16[2,27,16,128]{3,2,1,0:T(8,128)(2,1)S(1)}, u32[]{:S(2)}, u32[]{:S(2)}) collective-permute-start(bf16[2,27,16,128]{3,2,1,0:T(8,128)(2,1)S(1)} %get-tuple-element.58), channel_id=1, source_target_pairs={{0,24},{1,25},{2,26},{3,27},{4,28},{5,29},{6,30},{7,31},{8,16},{9,... | collective-permute-start | bytes 663560 | tf_op jit(solution)/shard_map/ppermute | solution.py:318
  171.8 14.7 %collective-permute-start.43 = (bf16[4,27,16,128]{3,2,1,0:T(8,128)(2,1)S(1)}, bf16[4,27,16,128]{3,2,1,0:T(8,128)(2,1)S(1)}, u32[]{:S(2)}, u32[]{:S(2)}) collective-permute-start(bf16[4,27,16,128]{3,2,1,0:T(8,128)(2,1)S(1)} %get-tuple-element.50), channel_id=1, source_target_pairs={{0,4},{1,5},{2,6},{3,7},{4,0},{5,1},{6,2},{7,3},{8,12},{9,13},{10,... | collective-permute-start | bytes 1327112 | tf_op jit(solution)/shard_map/ppermute | solution.py:318
  191.5 10.4 %collective-permute-start.45 = (bf16[27,16,128]{2,1,0:T(8,128)(2,1)S(1)}, bf16[27,16,128]{2,1,0:T(8,128)(2,1)S(1)}, u32[]{:S(2)}, u32[]{:S(2)}) collective-permute-start(bf16[27,16,128]{2,1,0:T(8,128)(2,1)S(1)} %get-tuple-element.53), channel_id=1, source_target_pairs={{0,16},{1,17},{2,18},{3,19},{4,20},{5,21},{6,22},{7,23},{8,24},{9,... | collective-permute-start | bytes 331784 | tf_op jit(solution)/shard_map/ppermute | solution.py:318
  191.5 10.4 %collective-permute-start.46 = (bf16[27,16,128]{2,1,0:T(8,128)(2,1)S(1)}, bf16[27,16,128]{2,1,0:T(8,128)(2,1)S(1)}, u32[]{:S(2)}, u32[]{:S(2)}) collective-permute-start(bf16[27,16,128]{2,1,0:T(8,128)(2,1)S(1)} %get-tuple-element.54), channel_id=1, source_target_pairs={{0,24},{1,25},{2,26},{3,27},{4,28},{5,29},{6,30},{7,31},{8,16},{9,... | collective-permute-start | bytes 331784 | tf_op jit(solution)/shard_map/ppermute | solution.py:318
  (59 other events, 552.1 us)

commit v4 on v3

--- a/solution.py
+++ b/solution.py
@@ -348,7 +348,7 @@
         out_shape=jax.ShapeDtypeStruct((nf, rows, slice_width), BF16),
         in_specs=[VMEM] * nz,
         out_specs=VMEM,
-        name="rank_round",
+        name="rr11",
         compiler_params=grant(4),
     )(sums[0], *got)
     stack = lax.all_to_all(for_f, ("z", "x"), 0, 0, tiled=True)
@@ -408,7 +408,7 @@
         in_specs=[SMEM] + [VMEM] * (nt + nf - 1),
         out_specs=[VMEM] * 2,
         scratch_shapes=scratch,
-        name="lowrank_first",
+        name="lf28",
         compiler_params=grant(14),
     )(idx, *ranks, *rights[:-1])
     far_products = pl.pallas_call(
@@ -460,7 +460,7 @@
         ],
         in_specs=[SMEM] * 3 + [VMEM] * 2,
         out_specs=[VMEM] * 2,
-        name="gate_grads",
+        name="gg27",
         compiler_params=grant(10),
     )(idx, gate_rows, gate_cols - base, tokens, dpre_gate)
 
@@ -474,7 +474,7 @@
         + [jax.ShapeDtypeStruct(support, BF16)] * (nz - 1),
         in_specs=[VMEM] * 2,
         out_specs=[VMEM] * nz,
-        name="gate_add",
+        name="ga26",
         compiler_params=grant(6),
     )(gate_keep, gate_got)
     for j in range(1, nz):

time: 204 us -> 204 us (level)
  no operation moved by 1% of the time
where the time goes in v4:
time: 204 us; the launch traced here: 203 us
  starting transfers between devices  76.7 us (38%)
  waiting for transfers between devices  62.4 us (31%)
  local copies, waits for them, and re-layouts  22.5 us (11%)
  blocking collectives  18.6 us (9%)
  Pallas kernels  15.8 us (8%)
  other arithmetic  5.67 us (3%)
    ppermute x51, starting transfers between devices, move(): return lax.ppermute(value, AXES, pairs)  76.7 us
    ppermute x51, waiting for transfers between devices, move(): return lax.ppermute(value, AXES, pairs)  62.4 us
    unnamed x85, local copies, waits for them, and re-layouts  21.4 us
    all_to_all x1, blocking collectives, exchange_device(): stack = lax.all_to_all(for_f, ('z', 'x'), 0, 0, tiled=True)  18.6 us
    select_n x2, other arithmetic, exchange_device(): jnp.where(x ^ k % 2 == 0, lax.dynamic_slice(gate_k, start, size), lax.dyn...  4.38 us
  transfers between devices with their start and end apart: 51, of which 19 were waited for; matrix products, arithmetic and copies ran while one was open for 3% of the time, Pallas kernels for 5%

profile of v4, /device:TPU:0, one launch (start us, length us, event | category | flops | bytes accessed | tf_op | source)
XLA Modules:
  0.0 202.8 jit_solution(3574099698561778621)
XLA Ops:
  1.7 3.1 %collective-permute-start.9 = (bf16[128,256]{1,0:T(8,128)(2,1)S(1)}, bf16[128,256]{1,0:T(8,128)(2,1)S(1)}, u32[]{:S(2)}, u32[]{:S(2)}) collective-permute-start(bf16[128,256]{1,0:T(8,128)(2,1)S(1)} %get-tuple-element.69), channel_id=1, source_target_pairs={{0,8},{1,9},{2,10},{3,11},{4,12},{5,13},{6,14},{7,15},{8,0},{9,1},... | collective-permute-start | bytes 196616 | tf_op jit(solution)/shard_map/ppermute | solution.py:318
  4.8 2.6 %collective-permute-start.10 = (bf16[128,256]{1,0:T(8,128)(2,1)S(1)}, bf16[128,256]{1,0:T(8,128)(2,1)S(1)}, u32[]{:S(2)}, u32[]{:S(2)}) collective-permute-start(bf16[128,256]{1,0:T(8,128)(2,1)S(1)} %get-tuple-element.68), channel_id=1, source_target_pairs={{0,16},{1,17},{2,18},{3,19},{4,20},{5,21},{6,22},{7,23},{8,24},{9,... | collective-permute-start | bytes 196616 | tf_op jit(solution)/shard_map/ppermute | solution.py:318
  25.9 3.5 %collective-permute-start.24 = (bf16[128,512]{1,0:T(8,128)(2,1)S(1)}, bf16[128,512]{1,0:T(8,128)(2,1)S(1)}, u32[]{:S(2)}, u32[]{:S(2)}) collective-permute-start(bf16[128,512]{1,0:T(8,128)(2,1)S(1)} %get-tuple-element.33), channel_id=1, source_target_pairs={{0,16},{1,17},{2,18},{3,19},{4,20},{5,21},{6,22},{7,23},{8,24},{9,... | collective-permute-start | bytes 393224 | tf_op jit(solution)/shard_map/ppermute | solution.py:318
  29.7 2.6 %collective-permute-done.23.refs_0_ = bf16[128,512]{1,0:T(8,128)(2,1)S(1)} collective-permute-done((bf16[128,512]{1,0:T(8,128)(2,1)S(1)}, bf16[128,512]{1,0:T(8,128)(2,1)S(1)}, u32[]{:S(2)}, u32[]{:S(2)}) %collective-permute-start.23) | collective-permute-done | bytes 131104 | tf_op jit(solution)/shard_map/ppermute | solution.py:318
  32.3 7.0 %collective-permute-done.24.refs_1_ = bf16[128,512]{1,0:T(8,128)(2,1)S(1)} collective-permute-done((bf16[128,512]{1,0:T(8,128)(2,1)S(1)}, bf16[128,512]{1,0:T(8,128)(2,1)S(1)}, u32[]{:S(2)}, u32[]{:S(2)}) %collective-permute-start.24) | collective-permute-done | bytes 131104 | tf_op jit(solution)/shard_map/ppermute | solution.py:318
  39.4 18.6 %all_to_all.5.refs_0_ = bf16[8,128,256]{2,1,0:T(8,128)(2,1)S(1)} all-to-all(bf16[8,128,256]{2,1,0:T(8,128)(2,1)S(1)} %rr11.1), channel_id=1, replica_groups=mesh['z'=4,'x'=2,'y'=2,'c'=2] {'z','x'}, dimensions={0} | all-to-all | bytes 1048576 | tf_op jit(solution)/shard_map/all_to_all | solution.py:354
  62.0 3.6 %collective-permute-start.32 = (bf16[128,896]{1,0:T(8,128)(2,1)S(1)}, bf16[128,896]{1,0:T(8,128)(2,1)S(1)}, u32[]{:S(2)}, u32[]{:S(2)}) collective-permute-start(bf16[128,896]{1,0:T(8,128)(2,1)S(1)} %get-tuple-element.66), channel_id=1, source_target_pairs={{0,16},{1,17},{2,18},{3,19},{4,20},{5,21},{6,22},{7,23},{8,24},{9,... | collective-permute-start | bytes 688136 | tf_op jit(solution)/shard_map/ppermute | solution.py:318
  66.5 2.6 %broadcast_select_fusion = (bf16[128,896]{1,0:T(8,128)(2,1)}, bf16[128,896]{1,0:T(8,128)(2,1)}, bf16[128,896]{1,0:T(8,128)(2,1)S(1)}, bf16[128,896]{1,0:T(8,128)...) fusion(pred[]{:T(512)S(6)} %eq.11, bf16[128,3584]{1,0:T(8,128)(2,1)} %param.19, s32[]{:T(128)S(6)} %select_n.116, ...), kind=kLoop, calls=%fused_computation.2 | loop fusion | flops 688128 | bytes 2752526 | tf_op jit(solution)/shard_map/jit(_where)/select_n | solution.py:365
  69.6 10.8 %collective-permute-start.30 = (bf16[128,896]{1,0:T(8,128)(2,1)S(1)}, bf16[128,896]{1,0:T(8,128)(2,1)S(1)}, u32[]{:S(2)}, u32[]{:S(2)}) collective-permute-start(bf16[128,896]{1,0:T(8,128)(2,1)S(1)} %get-tuple-element.61), channel_id=1, source_target_pairs={{0,8},{1,9},{2,10},{3,11},{4,12},{5,13},{6,14},{7,15},{8,0},{9,1},... | collective-permute-start | bytes 688136 | tf_op jit(solution)/shard_map/ppermute | solution.py:318
  80.4 4.0 %collective-permute-done.32.refs_8_ = bf16[128,896]{1,0:T(8,128)(2,1)S(1)} collective-permute-done((bf16[128,896]{1,0:T(8,128)(2,1)S(1)}, bf16[128,896]{1,0:T(8,128)(2,1)S(1)}, u32[]{:S(2)}, u32[]{:S(2)}) %collective-permute-start.32) | collective-permute-done | bytes 229408 | tf_op jit(solution)/shard_map/ppermute | solution.py:318
  84.9 2.9 %collective-permute-done.33.refs_9_ = bf16[128,896]{1,0:T(8,128)(2,1)S(1)} collective-permute-done((bf16[128,896]{1,0:T(8,128)(2,1)}, bf16[128,896]{1,0:T(8,128)(2,1)S(1)}, u32[]{:S(2)}, u32[]{:S(2)}) %collective-permute-start.33) | collective-permute-done | bytes 229408 | tf_op jit(solution)/shard_map/ppermute | solution.py:318
  90.9 5.4 %collective-permute-done.31.refs_7_ = bf16[128,896]{1,0:T(8,128)(2,1)} collective-permute-done((bf16[128,896]{1,0:T(8,128)(2,1)}, bf16[128,896]{1,0:T(8,128)(2,1)}, u32[]{:S(2)}, u32[]{:S(2)}) %collective-permute-start.31) | collective-permute-done | bytes 229408 | tf_op jit(solution)/shard_map/ppermute | solution.py:318
  96.4 3.4 %collective-permute-start.34 = (bf16[128,896]{1,0:T(8,128)(2,1)}, bf16[128,896]{1,0:T(8,128)(2,1)S(1)}, u32[]{:S(2)}, u32[]{:S(2)}) collective-permute-start(bf16[128,896]{1,0:T(8,128)(2,1)} %get-tuple-element.60), channel_id=1, source_target_pairs={{0,24},{1,25},{2,26},{3,27},{4,28},{5,29},{6,30},{7,31},{8,16},{9,... | collective-permute-start | bytes 688136 | tf_op jit(solution)/shard_map/ppermute | solution.py:318
  100.4 9.6 %collective-permute-done.4 = bf16[54,16,128]{2,1,0:T(8,128)(2,1)} collective-permute-done((bf16[54,16,128]{2,1,0:T(8,128)(2,1)}, bf16[54,16,128]{2,1,0:T(8,128)(2,1)}, u32[]{:S(2)}, u32[]{:S(2)}) %collective-permute-start.4) | collective-permute-done | bytes 221216 | tf_op jit(solution)/shard_map/ppermute | solution.py:318
  112.4 2.2 %collective-permute-start = (bf16[54,16,128]{2,1,0:T(8,128)(2,1)}, bf16[54,16,128]{2,1,0:T(8,128)(2,1)S(1)}, u32[]{:S(2)}, u32[]{:S(2)}) collective-permute-start(bf16[54,16,128]{2,1,0:T(8,128)(2,1)} %copy-done.11), channel_id=1, source_target_pairs={{0,4},{1,5},{2,6},{3,7},{4,0},{5,1},{6,2},{7,3},{8,12},{9,13},{10,... | collective-permute-start | bytes 663560 | tf_op jit(solution)/shard_map/ppermute | solution.py:318
  114.7 1.9 collective-permute-start.5
  116.7 2.5 %lf28.1 = (f32[512,896]{1,0:T(8,128)S(1)}, bf16[512,128]{1,0:T(8,128)(2,1)S(1)}) custom-call(s32[6]{0:T(128)S(1)} %stack.27.idx, bf16[8,128,256]{2,1,0:T(8,128)(2,1)S(1)} %all_to_all.5.refs_0_, bf16[8,128,256]{2,1,0:T(8,128)(2,1)S(1)} %collective-permute-done.26.refs_1_, bf16[8,128,256]{2,1,0:T(8,128)(2,1)S(1)} %collective-permute-done.27.refs_2_, ...), custom_call_target="tpu_custom_call" | custom-call | tf_op jit(solution)/shard_map/lf28/pallas_call | solution.py:402
  121.7 1.9 collective-permute-start.39
  124.9 2.0 collective-permute-start.8
  130.6 3.3 %lowrank_near.1 = (bf16[128,896]{1,0:T(8,128)(2,1)S(1)}, bf16[128,896]{1,0:T(8,128)(2,1)}, bf16[128,896]{1,0:T(8,128)(2,1)}, bf16[128,896]{1,0:T(8,128)(2,1)}) custom-call(s32[6]{0:T(128)S(1)} %stack.27.idx, bf16[8,128,256]{2,1,0:T(8,128)(2,1)S(1)} %all_to_all.5.refs_0_, bf16[8,128,256]{2,1,0:T(8,128)(2,1)S(1)} %collective-permute-done.26.refs_1_, ...), custom_call_target="tpu_custom_call" | custom-call | tf_op jit(solution)/shard_map/lowrank_near/pallas_call | solution.py:422
  135.3 2.1 %collective-permute-start.41 = (bf16[128,896]{1,0:T(8,128)(2,1)}, bf16[128,896]{1,0:T(8,128)(2,1)S(1)}, u32[]{:S(2)}, u32[]{:S(2)}) collective-permute-start(bf16[128,896]{1,0:T(8,128)(2,1)} %get-tuple-element.45), channel_id=1, source_target_pairs={{0,24},{1,25},{2,26},{3,27},{4,28},{5,29},{6,30},{7,31},{8,16},{9,... | collective-permute-start | bytes 688136 | tf_op jit(solution)/shard_map/ppermute | solution.py:318
  140.0 2.0 collective-permute-start.36
  142.7 3.2 %collective-permute-start.37 = (bf16[128,896]{1,0:T(8,128)(2,1)}, bf16[128,896]{1,0:T(8,128)(2,1)S(1)}, u32[]{:S(2)}, u32[]{:S(2)}) collective-permute-start(bf16[128,896]{1,0:T(8,128)(2,1)} %get-tuple-element.39), channel_id=1, source_target_pairs={{0,8},{1,9},{2,10},{3,11},{4,12},{5,13},{6,14},{7,15},{8,0},{9,1},... | collective-permute-start | bytes 688136 | tf_op jit(solution)/shard_map/ppermute | solution.py:318
  145.9 4.5 %collective-permute-done.40.refs_5_ = bf16[128,896]{1,0:T(8,128)(2,1)S(1)} collective-permute-done((bf16[128,896]{1,0:T(8,128)(2,1)S(1)}, bf16[128,896]{1,0:T(8,128)(2,1)S(1)}, u32[]{:S(2)}, u32[]{:S(2)}) %collective-permute-start.40) | collective-permute-done | bytes 229408 | tf_op jit(solution)/shard_map/ppermute | solution.py:318
  158.4 2.7 %sparse_forward.1.sparse = f32[2,128,3584]{2,1,0:T(8,128)S(1)} custom-call(s32[6]{0:T(128)S(1)} %stack.27.idx, s32[27]{0:T(128)S(1)} %copy-done.34, s32[27]{0:T(128)S(1)} %get-tuple-element.70.gate_cols.cols, s32[27]{0:T(128)S(1)} %copy-done.33, s32[27]{0:T(128)S(1)} %get-tuple-element.71.up_cols, bf16[128,4096]{1,0:T(8,128)(2,1)S(1)} %copy-done.1, ...), custom_call_target="tpu_custom_call" | custom-call | tf_op jit(solution)/shard_map/sparse_forward/pallas_call | solution.py:386
  161.2 3.4 %hidden_and_up_grads.1 = (bf16[128,3584]{1,0:T(8,128)(2,1)}, bf16[128,3584]{1,0:T(8,128)(2,1)S(1)}, f32[2,27,16,128]{3,2,1,0:T(8,128)S(1)}, bf16[2,27,16,128]{3,...) custom-call(s32[6]{0:T(128)S(1)} %stack.27.idx, s32[27]{0:T(128)S(1)} %copy-done.33, ...), custom_call_target="tpu_custom_call" | custom-call | tf_op jit(solution)/shard_map/hidden_and_up_grads/pallas_call | solution.py:436
  164.6 3.6 %collective-permute-start.47 = (bf16[2,27,16,128]{3,2,1,0:T(8,128)(2,1)S(1)}, bf16[2,27,16,128]{3,2,1,0:T(8,128)(2,1)S(1)}, u32[]{:S(2)}, u32[]{:S(2)}) collective-permute-start(bf16[2,27,16,128]{3,2,1,0:T(8,128)(2,1)S(1)} %get-tuple-element.56), channel_id=1, source_target_pairs={{0,8},{1,9},{2,10},{3,11},{4,12},{5,13},{6,14},{7,15},{8,0},{9,1},... | collective-permute-start | bytes 663560 | tf_op jit(solution)/shard_map/ppermute | solution.py:318
  172.2 5.2 %collective-permute-done.47 = bf16[2,27,16,128]{3,2,1,0:T(8,128)(2,1)S(1)} collective-permute-done((bf16[2,27,16,128]{3,2,1,0:T(8,128)(2,1)S(1)}, bf16[2,27,16,128]{3,2,1,0:T(8,128)(2,1)S(1)}, u32[]{:S(2)}, u32[]{:S(2)}) %collective-permute-start.47) | collective-permute-done | bytes 221216 | tf_op jit(solution)/shard_map/ppermute | solution.py:318
  177.4 7.8 %collective-permute-done.48 = bf16[2,27,16,128]{3,2,1,0:T(8,128)(2,1)S(1)} collective-permute-done((bf16[2,27,16,128]{3,2,1,0:T(8,128)(2,1)S(1)}, bf16[2,27,16,128]{3,2,1,0:T(8,128)(2,1)S(1)}, u32[]{:S(2)}, u32[]{:S(2)}) %collective-permute-start.48) | collective-permute-done | bytes 221216 | tf_op jit(solution)/shard_map/ppermute | solution.py:318
  186.6 4.9 %collective-permute-start.44 = (bf16[27,16,128]{2,1,0:T(8,128)(2,1)S(1)}, bf16[27,16,128]{2,1,0:T(8,128)(2,1)S(1)}, u32[]{:S(2)}, u32[]{:S(2)}) collective-permute-start(bf16[27,16,128]{2,1,0:T(8,128)(2,1)S(1)} %get-tuple-element.52), channel_id=1, source_target_pairs={{0,8},{1,9},{2,10},{3,11},{4,12},{5,13},{6,14},{7,15},{8,0},{9,1},... | collective-permute-start | bytes 331784 | tf_op jit(solution)/shard_map/ppermute | solution.py:318
  191.5 2.4 %collective-permute-start.46 = (bf16[27,16,128]{2,1,0:T(8,128)(2,1)S(1)}, bf16[27,16,128]{2,1,0:T(8,128)(2,1)S(1)}, u32[]{:S(2)}, u32[]{:S(2)}) collective-permute-start(bf16[27,16,128]{2,1,0:T(8,128)(2,1)S(1)} %get-tuple-element.54), channel_id=1, source_target_pairs={{0,24},{1,25},{2,26},{3,27},{4,28},{5,29},{6,30},{7,31},{8,16},{9,... | collective-permute-start | bytes 331784 | tf_op jit(solution)/shard_map/ppermute | solution.py:318
  195.0 6.9 %collective-permute-done.45 = bf16[27,16,128]{2,1,0:T(8,128)(2,1)S(1)} collective-permute-done((bf16[27,16,128]{2,1,0:T(8,128)(2,1)S(1)}, bf16[27,16,128]{2,1,0:T(8,128)(2,1)S(1)}, u32[]{:S(2)}, u32[]{:S(2)}) %collective-permute-start.45) | collective-permute-done | bytes 110624 | tf_op jit(solution)/shard_map/ppermute | solution.py:318
  (178 shorter events, 59.4 us)
Async XLA Ops:
  7.4 13.0 %collective-permute-start.21 = (bf16[512,256]{1,0:T(8,128)(2,1)}, bf16[512,256]{1,0:T(8,128)(2,1)S(1)}, u32[]{:S(2)}, u32[]{:S(2)}) collective-permute-start(bf16[512,256]{1,0:T(8,128)(2,1)} %refs_12_.1), channel_id=1, source_target_pairs={{0,4},{1,5},{2,6},{3,7},{4,0},{5,1},{6,2},{7,3},{8,12},{9,13},{10,... | collective-permute-start | bytes 786440 | tf_op jit(solution)/shard_map/ppermute | solution.py:318
  9.1 11.6 %collective-permute-start.22 = (bf16[512,256]{1,0:T(8,128)(2,1)}, bf16[512,256]{1,0:T(8,128)(2,1)S(1)}, u32[]{:S(2)}, u32[]{:S(2)}) collective-permute-start(bf16[512,256]{1,0:T(8,128)(2,1)} %refs_13_.1), channel_id=1, source_target_pairs={{0,4},{1,5},{2,6},{3,7},{4,0},{5,1},{6,2},{7,3},{8,12},{9,13},{10,... | collective-permute-start | bytes 786440 | tf_op jit(solution)/shard_map/ppermute | solution.py:318
  25.9 13.3 %collective-permute-start.24 = (bf16[128,512]{1,0:T(8,128)(2,1)S(1)}, bf16[128,512]{1,0:T(8,128)(2,1)S(1)}, u32[]{:S(2)}, u32[]{:S(2)}) collective-permute-start(bf16[128,512]{1,0:T(8,128)(2,1)S(1)} %get-tuple-element.33), channel_id=1, source_target_pairs={{0,16},{1,17},{2,18},{3,19},{4,20},{5,21},{6,22},{7,23},{8,24},{9,... | collective-permute-start | bytes 393224 | tf_op jit(solution)/shard_map/ppermute | solution.py:318
  58.0 26.4 %collective-permute-start.27 = (bf16[8,128,256]{2,1,0:T(8,128)(2,1)S(1)}, bf16[8,128,256]{2,1,0:T(8,128)(2,1)S(1)}, u32[]{:S(2)}, u32[]{:S(2)}) collective-permute-start(bf16[8,128,256]{2,1,0:T(8,128)(2,1)S(1)} %all_to_all.5.refs_0_), channel_id=1, source_target_pairs={{0,2},{1,3},{2,0},{3,1},{4,6},{5,7},{6,4},{7,5},{8,10},{9,11},{10,... | collective-permute-start | bytes 1572872 | tf_op jit(solution)/shard_map/ppermute | solution.py:318
  58.3 10.8 %collective-permute-start.1 = (bf16[54,16,128]{2,1,0:T(8,128)(2,1)S(1)}, bf16[54,16,128]{2,1,0:T(8,128)(2,1)}, u32[]{:S(2)}, u32[]{:S(2)}) collective-permute-start(bf16[54,16,128]{2,1,0:T(8,128)(2,1)S(1)} %slice.12.refs_0_), channel_id=1, source_target_pairs={{0,8},{1,9},{2,10},{3,11},{4,12},{5,13},{6,14},{7,15},{8,0},{9,1},... | collective-permute-start | bytes 663560 | tf_op jit(solution)/shard_map/ppermute | solution.py:318
  62.0 22.4 %collective-permute-start.32 = (bf16[128,896]{1,0:T(8,128)(2,1)S(1)}, bf16[128,896]{1,0:T(8,128)(2,1)S(1)}, u32[]{:S(2)}, u32[]{:S(2)}) collective-permute-start(bf16[128,896]{1,0:T(8,128)(2,1)S(1)} %get-tuple-element.66), channel_id=1, source_target_pairs={{0,16},{1,17},{2,18},{3,19},{4,20},{5,21},{6,22},{7,23},{8,24},{9,... | collective-permute-start | bytes 688136 | tf_op jit(solution)/shard_map/ppermute | solution.py:318
  65.6 22.2 %collective-permute-start.33 = (bf16[128,896]{1,0:T(8,128)(2,1)}, bf16[128,896]{1,0:T(8,128)(2,1)S(1)}, u32[]{:S(2)}, u32[]{:S(2)}) collective-permute-start(bf16[128,896]{1,0:T(8,128)(2,1)} %get-tuple-element.65), channel_id=1, source_target_pairs={{0,20},{1,21},{2,22},{3,23},{4,16},{5,17},{6,18},{7,19},{8,28},{9,... | collective-permute-start | bytes 688136 | tf_op jit(solution)/shard_map/ppermute | solution.py:318
  69.0 18.8 %collective-permute-start.29 = (bf16[128,896]{1,0:T(8,128)(2,1)S(1)}, bf16[128,896]{1,0:T(8,128)(2,1)S(1)}, u32[]{:S(2)}, u32[]{:S(2)}) collective-permute-start(bf16[128,896]{1,0:T(8,128)(2,1)S(1)} %get-tuple-element.64), channel_id=1, source_target_pairs={{0,4},{1,5},{2,6},{3,7},{4,0},{5,1},{6,2},{7,3},{8,12},{9,13},{10,... | collective-permute-start | bytes 688136 | tf_op jit(solution)/shard_map/ppermute | solution.py:318
  69.6 20.0 %collective-permute-start.30 = (bf16[128,896]{1,0:T(8,128)(2,1)S(1)}, bf16[128,896]{1,0:T(8,128)(2,1)S(1)}, u32[]{:S(2)}, u32[]{:S(2)}) collective-permute-start(bf16[128,896]{1,0:T(8,128)(2,1)S(1)} %get-tuple-element.61), channel_id=1, source_target_pairs={{0,8},{1,9},{2,10},{3,11},{4,12},{5,13},{6,14},{7,15},{8,0},{9,1},... | collective-permute-start | bytes 688136 | tf_op jit(solution)/shard_map/ppermute | solution.py:318
  84.4 30.2 %collective-permute-start.26 = (bf16[8,128,256]{2,1,0:T(8,128)(2,1)S(1)}, bf16[8,128,256]{2,1,0:T(8,128)(2,1)S(1)}, u32[]{:S(2)}, u32[]{:S(2)}) collective-permute-start(bf16[8,128,256]{2,1,0:T(8,128)(2,1)S(1)} %all_to_all.5.refs_0_), channel_id=1, source_target_pairs={{0,1},{1,0},{2,3},{3,2},{4,5},{5,4},{6,7},{7,6},{8,9},{9,8},{10,11... | collective-permute-start | bytes 1572872 | tf_op jit(solution)/shard_map/ppermute | solution.py:318
  84.4 30.3 %collective-permute-start.28 = (bf16[8,128,256]{2,1,0:T(8,128)(2,1)S(1)}, bf16[8,128,256]{2,1,0:T(8,128)(2,1)S(1)}, u32[]{:S(2)}, u32[]{:S(2)}) collective-permute-start(bf16[8,128,256]{2,1,0:T(8,128)(2,1)S(1)} %collective-permute-done.27.refs_2_), channel_id=1, source_target_pairs={{0,1},{1,0},{2,3},{3,2},{4,5},{5,4},{6,7},{7,6},{8,9},{9,8},{10,11... | collective-permute-start | bytes 1572872 | tf_op jit(solution)/shard_map/ppermute | solution.py:318
  87.8 12.0 %collective-permute-start.6 = (bf16[54,16,128]{2,1,0:T(8,128)(2,1)}, bf16[54,16,128]{2,1,0:T(8,128)(2,1)}, u32[]{:S(2)}, u32[]{:S(2)}) collective-permute-start(bf16[54,16,128]{2,1,0:T(8,128)(2,1)} %collective-permute-done.1.refs_2_), channel_id=1, source_target_pairs={{8,16},{9,17},{10,18},{11,19},{12,20},{13,21},{14,22},{15,23},{16,... | collective-permute-start | bytes 663560 | tf_op jit(solution)/shard_map/ppermute | solution.py:318
  89.6 20.3 %collective-permute-start.4 = (bf16[54,16,128]{2,1,0:T(8,128)(2,1)}, bf16[54,16,128]{2,1,0:T(8,128)(2,1)}, u32[]{:S(2)}, u32[]{:S(2)}) collective-permute-start(bf16[54,16,128]{2,1,0:T(8,128)(2,1)} %copy-done.35), channel_id=1, source_target_pairs={{8,0},{9,1},{10,2},{11,3},{12,4},{13,5},{14,6},{15,7},{16,24},{17,... | collective-permute-start | bytes 663560 | tf_op jit(solution)/shard_map/ppermute | solution.py:318
  96.4 16.0 %collective-permute-start.34 = (bf16[128,896]{1,0:T(8,128)(2,1)}, bf16[128,896]{1,0:T(8,128)(2,1)S(1)}, u32[]{:S(2)}, u32[]{:S(2)}) collective-permute-start(bf16[128,896]{1,0:T(8,128)(2,1)} %get-tuple-element.60), channel_id=1, source_target_pairs={{0,24},{1,25},{2,26},{3,27},{4,28},{5,29},{6,30},{7,31},{8,16},{9,... | collective-permute-start | bytes 688136 | tf_op jit(solution)/shard_map/ppermute | solution.py:318
  99.8 20.7 %collective-permute-start.35 = (bf16[128,896]{1,0:T(8,128)(2,1)}, bf16[128,896]{1,0:T(8,128)(2,1)S(1)}, u32[]{:S(2)}, u32[]{:S(2)}) collective-permute-start(bf16[128,896]{1,0:T(8,128)(2,1)} %get-tuple-element.59), channel_id=1, source_target_pairs={{0,28},{1,29},{2,30},{3,31},{4,24},{5,25},{6,26},{7,27},{8,20},{9,... | collective-permute-start | bytes 688136 | tf_op jit(solution)/shard_map/ppermute | solution.py:318
  110.0 13.6 %collective-permute-start.7 = (bf16[54,16,128]{2,1,0:T(8,128)(2,1)}, bf16[54,16,128]{2,1,0:T(8,128)(2,1)S(1)}, u32[]{:S(2)}, u32[]{:S(2)}) collective-permute-start(bf16[54,16,128]{2,1,0:T(8,128)(2,1)} %collective-permute-done.6), channel_id=1, source_target_pairs={{8,0},{9,1},{10,2},{11,3},{12,4},{13,5},{14,6},{15,7},{16,24},{17,... | collective-permute-start | bytes 663560 | tf_op jit(solution)/shard_map/ppermute | solution.py:318
  112.4 11.7 %collective-permute-start = (bf16[54,16,128]{2,1,0:T(8,128)(2,1)}, bf16[54,16,128]{2,1,0:T(8,128)(2,1)S(1)}, u32[]{:S(2)}, u32[]{:S(2)}) collective-permute-start(bf16[54,16,128]{2,1,0:T(8,128)(2,1)} %copy-done.11), channel_id=1, source_target_pairs={{0,4},{1,5},{2,6},{3,7},{4,0},{5,1},{6,2},{7,3},{8,12},{9,13},{10,... | collective-permute-start | bytes 663560 | tf_op jit(solution)/shard_map/ppermute | solution.py:318
  114.6 20.0 %collective-permute-start.2 = (bf16[54,16,128]{2,1,0:T(8,128)(2,1)}, bf16[54,16,128]{2,1,0:T(8,128)(2,1)S(1)}, u32[]{:S(2)}, u32[]{:S(2)}) collective-permute-start(bf16[54,16,128]{2,1,0:T(8,128)(2,1)} %collective-permute-done.1.refs_2_), channel_id=1, source_target_pairs={{0,4},{1,5},{2,6},{3,7},{4,0},{5,1},{6,2},{7,3},{8,12},{9,13},{10,... | collective-permute-start | bytes 663560 | tf_op jit(solution)/shard_map/ppermute | solution.py:318
  114.7 22.7 %collective-permute-start.5 = (bf16[54,16,128]{2,1,0:T(8,128)(2,1)S(1)}, bf16[54,16,128]{2,1,0:T(8,128)(2,1)S(1)}, u32[]{:S(2)}, u32[]{:S(2)}) collective-permute-start(bf16[54,16,128]{2,1,0:T(8,128)(2,1)S(1)} %broadcast_select_fusion.9.refs_4_), channel_id=1, source_target_pairs={{0,4},{1,5},{2,6},{3,7},{4,0},{5,1},{6,2},{7,3},{8,12},{9,13},{10,... | collective-permute-start | bytes 663560 | tf_op jit(solution)/shard_map/ppermute | solution.py:318
  121.7 20.3 %collective-permute-start.39 = (bf16[128,896]{1,0:T(8,128)(2,1)S(1)}, bf16[128,896]{1,0:T(8,128)(2,1)S(1)}, u32[]{:S(2)}, u32[]{:S(2)}) collective-permute-start(bf16[128,896]{1,0:T(8,128)(2,1)S(1)} %get-tuple-element.43), channel_id=1, source_target_pairs={{0,16},{1,17},{2,18},{3,19},{4,20},{5,21},{6,22},{7,23},{8,24},{9,... | collective-permute-start | bytes 688136 | tf_op jit(solution)/shard_map/ppermute | solution.py:318
  123.6 26.9 %collective-permute-start.40 = (bf16[128,896]{1,0:T(8,128)(2,1)S(1)}, bf16[128,896]{1,0:T(8,128)(2,1)S(1)}, u32[]{:S(2)}, u32[]{:S(2)}) collective-permute-start(bf16[128,896]{1,0:T(8,128)(2,1)S(1)} %get-tuple-element.44), channel_id=1, source_target_pairs={{0,20},{1,21},{2,22},{3,23},{4,16},{5,17},{6,18},{7,19},{8,28},{9,... | collective-permute-start | bytes 688136 | tf_op jit(solution)/shard_map/ppermute | solution.py:318
  124.9 14.4 %collective-permute-start.8 = (bf16[54,16,128]{2,1,0:T(8,128)(2,1)S(1)}, bf16[54,16,128]{2,1,0:T(8,128)(2,1)S(1)}, u32[]{:S(2)}, u32[]{:S(2)}) collective-permute-start(bf16[54,16,128]{2,1,0:T(8,128)(2,1)S(1)} %broadcast_select_fusion.8.refs_6_), channel_id=1, source_target_pairs={{0,4},{1,5},{2,6},{3,7},{4,0},{5,1},{6,2},{7,3},{8,12},{9,13},{10,... | collective-permute-start | bytes 663560 | tf_op jit(solution)/shard_map/ppermute | solution.py:318
  135.3 25.8 %collective-permute-start.41 = (bf16[128,896]{1,0:T(8,128)(2,1)}, bf16[128,896]{1,0:T(8,128)(2,1)S(1)}, u32[]{:S(2)}, u32[]{:S(2)}) collective-permute-start(bf16[128,896]{1,0:T(8,128)(2,1)} %get-tuple-element.45), channel_id=1, source_target_pairs={{0,24},{1,25},{2,26},{3,27},{4,28},{5,29},{6,30},{7,31},{8,16},{9,... | collective-permute-start | bytes 688136 | tf_op jit(solution)/shard_map/ppermute | solution.py:318
  138.1 23.0 %collective-permute-start.42 = (bf16[128,896]{1,0:T(8,128)(2,1)}, bf16[128,896]{1,0:T(8,128)(2,1)S(1)}, u32[]{:S(2)}, u32[]{:S(2)}) collective-permute-start(bf16[128,896]{1,0:T(8,128)(2,1)} %get-tuple-element.46), channel_id=1, source_target_pairs={{0,28},{1,29},{2,30},{3,31},{4,24},{5,25},{6,26},{7,27},{8,20},{9,... | collective-permute-start | bytes 688136 | tf_op jit(solution)/shard_map/ppermute | solution.py:318
  140.0 21.1 %collective-permute-start.36 = (bf16[128,896]{1,0:T(8,128)(2,1)}, bf16[128,896]{1,0:T(8,128)(2,1)S(1)}, u32[]{:S(2)}, u32[]{:S(2)}) collective-permute-start(bf16[128,896]{1,0:T(8,128)(2,1)} %get-tuple-element.38), channel_id=1, source_target_pairs={{0,4},{1,5},{2,6},{3,7},{4,0},{5,1},{6,2},{7,3},{8,12},{9,13},{10,... | collective-permute-start | bytes 688136 | tf_op jit(solution)/shard_map/ppermute | solution.py:318
  142.7 18.5 %collective-permute-start.37 = (bf16[128,896]{1,0:T(8,128)(2,1)}, bf16[128,896]{1,0:T(8,128)(2,1)S(1)}, u32[]{:S(2)}, u32[]{:S(2)}) collective-permute-start(bf16[128,896]{1,0:T(8,128)(2,1)} %get-tuple-element.39), channel_id=1, source_target_pairs={{0,8},{1,9},{2,10},{3,11},{4,12},{5,13},{6,14},{7,15},{8,0},{9,1},... | collective-permute-start | bytes 688136 | tf_op jit(solution)/shard_map/ppermute | solution.py:318
  164.6 12.8 %collective-permute-start.47 = (bf16[2,27,16,128]{3,2,1,0:T(8,128)(2,1)S(1)}, bf16[2,27,16,128]{3,2,1,0:T(8,128)(2,1)S(1)}, u32[]{:S(2)}, u32[]{:S(2)}) collective-permute-start(bf16[2,27,16,128]{3,2,1,0:T(8,128)(2,1)S(1)} %get-tuple-element.56), channel_id=1, source_target_pairs={{0,8},{1,9},{2,10},{3,11},{4,12},{5,13},{6,14},{7,15},{8,0},{9,1},... | collective-permute-start | bytes 663560 | tf_op jit(solution)/shard_map/ppermute | solution.py:318
  168.2 17.0 %collective-permute-start.48 = (bf16[2,27,16,128]{3,2,1,0:T(8,128)(2,1)S(1)}, bf16[2,27,16,128]{3,2,1,0:T(8,128)(2,1)S(1)}, u32[]{:S(2)}, u32[]{:S(2)}) collective-permute-start(bf16[2,27,16,128]{3,2,1,0:T(8,128)(2,1)S(1)} %get-tuple-element.57), channel_id=1, source_target_pairs={{0,16},{1,17},{2,18},{3,19},{4,20},{5,21},{6,22},{7,23},{8,24},{9,... | collective-permute-start | bytes 663560 | tf_op jit(solution)/shard_map/ppermute | solution.py:318
  169.2 16.0 %collective-permute-start.49 = (bf16[2,27,16,128]{3,2,1,0:T(8,128)(2,1)S(1)}, bf16[2,27,16,128]{3,2,1,0:T(8,128)(2,1)S(1)}, u32[]{:S(2)}, u32[]{:S(2)}) collective-permute-start(bf16[2,27,16,128]{3,2,1,0:T(8,128)(2,1)S(1)} %get-tuple-element.58), channel_id=1, source_target_pairs={{0,24},{1,25},{2,26},{3,27},{4,28},{5,29},{6,30},{7,31},{8,16},{9,... | collective-permute-start | bytes 663560 | tf_op jit(solution)/shard_map/ppermute | solution.py:318
  171.8 14.7 %collective-permute-start.43 = (bf16[4,27,16,128]{3,2,1,0:T(8,128)(2,1)S(1)}, bf16[4,27,16,128]{3,2,1,0:T(8,128)(2,1)S(1)}, u32[]{:S(2)}, u32[]{:S(2)}) collective-permute-start(bf16[4,27,16,128]{3,2,1,0:T(8,128)(2,1)S(1)} %get-tuple-element.50), channel_id=1, source_target_pairs={{0,4},{1,5},{2,6},{3,7},{4,0},{5,1},{6,2},{7,3},{8,12},{9,13},{10,... | collective-permute-start | bytes 1327112 | tf_op jit(solution)/shard_map/ppermute | solution.py:318
  191.5 10.4 %collective-permute-start.45 = (bf16[27,16,128]{2,1,0:T(8,128)(2,1)S(1)}, bf16[27,16,128]{2,1,0:T(8,128)(2,1)S(1)}, u32[]{:S(2)}, u32[]{:S(2)}) collective-permute-start(bf16[27,16,128]{2,1,0:T(8,128)(2,1)S(1)} %get-tuple-element.53), channel_id=1, source_target_pairs={{0,16},{1,17},{2,18},{3,19},{4,20},{5,21},{6,22},{7,23},{8,24},{9,... | collective-permute-start | bytes 331784 | tf_op jit(solution)/shard_map/ppermute | solution.py:318
  191.5 10.4 %collective-permute-start.46 = (bf16[27,16,128]{2,1,0:T(8,128)(2,1)S(1)}, bf16[27,16,128]{2,1,0:T(8,128)(2,1)S(1)}, u32[]{:S(2)}, u32[]{:S(2)}) collective-permute-start(bf16[27,16,128]{2,1,0:T(8,128)(2,1)S(1)} %get-tuple-element.54), channel_id=1, source_target_pairs={{0,24},{1,25},{2,26},{3,27},{4,28},{5,29},{6,30},{7,31},{8,16},{9,... | collective-permute-start | bytes 331784 | tf_op jit(solution)/shard_map/ppermute | solution.py:318
  (59 other events, 552.1 us)

commit v5 on v4

--- a/solution.py
+++ b/solution.py
@@ -94,6 +94,7 @@
 
 ANY = pl.BlockSpec(memory_space=pl.ANY)
 VMEM = pl.BlockSpec(memory_space=pltpu.VMEM)
+HBM = pl.BlockSpec(memory_space=pltpu.HBM)
 SMEM = pl.BlockSpec(memory_space=pltpu.SMEM)
 BF16, F32 = jnp.bfloat16, jnp.float32
 AXES = ("z", "x", "y", "c")
@@ -118,17 +119,23 @@
     n = nz - 1
     quarters, (left_g, left_u, recv_g, recv_u) = refs[: 4 * n], refs[4 * n : 4 * nz]
     own_out, outs = refs[4 * nz], refs[4 * nz + 1 : 5 * nz]
-    left, toks = refs[5 * nz :]
+    left, toks, sems = refs[5 * nz :]
     z, x, c, y = idx[0], idx[1], idx[2], idx[5]
     depth, width = left_g.shape
-    left[x, :, :width], left[x, :, width:] = left_g[...], left_u[...]
+    pairs = [
+        (left_g, left.at[x, :, pl.ds(0, width)]),
+        (left_u, left.at[x, :, pl.ds(width, width)]),
+        (tokens.at[:, at(z * 2 * depth, 2 * depth)], toks.at[0]),
+    ]
+    copies = run_copies(pairs, sems)
     left[1 - x, :, :width], left[1 - x, :, width:] = recv_g[...], recv_u[...]
-    toks[0] = tokens[:, at(z * 2 * depth, 2 * depth)]
     quarter = depth // 2
     for i, (dc, dy) in enumerate(((0, 0), (0, 1), (1, 0), (1, 1))):
         start = (c ^ dc) * depth + (y ^ dy) * quarter
         for j in range(1, nz):
             toks[j, :, at(start, quarter)] = quarters[i * n + j - 1][...]
+    for copy in copies:
+        copy.wait()
     weights = left[...].reshape(2 * depth, 2 * width)
     rows = toks.shape[1]
     total = jnp.dot(
@@ -333,11 +340,12 @@
         functools.partial(partial_kernel, nz),
         out_shape=[jax.ShapeDtypeStruct((rows, 2 * slice_width), F32)]
         + [jax.ShapeDtypeStruct((rows, 2 * slice_width), BF16)] * (nz - 1),
-        in_specs=[SMEM] + [VMEM] * (4 * nz + 1),
+        in_specs=[SMEM, HBM] + [VMEM] * (4 * nz - 4) + [HBM] * 2 + [VMEM] * 2,
         out_specs=[VMEM] * nz,
         scratch_shapes=[
             pltpu.VMEM((2, depth, 2 * slice_width), BF16),
             pltpu.VMEM((nz, rows, 2 * depth), BF16),
+            pltpu.SemaphoreType.DMA((3,)),
         ],
         name="rank_partial",
             compiler_params=grant(10),
@@ -393,7 +401,7 @@
             pltpu.SemaphoreType.DMA((nf,)),
         ],
         name="sparse_forward",
-        compiler_params=grant(14),
+        compiler_params=grant(10),
     )(*index, tokens, *values)
 
     depth_k, far, near_slots = gate_right.shape[0], range(nf // 2, nf), range(nf // 2)
@@ -409,7 +417,7 @@
         out_specs=[VMEM] * 2,
         scratch_shapes=scratch,
         name="lf28",
-        compiler_params=grant(14),
+        compiler_params=grant(9),
     )(idx, *ranks, *rights[:-1])
     far_products = pl.pallas_call(
         lowrank_last_kernel,
@@ -417,7 +425,7 @@
         in_specs=[VMEM] * 3,
         out_specs=[VMEM] * (nf // 2),
         name="lowrank_last",
-            compiler_params=grant(10),
+            compiler_params=grant(6),
     )(first, columns, rights[-1])
     near_products = pl.pallas_call(
         functools.partial(lowrank_kernel, nf, nt, near_slots),
@@ -426,7 +434,7 @@
         out_specs=[VMEM] * (nf // 2),
         scratch_shapes=scratch,
         name="lowrank_near",
-            compiler_params=grant(14),
+            compiler_params=grant(9),
     )(idx, *ranks, *rights)
     pieces = [near_products[0]]
     pieces += [move(near_products[k], df=k) for k in near_slots[1:]]
@@ -449,7 +457,7 @@
             pltpu.VMEM((nz, 2) + support, BF16),
         ],
         name="hidden_and_up_grads",
-            compiler_params=grant(24),
+            compiler_params=grant(16),
     )(idx, up_rows, up_cols - base, tokens, grad_hidden, sparse, *pieces)
     hidden, dpre_gate, up_keep, *up_sends = outs
     gate_keep, gate_send = pl.pallas_call(
@@ -461,7 +469,7 @@
         in_specs=[SMEM] * 3 + [VMEM] * 2,
         out_specs=[VMEM] * 2,
         name="gg27",
-        compiler_params=grant(10),
+        compiler_params=grant(8),
     )(idx, gate_rows, gate_cols - base, tokens, dpre_gate)
 
     up_sum = up_keep

time: 204 us -> 204 us (level)
  waiting for transfers between devices: 62.4 us -> 66 us
  starting transfers between devices: 76.7 us -> 73.9 us
    ppermute x51, waiting for transfers between devices: 62.4 us -> 66 us  [move(): return lax.ppermute(value, AXES, pairs)]
    ppermute x51, starting transfers between devices: 76.7 us -> 73.9 us  [move(): return lax.ppermute(value, AXES, pairs)]
  transfers between devices with their start and end apart: 51 -> 51, of which waited for: 19 -> 20; matrix products, arithmetic and copies ran while one was open for 3% -> 3% of each run, Pallas kernels for 5% -> 5%
where the time goes in v5:
time: 204 us; the launch traced here: 203 us
  starting transfers between devices  73.9 us (36%)
  waiting for transfers between devices  66 us (32%)
  local copies, waits for them, and re-layouts  21.7 us (11%)
  blocking collectives  18.6 us (9%)
  Pallas kernels  15.8 us (8%)
  other arithmetic  5.67 us (3%)
    ppermute x51, starting transfers between devices, move(): return lax.ppermute(value, AXES, pairs)  73.9 us
    ppermute x51, waiting for transfers between devices, move(): return lax.ppermute(value, AXES, pairs)  66 us
    unnamed x85, local copies, waits for them, and re-layouts  20.7 us
    all_to_all x1, blocking collectives, exchange_device(): stack = lax.all_to_all(for_f, ('z', 'x'), 0, 0, tiled=True)  18.6 us
    select_n x2, other arithmetic, exchange_device(): jnp.where(x ^ k % 2 == 0, lax.dynamic_slice(gate_k, start, size), lax.dyn...  4.38 us
  transfers between devices with their start and end apart: 51, of which 20 were waited for; matrix products, arithmetic and copies ran while one was open for 3% of the time, Pallas kernels for 5%

profile of v5, /device:TPU:0, one launch (start us, length us, event | category | flops | bytes accessed | tf_op | source)
XLA Modules:
  0.0 202.8 jit_solution(11038863757656620142)
XLA Ops:
  1.7 3.1 %collective-permute-start.9 = (bf16[128,256]{1,0:T(8,128)(2,1)S(1)}, bf16[128,256]{1,0:T(8,128)(2,1)S(1)}, u32[]{:S(2)}, u32[]{:S(2)}) collective-permute-start(bf16[128,256]{1,0:T(8,128)(2,1)S(1)} %get-tuple-element.69), channel_id=1, source_target_pairs={{0,8},{1,9},{2,10},{3,11},{4,12},{5,13},{6,14},{7,15},{8,0},{9,1},... | collective-permute-start | bytes 196616 | tf_op jit(solution)/shard_map/ppermute | solution.py:325
  4.8 2.6 %collective-permute-start.10 = (bf16[128,256]{1,0:T(8,128)(2,1)S(1)}, bf16[128,256]{1,0:T(8,128)(2,1)S(1)}, u32[]{:S(2)}, u32[]{:S(2)}) collective-permute-start(bf16[128,256]{1,0:T(8,128)(2,1)S(1)} %get-tuple-element.68), channel_id=1, source_target_pairs={{0,16},{1,17},{2,18},{3,19},{4,20},{5,21},{6,22},{7,23},{8,24},{9,... | collective-permute-start | bytes 196616 | tf_op jit(solution)/shard_map/ppermute | solution.py:325
  26.0 3.5 %collective-permute-start.24 = (bf16[128,512]{1,0:T(8,128)(2,1)S(1)}, bf16[128,512]{1,0:T(8,128)(2,1)S(1)}, u32[]{:S(2)}, u32[]{:S(2)}) collective-permute-start(bf16[128,512]{1,0:T(8,128)(2,1)S(1)} %get-tuple-element.33), channel_id=1, source_target_pairs={{0,16},{1,17},{2,18},{3,19},{4,20},{5,21},{6,22},{7,23},{8,24},{9,... | collective-permute-start | bytes 393224 | tf_op jit(solution)/shard_map/ppermute | solution.py:325
  29.8 2.6 %collective-permute-done.23.refs_0_ = bf16[128,512]{1,0:T(8,128)(2,1)S(1)} collective-permute-done((bf16[128,512]{1,0:T(8,128)(2,1)S(1)}, bf16[128,512]{1,0:T(8,128)(2,1)S(1)}, u32[]{:S(2)}, u32[]{:S(2)}) %collective-permute-start.23) | collective-permute-done | bytes 131104 | tf_op jit(solution)/shard_map/ppermute | solution.py:325
  32.3 7.0 %collective-permute-done.24.refs_1_ = bf16[128,512]{1,0:T(8,128)(2,1)S(1)} collective-permute-done((bf16[128,512]{1,0:T(8,128)(2,1)S(1)}, bf16[128,512]{1,0:T(8,128)(2,1)S(1)}, u32[]{:S(2)}, u32[]{:S(2)}) %collective-permute-start.24) | collective-permute-done | bytes 131104 | tf_op jit(solution)/shard_map/ppermute | solution.py:325
  39.4 18.6 %all_to_all.5.refs_0_ = bf16[8,128,256]{2,1,0:T(8,128)(2,1)S(1)} all-to-all(bf16[8,128,256]{2,1,0:T(8,128)(2,1)S(1)} %rr11.1), channel_id=1, replica_groups=mesh['z'=4,'x'=2,'y'=2,'c'=2] {'z','x'}, dimensions={0} | all-to-all | bytes 1048576 | tf_op jit(solution)/shard_map/all_to_all | solution.py:362
  62.0 3.6 %collective-permute-start.32 = (bf16[128,896]{1,0:T(8,128)(2,1)S(1)}, bf16[128,896]{1,0:T(8,128)(2,1)S(1)}, u32[]{:S(2)}, u32[]{:S(2)}) collective-permute-start(bf16[128,896]{1,0:T(8,128)(2,1)S(1)} %get-tuple-element.66), channel_id=1, source_target_pairs={{0,16},{1,17},{2,18},{3,19},{4,20},{5,21},{6,22},{7,23},{8,24},{9,... | collective-permute-start | bytes 688136 | tf_op jit(solution)/shard_map/ppermute | solution.py:325
  66.5 2.6 %broadcast_select_fusion = (bf16[128,896]{1,0:T(8,128)(2,1)}, bf16[128,896]{1,0:T(8,128)(2,1)}, bf16[128,896]{1,0:T(8,128)(2,1)S(1)}, bf16[128,896]{1,0:T(8,128)...) fusion(pred[]{:T(512)S(6)} %eq.11, bf16[128,3584]{1,0:T(8,128)(2,1)} %param.19, s32[]{:T(128)S(6)} %select_n.116, ...), kind=kLoop, calls=%fused_computation.2 | loop fusion | flops 688128 | bytes 2752526 | tf_op jit(solution)/shard_map/jit(_where)/select_n | solution.py:373
  69.7 10.8 %collective-permute-start.30 = (bf16[128,896]{1,0:T(8,128)(2,1)S(1)}, bf16[128,896]{1,0:T(8,128)(2,1)S(1)}, u32[]{:S(2)}, u32[]{:S(2)}) collective-permute-start(bf16[128,896]{1,0:T(8,128)(2,1)S(1)} %get-tuple-element.61), channel_id=1, source_target_pairs={{0,8},{1,9},{2,10},{3,11},{4,12},{5,13},{6,14},{7,15},{8,0},{9,1},... | collective-permute-start | bytes 688136 | tf_op jit(solution)/shard_map/ppermute | solution.py:325
  80.5 4.0 %collective-permute-done.32.refs_8_ = bf16[128,896]{1,0:T(8,128)(2,1)S(1)} collective-permute-done((bf16[128,896]{1,0:T(8,128)(2,1)S(1)}, bf16[128,896]{1,0:T(8,128)(2,1)S(1)}, u32[]{:S(2)}, u32[]{:S(2)}) %collective-permute-start.32) | collective-permute-done | bytes 229408 | tf_op jit(solution)/shard_map/ppermute | solution.py:325
  85.0 2.9 %collective-permute-done.33.refs_9_ = bf16[128,896]{1,0:T(8,128)(2,1)S(1)} collective-permute-done((bf16[128,896]{1,0:T(8,128)(2,1)}, bf16[128,896]{1,0:T(8,128)(2,1)S(1)}, u32[]{:S(2)}, u32[]{:S(2)}) %collective-permute-start.33) | collective-permute-done | bytes 229408 | tf_op jit(solution)/shard_map/ppermute | solution.py:325
  91.0 5.4 %collective-permute-done.31.refs_7_ = bf16[128,896]{1,0:T(8,128)(2,1)} collective-permute-done((bf16[128,896]{1,0:T(8,128)(2,1)}, bf16[128,896]{1,0:T(8,128)(2,1)}, u32[]{:S(2)}, u32[]{:S(2)}) %collective-permute-start.31) | collective-permute-done | bytes 229408 | tf_op jit(solution)/shard_map/ppermute | solution.py:325
  96.4 3.4 %collective-permute-start.34 = (bf16[128,896]{1,0:T(8,128)(2,1)}, bf16[128,896]{1,0:T(8,128)(2,1)S(1)}, u32[]{:S(2)}, u32[]{:S(2)}) collective-permute-start(bf16[128,896]{1,0:T(8,128)(2,1)} %get-tuple-element.60), channel_id=1, source_target_pairs={{0,24},{1,25},{2,26},{3,27},{4,28},{5,29},{6,30},{7,31},{8,16},{9,... | collective-permute-start | bytes 688136 | tf_op jit(solution)/shard_map/ppermute | solution.py:325
  100.4 9.6 %collective-permute-done.4 = bf16[54,16,128]{2,1,0:T(8,128)(2,1)} collective-permute-done((bf16[54,16,128]{2,1,0:T(8,128)(2,1)}, bf16[54,16,128]{2,1,0:T(8,128)(2,1)}, u32[]{:S(2)}, u32[]{:S(2)}) %collective-permute-start.4) | collective-permute-done | bytes 221216 | tf_op jit(solution)/shard_map/ppermute | solution.py:325
  112.5 2.2 %collective-permute-start = (bf16[54,16,128]{2,1,0:T(8,128)(2,1)}, bf16[54,16,128]{2,1,0:T(8,128)(2,1)S(1)}, u32[]{:S(2)}, u32[]{:S(2)}) collective-permute-start(bf16[54,16,128]{2,1,0:T(8,128)(2,1)} %copy-done.11), channel_id=1, source_target_pairs={{0,4},{1,5},{2,6},{3,7},{4,0},{5,1},{6,2},{7,3},{8,12},{9,13},{10,... | collective-permute-start | bytes 663560 | tf_op jit(solution)/shard_map/ppermute | solution.py:325
  114.8 1.9 collective-permute-start.5
  116.7 2.5 %lf28.1 = (f32[512,896]{1,0:T(8,128)S(1)}, bf16[512,128]{1,0:T(8,128)(2,1)S(1)}) custom-call(s32[6]{0:T(128)S(1)} %stack.27.idx, bf16[8,128,256]{2,1,0:T(8,128)(2,1)S(1)} %all_to_all.5.refs_0_, bf16[8,128,256]{2,1,0:T(8,128)(2,1)S(1)} %collective-permute-done.26.refs_1_, bf16[8,128,256]{2,1,0:T(8,128)(2,1)S(1)} %collective-permute-done.27.refs_2_, ...), custom_call_target="tpu_custom_call" | custom-call | tf_op jit(solution)/shard_map/lf28/pallas_call | solution.py:410
  121.7 1.9 collective-permute-start.39
  124.2 2.0 collective-permute-start.8
  130.0 3.3 %lowrank_near.1 = (bf16[128,896]{1,0:T(8,128)(2,1)S(1)}, bf16[128,896]{1,0:T(8,128)(2,1)}, bf16[128,896]{1,0:T(8,128)(2,1)}, bf16[128,896]{1,0:T(8,128)(2,1)}) custom-call(s32[6]{0:T(128)S(1)} %stack.27.idx, bf16[8,128,256]{2,1,0:T(8,128)(2,1)S(1)} %all_to_all.5.refs_0_, bf16[8,128,256]{2,1,0:T(8,128)(2,1)S(1)} %collective-permute-done.26.refs_1_, ...), custom_call_target="tpu_custom_call" | custom-call | tf_op jit(solution)/shard_map/lowrank_near/pallas_call | solution.py:430
  134.7 2.1 %collective-permute-start.41 = (bf16[128,896]{1,0:T(8,128)(2,1)}, bf16[128,896]{1,0:T(8,128)(2,1)S(1)}, u32[]{:S(2)}, u32[]{:S(2)}) collective-permute-start(bf16[128,896]{1,0:T(8,128)(2,1)} %get-tuple-element.45), channel_id=1, source_target_pairs={{0,24},{1,25},{2,26},{3,27},{4,28},{5,29},{6,30},{7,31},{8,16},{9,... | collective-permute-start | bytes 688136 | tf_op jit(solution)/shard_map/ppermute | solution.py:325
  139.4 2.0 collective-permute-start.36
  141.4 4.6 %collective-permute-done.39.refs_4_ = bf16[128,896]{1,0:T(8,128)(2,1)S(1)} collective-permute-done((bf16[128,896]{1,0:T(8,128)(2,1)S(1)}, bf16[128,896]{1,0:T(8,128)(2,1)S(1)}, u32[]{:S(2)}, u32[]{:S(2)}) %collective-permute-start.39) | collective-permute-done | bytes 229408 | tf_op jit(solution)/shard_map/ppermute | solution.py:325
  147.1 3.5 %collective-permute-done.40.refs_5_ = bf16[128,896]{1,0:T(8,128)(2,1)S(1)} collective-permute-done((bf16[128,896]{1,0:T(8,128)(2,1)S(1)}, bf16[128,896]{1,0:T(8,128)(2,1)S(1)}, u32[]{:S(2)}, u32[]{:S(2)}) %collective-permute-start.40) | collective-permute-done | bytes 229408 | tf_op jit(solution)/shard_map/ppermute | solution.py:325
  158.4 2.7 %sparse_forward.1.sparse = f32[2,128,3584]{2,1,0:T(8,128)S(1)} custom-call(s32[6]{0:T(128)S(1)} %stack.27.idx, s32[27]{0:T(128)S(1)} %copy-done.34, s32[27]{0:T(128)S(1)} %get-tuple-element.70.gate_cols.cols, s32[27]{0:T(128)S(1)} %copy-done.33, s32[27]{0:T(128)S(1)} %get-tuple-element.71.up_cols, bf16[128,4096]{1,0:T(8,128)(2,1)S(1)} %copy-done.1, ...), custom_call_target="tpu_custom_call" | custom-call | tf_op jit(solution)/shard_map/sparse_forward/pallas_call | solution.py:394
  161.3 3.4 %hidden_and_up_grads.1 = (bf16[128,3584]{1,0:T(8,128)(2,1)}, bf16[128,3584]{1,0:T(8,128)(2,1)S(1)}, f32[2,27,16,128]{3,2,1,0:T(8,128)S(1)}, bf16[2,27,16,128]{3,...) custom-call(s32[6]{0:T(128)S(1)} %stack.27.idx, s32[27]{0:T(128)S(1)} %copy-done.33, ...), custom_call_target="tpu_custom_call" | custom-call | tf_op jit(solution)/shard_map/hidden_and_up_grads/pallas_call | solution.py:444
  164.7 3.6 %collective-permute-start.47 = (bf16[2,27,16,128]{3,2,1,0:T(8,128)(2,1)S(1)}, bf16[2,27,16,128]{3,2,1,0:T(8,128)(2,1)S(1)}, u32[]{:S(2)}, u32[]{:S(2)}) collective-permute-start(bf16[2,27,16,128]{3,2,1,0:T(8,128)(2,1)S(1)} %get-tuple-element.56), channel_id=1, source_target_pairs={{0,8},{1,9},{2,10},{3,11},{4,12},{5,13},{6,14},{7,15},{8,0},{9,1},... | collective-permute-start | bytes 663560 | tf_op jit(solution)/shard_map/ppermute | solution.py:325
  172.3 5.2 %collective-permute-done.47 = bf16[2,27,16,128]{3,2,1,0:T(8,128)(2,1)S(1)} collective-permute-done((bf16[2,27,16,128]{3,2,1,0:T(8,128)(2,1)S(1)}, bf16[2,27,16,128]{3,2,1,0:T(8,128)(2,1)S(1)}, u32[]{:S(2)}, u32[]{:S(2)}) %collective-permute-start.47) | collective-permute-done | bytes 221216 | tf_op jit(solution)/shard_map/ppermute | solution.py:325
  177.5 7.8 %collective-permute-done.48 = bf16[2,27,16,128]{3,2,1,0:T(8,128)(2,1)S(1)} collective-permute-done((bf16[2,27,16,128]{3,2,1,0:T(8,128)(2,1)S(1)}, bf16[2,27,16,128]{3,2,1,0:T(8,128)(2,1)S(1)}, u32[]{:S(2)}, u32[]{:S(2)}) %collective-permute-start.48) | collective-permute-done | bytes 221216 | tf_op jit(solution)/shard_map/ppermute | solution.py:325
  186.6 4.9 %collective-permute-start.44 = (bf16[27,16,128]{2,1,0:T(8,128)(2,1)S(1)}, bf16[27,16,128]{2,1,0:T(8,128)(2,1)S(1)}, u32[]{:S(2)}, u32[]{:S(2)}) collective-permute-start(bf16[27,16,128]{2,1,0:T(8,128)(2,1)S(1)} %get-tuple-element.52), channel_id=1, source_target_pairs={{0,8},{1,9},{2,10},{3,11},{4,12},{5,13},{6,14},{7,15},{8,0},{9,1},... | collective-permute-start | bytes 331784 | tf_op jit(solution)/shard_map/ppermute | solution.py:325
  191.5 2.4 %collective-permute-start.46 = (bf16[27,16,128]{2,1,0:T(8,128)(2,1)S(1)}, bf16[27,16,128]{2,1,0:T(8,128)(2,1)S(1)}, u32[]{:S(2)}, u32[]{:S(2)}) collective-permute-start(bf16[27,16,128]{2,1,0:T(8,128)(2,1)S(1)} %get-tuple-element.54), channel_id=1, source_target_pairs={{0,24},{1,25},{2,26},{3,27},{4,28},{5,29},{6,30},{7,31},{8,16},{9,... | collective-permute-start | bytes 331784 | tf_op jit(solution)/shard_map/ppermute | solution.py:325
  195.0 6.9 %collective-permute-done.45 = bf16[27,16,128]{2,1,0:T(8,128)(2,1)S(1)} collective-permute-done((bf16[27,16,128]{2,1,0:T(8,128)(2,1)S(1)}, bf16[27,16,128]{2,1,0:T(8,128)(2,1)S(1)}, u32[]{:S(2)}, u32[]{:S(2)}) %collective-permute-start.45) | collective-permute-done | bytes 110624 | tf_op jit(solution)/shard_map/ppermute | solution.py:325
  (178 shorter events, 59.1 us)
Async XLA Ops:
  7.4 13.0 %collective-permute-start.21 = (bf16[512,256]{1,0:T(8,128)(2,1)}, bf16[512,256]{1,0:T(8,128)(2,1)S(1)}, u32[]{:S(2)}, u32[]{:S(2)}) collective-permute-start(bf16[512,256]{1,0:T(8,128)(2,1)} %refs_12_.1), channel_id=1, source_target_pairs={{0,4},{1,5},{2,6},{3,7},{4,0},{5,1},{6,2},{7,3},{8,12},{9,13},{10,... | collective-permute-start | bytes 786440 | tf_op jit(solution)/shard_map/ppermute | solution.py:325
  9.1 11.6 %collective-permute-start.22 = (bf16[512,256]{1,0:T(8,128)(2,1)}, bf16[512,256]{1,0:T(8,128)(2,1)S(1)}, u32[]{:S(2)}, u32[]{:S(2)}) collective-permute-start(bf16[512,256]{1,0:T(8,128)(2,1)} %refs_13_.1), channel_id=1, source_target_pairs={{0,4},{1,5},{2,6},{3,7},{4,0},{5,1},{6,2},{7,3},{8,12},{9,13},{10,... | collective-permute-start | bytes 786440 | tf_op jit(solution)/shard_map/ppermute | solution.py:325
  26.0 13.3 %collective-permute-start.24 = (bf16[128,512]{1,0:T(8,128)(2,1)S(1)}, bf16[128,512]{1,0:T(8,128)(2,1)S(1)}, u32[]{:S(2)}, u32[]{:S(2)}) collective-permute-start(bf16[128,512]{1,0:T(8,128)(2,1)S(1)} %get-tuple-element.33), channel_id=1, source_target_pairs={{0,16},{1,17},{2,18},{3,19},{4,20},{5,21},{6,22},{7,23},{8,24},{9,... | collective-permute-start | bytes 393224 | tf_op jit(solution)/shard_map/ppermute | solution.py:325
  58.0 26.4 %collective-permute-start.27 = (bf16[8,128,256]{2,1,0:T(8,128)(2,1)S(1)}, bf16[8,128,256]{2,1,0:T(8,128)(2,1)S(1)}, u32[]{:S(2)}, u32[]{:S(2)}) collective-permute-start(bf16[8,128,256]{2,1,0:T(8,128)(2,1)S(1)} %all_to_all.5.refs_0_), channel_id=1, source_target_pairs={{0,2},{1,3},{2,0},{3,1},{4,6},{5,7},{6,4},{7,5},{8,10},{9,11},{10,... | collective-permute-start | bytes 1572872 | tf_op jit(solution)/shard_map/ppermute | solution.py:325
  58.3 10.8 %collective-permute-start.1 = (bf16[54,16,128]{2,1,0:T(8,128)(2,1)S(1)}, bf16[54,16,128]{2,1,0:T(8,128)(2,1)}, u32[]{:S(2)}, u32[]{:S(2)}) collective-permute-start(bf16[54,16,128]{2,1,0:T(8,128)(2,1)S(1)} %slice.12.refs_0_), channel_id=1, source_target_pairs={{0,8},{1,9},{2,10},{3,11},{4,12},{5,13},{6,14},{7,15},{8,0},{9,1},... | collective-permute-start | bytes 663560 | tf_op jit(solution)/shard_map/ppermute | solution.py:325
  62.0 22.4 %collective-permute-start.32 = (bf16[128,896]{1,0:T(8,128)(2,1)S(1)}, bf16[128,896]{1,0:T(8,128)(2,1)S(1)}, u32[]{:S(2)}, u32[]{:S(2)}) collective-permute-start(bf16[128,896]{1,0:T(8,128)(2,1)S(1)} %get-tuple-element.66), channel_id=1, source_target_pairs={{0,16},{1,17},{2,18},{3,19},{4,20},{5,21},{6,22},{7,23},{8,24},{9,... | collective-permute-start | bytes 688136 | tf_op jit(solution)/shard_map/ppermute | solution.py:325
  65.6 22.2 %collective-permute-start.33 = (bf16[128,896]{1,0:T(8,128)(2,1)}, bf16[128,896]{1,0:T(8,128)(2,1)S(1)}, u32[]{:S(2)}, u32[]{:S(2)}) collective-permute-start(bf16[128,896]{1,0:T(8,128)(2,1)} %get-tuple-element.65), channel_id=1, source_target_pairs={{0,20},{1,21},{2,22},{3,23},{4,16},{5,17},{6,18},{7,19},{8,28},{9,... | collective-permute-start | bytes 688136 | tf_op jit(solution)/shard_map/ppermute | solution.py:325
  69.1 18.8 %collective-permute-start.29 = (bf16[128,896]{1,0:T(8,128)(2,1)S(1)}, bf16[128,896]{1,0:T(8,128)(2,1)S(1)}, u32[]{:S(2)}, u32[]{:S(2)}) collective-permute-start(bf16[128,896]{1,0:T(8,128)(2,1)S(1)} %get-tuple-element.64), channel_id=1, source_target_pairs={{0,4},{1,5},{2,6},{3,7},{4,0},{5,1},{6,2},{7,3},{8,12},{9,13},{10,... | collective-permute-start | bytes 688136 | tf_op jit(solution)/shard_map/ppermute | solution.py:325
  69.7 20.0 %collective-permute-start.30 = (bf16[128,896]{1,0:T(8,128)(2,1)S(1)}, bf16[128,896]{1,0:T(8,128)(2,1)S(1)}, u32[]{:S(2)}, u32[]{:S(2)}) collective-permute-start(bf16[128,896]{1,0:T(8,128)(2,1)S(1)} %get-tuple-element.61), channel_id=1, source_target_pairs={{0,8},{1,9},{2,10},{3,11},{4,12},{5,13},{6,14},{7,15},{8,0},{9,1},... | collective-permute-start | bytes 688136 | tf_op jit(solution)/shard_map/ppermute | solution.py:325
  84.4 30.2 %collective-permute-start.26 = (bf16[8,128,256]{2,1,0:T(8,128)(2,1)S(1)}, bf16[8,128,256]{2,1,0:T(8,128)(2,1)S(1)}, u32[]{:S(2)}, u32[]{:S(2)}) collective-permute-start(bf16[8,128,256]{2,1,0:T(8,128)(2,1)S(1)} %all_to_all.5.refs_0_), channel_id=1, source_target_pairs={{0,1},{1,0},{2,3},{3,2},{4,5},{5,4},{6,7},{7,6},{8,9},{9,8},{10,11... | collective-permute-start | bytes 1572872 | tf_op jit(solution)/shard_map/ppermute | solution.py:325
  84.4 30.3 %collective-permute-start.28 = (bf16[8,128,256]{2,1,0:T(8,128)(2,1)S(1)}, bf16[8,128,256]{2,1,0:T(8,128)(2,1)S(1)}, u32[]{:S(2)}, u32[]{:S(2)}) collective-permute-start(bf16[8,128,256]{2,1,0:T(8,128)(2,1)S(1)} %collective-permute-done.27.refs_2_), channel_id=1, source_target_pairs={{0,1},{1,0},{2,3},{3,2},{4,5},{5,4},{6,7},{7,6},{8,9},{9,8},{10,11... | collective-permute-start | bytes 1572872 | tf_op jit(solution)/shard_map/ppermute | solution.py:325
  87.9 12.0 %collective-permute-start.6 = (bf16[54,16,128]{2,1,0:T(8,128)(2,1)}, bf16[54,16,128]{2,1,0:T(8,128)(2,1)}, u32[]{:S(2)}, u32[]{:S(2)}) collective-permute-start(bf16[54,16,128]{2,1,0:T(8,128)(2,1)} %collective-permute-done.1.refs_2_), channel_id=1, source_target_pairs={{8,16},{9,17},{10,18},{11,19},{12,20},{13,21},{14,22},{15,23},{16,... | collective-permute-start | bytes 663560 | tf_op jit(solution)/shard_map/ppermute | solution.py:325
  89.7 20.3 %collective-permute-start.4 = (bf16[54,16,128]{2,1,0:T(8,128)(2,1)}, bf16[54,16,128]{2,1,0:T(8,128)(2,1)}, u32[]{:S(2)}, u32[]{:S(2)}) collective-permute-start(bf16[54,16,128]{2,1,0:T(8,128)(2,1)} %copy-done.35), channel_id=1, source_target_pairs={{8,0},{9,1},{10,2},{11,3},{12,4},{13,5},{14,6},{15,7},{16,24},{17,... | collective-permute-start | bytes 663560 | tf_op jit(solution)/shard_map/ppermute | solution.py:325
  96.4 16.0 %collective-permute-start.34 = (bf16[128,896]{1,0:T(8,128)(2,1)}, bf16[128,896]{1,0:T(8,128)(2,1)S(1)}, u32[]{:S(2)}, u32[]{:S(2)}) collective-permute-start(bf16[128,896]{1,0:T(8,128)(2,1)} %get-tuple-element.60), channel_id=1, source_target_pairs={{0,24},{1,25},{2,26},{3,27},{4,28},{5,29},{6,30},{7,31},{8,16},{9,... | collective-permute-start | bytes 688136 | tf_op jit(solution)/shard_map/ppermute | solution.py:325
  99.9 20.7 %collective-permute-start.35 = (bf16[128,896]{1,0:T(8,128)(2,1)}, bf16[128,896]{1,0:T(8,128)(2,1)S(1)}, u32[]{:S(2)}, u32[]{:S(2)}) collective-permute-start(bf16[128,896]{1,0:T(8,128)(2,1)} %get-tuple-element.59), channel_id=1, source_target_pairs={{0,28},{1,29},{2,30},{3,31},{4,24},{5,25},{6,26},{7,27},{8,20},{9,... | collective-permute-start | bytes 688136 | tf_op jit(solution)/shard_map/ppermute | solution.py:325
  110.0 13.6 %collective-permute-start.7 = (bf16[54,16,128]{2,1,0:T(8,128)(2,1)}, bf16[54,16,128]{2,1,0:T(8,128)(2,1)S(1)}, u32[]{:S(2)}, u32[]{:S(2)}) collective-permute-start(bf16[54,16,128]{2,1,0:T(8,128)(2,1)} %collective-permute-done.6), channel_id=1, source_target_pairs={{8,0},{9,1},{10,2},{11,3},{12,4},{13,5},{14,6},{15,7},{16,24},{17,... | collective-permute-start | bytes 663560 | tf_op jit(solution)/shard_map/ppermute | solution.py:325
  112.5 11.7 %collective-permute-start = (bf16[54,16,128]{2,1,0:T(8,128)(2,1)}, bf16[54,16,128]{2,1,0:T(8,128)(2,1)S(1)}, u32[]{:S(2)}, u32[]{:S(2)}) collective-permute-start(bf16[54,16,128]{2,1,0:T(8,128)(2,1)} %copy-done.11), channel_id=1, source_target_pairs={{0,4},{1,5},{2,6},{3,7},{4,0},{5,1},{6,2},{7,3},{8,12},{9,13},{10,... | collective-permute-start | bytes 663560 | tf_op jit(solution)/shard_map/ppermute | solution.py:325
  114.7 19.3 %collective-permute-start.2 = (bf16[54,16,128]{2,1,0:T(8,128)(2,1)}, bf16[54,16,128]{2,1,0:T(8,128)(2,1)S(1)}, u32[]{:S(2)}, u32[]{:S(2)}) collective-permute-start(bf16[54,16,128]{2,1,0:T(8,128)(2,1)} %collective-permute-done.1.refs_2_), channel_id=1, source_target_pairs={{0,4},{1,5},{2,6},{3,7},{4,0},{5,1},{6,2},{7,3},{8,12},{9,13},{10,... | collective-permute-start | bytes 663560 | tf_op jit(solution)/shard_map/ppermute | solution.py:325
  114.8 22.1 %collective-permute-start.5 = (bf16[54,16,128]{2,1,0:T(8,128)(2,1)S(1)}, bf16[54,16,128]{2,1,0:T(8,128)(2,1)S(1)}, u32[]{:S(2)}, u32[]{:S(2)}) collective-permute-start(bf16[54,16,128]{2,1,0:T(8,128)(2,1)S(1)} %broadcast_select_fusion.9.refs_4_), channel_id=1, source_target_pairs={{0,4},{1,5},{2,6},{3,7},{4,0},{5,1},{6,2},{7,3},{8,12},{9,13},{10,... | collective-permute-start | bytes 663560 | tf_op jit(solution)/shard_map/ppermute | solution.py:325
  121.7 24.3 %collective-permute-start.39 = (bf16[128,896]{1,0:T(8,128)(2,1)S(1)}, bf16[128,896]{1,0:T(8,128)(2,1)S(1)}, u32[]{:S(2)}, u32[]{:S(2)}) collective-permute-start(bf16[128,896]{1,0:T(8,128)(2,1)S(1)} %get-tuple-element.43), channel_id=1, source_target_pairs={{0,16},{1,17},{2,18},{3,19},{4,20},{5,21},{6,22},{7,23},{8,24},{9,... | collective-permute-start | bytes 688136 | tf_op jit(solution)/shard_map/ppermute | solution.py:325
  123.7 26.9 %collective-permute-start.40 = (bf16[128,896]{1,0:T(8,128)(2,1)S(1)}, bf16[128,896]{1,0:T(8,128)(2,1)S(1)}, u32[]{:S(2)}, u32[]{:S(2)}) collective-permute-start(bf16[128,896]{1,0:T(8,128)(2,1)S(1)} %get-tuple-element.44), channel_id=1, source_target_pairs={{0,20},{1,21},{2,22},{3,23},{4,16},{5,17},{6,18},{7,19},{8,28},{9,... | collective-permute-start | bytes 688136 | tf_op jit(solution)/shard_map/ppermute | solution.py:325
  124.2 14.5 %collective-permute-start.8 = (bf16[54,16,128]{2,1,0:T(8,128)(2,1)S(1)}, bf16[54,16,128]{2,1,0:T(8,128)(2,1)S(1)}, u32[]{:S(2)}, u32[]{:S(2)}) collective-permute-start(bf16[54,16,128]{2,1,0:T(8,128)(2,1)S(1)} %broadcast_select_fusion.8.refs_6_), channel_id=1, source_target_pairs={{0,4},{1,5},{2,6},{3,7},{4,0},{5,1},{6,2},{7,3},{8,12},{9,13},{10,... | collective-permute-start | bytes 663560 | tf_op jit(solution)/shard_map/ppermute | solution.py:325
  134.7 26.5 %collective-permute-start.41 = (bf16[128,896]{1,0:T(8,128)(2,1)}, bf16[128,896]{1,0:T(8,128)(2,1)S(1)}, u32[]{:S(2)}, u32[]{:S(2)}) collective-permute-start(bf16[128,896]{1,0:T(8,128)(2,1)} %get-tuple-element.45), channel_id=1, source_target_pairs={{0,24},{1,25},{2,26},{3,27},{4,28},{5,29},{6,30},{7,31},{8,16},{9,... | collective-permute-start | bytes 688136 | tf_op jit(solution)/shard_map/ppermute | solution.py:325
  137.5 23.7 %collective-permute-start.42 = (bf16[128,896]{1,0:T(8,128)(2,1)}, bf16[128,896]{1,0:T(8,128)(2,1)S(1)}, u32[]{:S(2)}, u32[]{:S(2)}) collective-permute-start(bf16[128,896]{1,0:T(8,128)(2,1)} %get-tuple-element.46), channel_id=1, source_target_pairs={{0,28},{1,29},{2,30},{3,31},{4,24},{5,25},{6,26},{7,27},{8,20},{9,... | collective-permute-start | bytes 688136 | tf_op jit(solution)/shard_map/ppermute | solution.py:325
  139.4 21.8 %collective-permute-start.36 = (bf16[128,896]{1,0:T(8,128)(2,1)}, bf16[128,896]{1,0:T(8,128)(2,1)S(1)}, u32[]{:S(2)}, u32[]{:S(2)}) collective-permute-start(bf16[128,896]{1,0:T(8,128)(2,1)} %get-tuple-element.38), channel_id=1, source_target_pairs={{0,4},{1,5},{2,6},{3,7},{4,0},{5,1},{6,2},{7,3},{8,12},{9,13},{10,... | collective-permute-start | bytes 688136 | tf_op jit(solution)/shard_map/ppermute | solution.py:325
  146.7 14.5 %collective-permute-start.37 = (bf16[128,896]{1,0:T(8,128)(2,1)}, bf16[128,896]{1,0:T(8,128)(2,1)S(1)}, u32[]{:S(2)}, u32[]{:S(2)}) collective-permute-start(bf16[128,896]{1,0:T(8,128)(2,1)} %get-tuple-element.39), channel_id=1, source_target_pairs={{0,8},{1,9},{2,10},{3,11},{4,12},{5,13},{6,14},{7,15},{8,0},{9,1},... | collective-permute-start | bytes 688136 | tf_op jit(solution)/shard_map/ppermute | solution.py:325
  164.7 12.8 %collective-permute-start.47 = (bf16[2,27,16,128]{3,2,1,0:T(8,128)(2,1)S(1)}, bf16[2,27,16,128]{3,2,1,0:T(8,128)(2,1)S(1)}, u32[]{:S(2)}, u32[]{:S(2)}) collective-permute-start(bf16[2,27,16,128]{3,2,1,0:T(8,128)(2,1)S(1)} %get-tuple-element.56), channel_id=1, source_target_pairs={{0,8},{1,9},{2,10},{3,11},{4,12},{5,13},{6,14},{7,15},{8,0},{9,1},... | collective-permute-start | bytes 663560 | tf_op jit(solution)/shard_map/ppermute | solution.py:325
  168.3 17.0 %collective-permute-start.48 = (bf16[2,27,16,128]{3,2,1,0:T(8,128)(2,1)S(1)}, bf16[2,27,16,128]{3,2,1,0:T(8,128)(2,1)S(1)}, u32[]{:S(2)}, u32[]{:S(2)}) collective-permute-start(bf16[2,27,16,128]{3,2,1,0:T(8,128)(2,1)S(1)} %get-tuple-element.57), channel_id=1, source_target_pairs={{0,16},{1,17},{2,18},{3,19},{4,20},{5,21},{6,22},{7,23},{8,24},{9,... | collective-permute-start | bytes 663560 | tf_op jit(solution)/shard_map/ppermute | solution.py:325
  169.3 16.0 %collective-permute-start.49 = (bf16[2,27,16,128]{3,2,1,0:T(8,128)(2,1)S(1)}, bf16[2,27,16,128]{3,2,1,0:T(8,128)(2,1)S(1)}, u32[]{:S(2)}, u32[]{:S(2)}) collective-permute-start(bf16[2,27,16,128]{3,2,1,0:T(8,128)(2,1)S(1)} %get-tuple-element.58), channel_id=1, source_target_pairs={{0,24},{1,25},{2,26},{3,27},{4,28},{5,29},{6,30},{7,31},{8,16},{9,... | collective-permute-start | bytes 663560 | tf_op jit(solution)/shard_map/ppermute | solution.py:325
  171.9 14.7 %collective-permute-start.43 = (bf16[4,27,16,128]{3,2,1,0:T(8,128)(2,1)S(1)}, bf16[4,27,16,128]{3,2,1,0:T(8,128)(2,1)S(1)}, u32[]{:S(2)}, u32[]{:S(2)}) collective-permute-start(bf16[4,27,16,128]{3,2,1,0:T(8,128)(2,1)S(1)} %get-tuple-element.50), channel_id=1, source_target_pairs={{0,4},{1,5},{2,6},{3,7},{4,0},{5,1},{6,2},{7,3},{8,12},{9,13},{10,... | collective-permute-start | bytes 1327112 | tf_op jit(solution)/shard_map/ppermute | solution.py:325
  191.5 10.4 %collective-permute-start.45 = (bf16[27,16,128]{2,1,0:T(8,128)(2,1)S(1)}, bf16[27,16,128]{2,1,0:T(8,128)(2,1)S(1)}, u32[]{:S(2)}, u32[]{:S(2)}) collective-permute-start(bf16[27,16,128]{2,1,0:T(8,128)(2,1)S(1)} %get-tuple-element.53), channel_id=1, source_target_pairs={{0,16},{1,17},{2,18},{3,19},{4,20},{5,21},{6,22},{7,23},{8,24},{9,... | collective-permute-start | bytes 331784 | tf_op jit(solution)/shard_map/ppermute | solution.py:325
  191.5 10.4 %collective-permute-start.46 = (bf16[27,16,128]{2,1,0:T(8,128)(2,1)S(1)}, bf16[27,16,128]{2,1,0:T(8,128)(2,1)S(1)}, u32[]{:S(2)}, u32[]{:S(2)}) collective-permute-start(bf16[27,16,128]{2,1,0:T(8,128)(2,1)S(1)} %get-tuple-element.54), channel_id=1, source_target_pairs={{0,24},{1,25},{2,26},{3,27},{4,28},{5,29},{6,30},{7,31},{8,16},{9,... | collective-permute-start | bytes 331784 | tf_op jit(solution)/shard_map/ppermute | solution.py:325
  (59 other events, 577.1 us)
